TPU v7x, 128 devices: a whole 4x4x4 slice. The times are simulated.
128 devices in a mesh: seq: 16 (over x, y), dp: 8 (over z, core).
Axes of the slice: x: 4, y: 4, z: 4, core: 2. Of those that a mesh axis runs over, the one named last changes fastest.
Arguments:
- tokens: bfloat16 [8, 8192, 2048], P('dp', 'seq'), may hold values from -6 to 6
- weights_master: float32 [2048, 3072], P('dp'), may hold values from -0.125 to 0.125
- adam_first: float32 [2048, 3072], P('dp'), may hold values from -6 to 6
- adam_second: float32 [2048, 3072], P('dp'), may hold values from 0.5 to 2
- cotangent: bfloat16 [8, 8192, 1024], P('dp', 'seq'), may hold values from -0.0234375 to 0.0234375
Outputs:
- attended: bfloat16 [8, 8192, 1024], P('dp', 'seq')
- new_weights: float32 [2048, 3072], P('dp')
- new_first: float32 [2048, 3072], P('dp')
- new_second: float32 [2048, 3072], P('dp')
All inputs are finite; a program needn't handle non-finite values.
Results may differ from a plain program's by a relative error of at most 0.0035.
The roundings to bfloat16 on the way count: a program that leaves them out, or rounds other values in their place, can miss the bound.
Values may be sent and summed in bfloat16 or wider, within the bound.
No kernel may reach another device: no remote copies, remote signals or barrier semaphores. Data moves between devices by JAX's collectives and lax.ppermute only.
A program may use at most 128 MiB of HBM per device.

v0:
```python
import jax
import jax.numpy as jnp
from jax import lax
from jax.experimental import pallas as pl
from jax.experimental.pallas import tpu as pltpu
from jax.sharding import Mesh, PartitionSpec as P


HDIM = 128
BLOCK = 512
STEP = 100
HEADS_CORE = 4

EPS_NORM = 1e-05
BETA_ONE = 0.9
BETA_TWO = 0.95
LEARN_RATE = 0.001
DECAY_WEIGHT = 0.1
EPS_ADAM = 1e-08

BF = jnp.bfloat16
F32 = jnp.float32


PAIRS = {
    "0": [(0, 1), (1, 0), (2, 3), (3, 2)],
    "1": [(1, 2), (2, 1), (3, 0), (0, 3)],
}
CORE_SWAP = [(0, 1), (1, 0)]

GATHER_ORDERS = [("z0", "z1"), ("z1", "z0")]
HALVING = [
    ("x0", "z0", "z1"),
    ("y0", "z1", "z0"),
    ("z0", "x0", "z1"),
    ("z1", "y0", "z0"),
    ("x1", "z0", "z1"),
    ("y1", "z1", "z0"),
]
GROUPS = [
    ((0, 2), ("x1", "y1", "y0"), "x0"),
    ((1, 3), ("y1", "x1", "x0"), "y0"),
    ((4,), ("y0", "x0", "y1"), "x1"),
    ((5,), ("x0", "y0", "x1"), "y1"),
]
WIDTH = HEADS_CORE * HDIM
ROWS = 2 * BLOCK
VMEM = pl.BlockSpec(memory_space=pltpu.VMEM)
barrier = lax.optimization_barrier


def swap(x, dim):
    if dim == "c":
        return lax.ppermute(x, "c", CORE_SWAP)
    return lax.ppermute(x, dim[0], PAIRS[dim[1]])


def gray(place):
    return place ^ (place >> 1)


def place_bit(dim):
    code = gray(lax.axis_index(dim[0]))
    return (code >> int(dim[1])) & 1


def colour():
    return (lax.axis_index("x") + lax.axis_index("y")) & 1


def block_order():
    blocks = []
    for i in range(8):
        code = gray(lax.axis_index("z")) ^ (i >> 2) ^ (((i >> 1) & 1) << 1)
        blocks.append(2 * (code ^ (code >> 1)) + (colour() ^ (i & 1)))
    return jnp.stack(blocks).astype(jnp.int32)


def dot(a, b, ca, cb):
    return lax.dot_general(a, b, (((ca,), (cb,)), ((), ())), preferred_element_type=F32)


def causal(x):
    rows = lax.broadcasted_iota(jnp.int32, x.shape, 0)
    cols = lax.broadcasted_iota(jnp.int32, x.shape, 1)
    return jnp.where(rows >= cols, x, 0.0).astype(BF)


def shape(dims, dtype):
    return jax.ShapeDtypeStruct(dims, dtype)


def prepare_kernel(core, *refs):
    for out, parts in ((refs[7], refs[:3]), (refs[8], refs[3:6])):
        for t in range(HEADS_CORE):
            for u in range(3):
                kind, head = place_of(t, u)
                out[t, :, u * HDIM : (u + 1) * HDIM] = parts[kind][:, cols(head)].astype(BF)
    refs[9][...] = refs[6][...]


def place_of(chunk, slot):
    place = 3 * (chunk % 2) + slot
    return place // 2, 2 * (chunk // 2) + place % 2


def cols(h):
    return slice(h * HDIM, (h + 1) * HDIM)


def prepare(core, master, cot):
    def spec(j, other):
        def index(i, c):
            return i, 2 * j + (1 - c[0] if other else c[0])

        return pl.BlockSpec((128, WIDTH), index)

    out = pl.BlockSpec((HEADS_CORE, 128, 3 * HDIM), lambda i, c: (0, i, 0))
    return pl.pallas_call(
        prepare_kernel,
        name="prepare",
        grid_spec=pltpu.PrefetchScalarGridSpec(
            num_scalar_prefetch=1,
            grid=(2,),
            in_specs=[spec(j, other) for other in (False, True) for j in range(3)]
            + [pl.BlockSpec((256, WIDTH), lambda i, c: (i, 1 - c[0]))],
            out_specs=(out, out, pl.BlockSpec((256, WIDTH), lambda i, c: (i, 0))),
        ),
        out_shape=(shape((HEADS_CORE, 256, 3 * HDIM), BF),) * 2 + (shape((BLOCK, WIDTH), BF),),
    )(core.reshape(1), *([master] * 6), cot)


def arrange_kernel(blocks, own, other, out):
    out[:BLOCK, :] = own[...]
    out[BLOCK:, :] = other[...]


def arrange(blocks, own, other):
    tile = pl.BlockSpec((BLOCK, 256), lambda i, b: (0, b[i]))
    return pl.pallas_call(
        arrange_kernel,
        name="arrange",
        grid_spec=pltpu.PrefetchScalarGridSpec(
            num_scalar_prefetch=1,
            grid=(8,),
            in_specs=[tile, tile],
            out_specs=pl.BlockSpec((ROWS, 256), lambda i, b: (0, i)),
        ),
        out_shape=shape((ROWS, own.shape[1]), BF),
    )(blocks, own, other)


def outer_kernel(pair, keys, values, before, kv):
    for h in range(2):
        kv[h, 0] = dot(keys[:, cols(h)], values[:, cols(h)], 0, 0)


def project(pair, tokens, pieces, before):
    chunks = []
    for h, order in enumerate(GATHER_ORDERS):
        mine, low, high = pieces[3 * h : 3 * h + 3]
        theirs = (low, high)
        rows = []
        for i in range(8):
            flips = {"z0": i >> 2, "z1": (i >> 1) & 1}
            place = flips[order[0]] + 2 * flips[order[1]]
            rows.append(theirs[place // 2][place % 2] if i & 1 else mine[place])
        chunks.append(jnp.concatenate(rows, 0))
    weights = jnp.concatenate(chunks, 1)
    qkv = jnp.dot(tokens, weights, preferred_element_type=F32).astype(BF)
    kv = pl.pallas_call(
        outer_kernel,
        name="outer",
        grid_spec=pltpu.PrefetchScalarGridSpec(
            num_scalar_prefetch=1,
            grid=(2,),
            in_specs=[
                pl.BlockSpec((BLOCK, 256), lambda s, p: (s, 1)),
                pl.BlockSpec((BLOCK, 256), lambda s, p: (s, 2)),
                pl.BlockSpec(memory_space=pl.ANY),
            ],
            out_specs=pl.BlockSpec((2, 1, HDIM, HDIM), lambda s, p: (p[0], s, 0, 0)),
        ),
        out_shape=shape((HEADS_CORE, 2, HDIM, HDIM), F32),
        input_output_aliases={3: 0},
    )(jnp.full((1,), pair, jnp.int32), qkv, qkv, before)
    return qkv, kv


def lower_scores(a, b):
    low = dot(a[256:], b, 1, 1)
    return causal(dot(a[:256], b[:256], 1, 1)), low[:, :256].astype(BF), causal(low[:, 256:])


def times(scores, x):
    first, left, right = scores
    low = jnp.concatenate([left, right], 1)
    return jnp.concatenate([dot(first, x[:256], 1, 0), dot(low, x, 1, 0)], 0)


def turned_times(scores, x):
    first, left, right = scores
    column = jnp.concatenate([first, left], 0)
    return jnp.concatenate([dot(column, x, 0, 0), dot(right, x[256:], 0, 0)], 0)


def running_kernel(received, out):
    total = jnp.zeros(received.shape[1:], F32)
    for place in range(received.shape[0]):
        out[place] = total.astype(BF)
        total = total + received[place]


def earlier_states(kv):
    cut = kv.reshape(16, -1, HDIM)
    received = lax.all_to_all(cut, ("x", "y"), 0, 0, tiled=True)
    sums = pl.pallas_call(
        running_kernel,
        name="running",
        out_shape=shape(received.shape, BF),
        in_specs=[VMEM],
        out_specs=VMEM,
    )(received)
    return lax.all_to_all(sums, ("x", "y"), 0, 0, tiled=True).reshape(kv.shape)


def head_of(ref, h, kind):
    return ref[:, pl.ds(pl.multiple_of((2 * "qkv".index(kind) + h) * HDIM, HDIM), HDIM)]


def head_cols(h):
    return pl.ds(pl.multiple_of(h * HDIM, HDIM), HDIM)


def each_head(body):
    def one(h, carry):
        body(h)
        return carry

    lax.fori_loop(0, 2, one, 0)


def pair_specs():
    qkv_rows = (BLOCK, 6 * HDIM)
    return [
        pl.BlockSpec(qkv_rows, lambda p, s, *_: (jnp.where(p == 0, s, 1), 0)),
        pl.BlockSpec(qkv_rows, lambda p, s, *_: (jnp.where(p == 0, 0, s), 0)),
    ]


def head_rows():
    return pl.BlockSpec((BLOCK, 256), lambda p, s, *_: (s, p))


def pick(first, second, h, kinds):
    pair = pl.program_id(0)
    return [jnp.where(pair == 0, head_of(first, h, j), head_of(second, h, j)) for j in kinds]


def within_kernel(first, second, out):
    @each_head
    def _(h):
        q, k, v = pick(first, second, h, "qkv")
        out[:, head_cols(h)] = times(lower_scores(q, k), v)


def local_scores(first, second):
    return pl.pallas_call(
        within_kernel,
        name="within",
        grid=(2, 2),
        in_specs=pair_specs(),
        out_specs=head_rows(),
        out_shape=shape((ROWS, WIDTH), F32),
    )(first, second)


def forward_kernel(core, first, second, within, state, cot_own, cot_other, attended, grad, qg):
    s = pl.program_id(1)

    @each_head
    def _(h):
        (q,) = pick(first, second, h, "q")
        at = head_cols(h)
        mixed = within[:, at] + dot(q, state[h, 0], 1, 0)
        inverse = lax.rsqrt(jnp.mean(mixed * mixed, -1, keepdims=True) + EPS_NORM)
        normed = mixed * inverse
        attended[:, at] = normed.astype(BF)
        out_grad = jnp.where(s == 0, cot_own[:, at], cot_other[:, at]).astype(F32)
        along = jnp.mean(out_grad * normed, -1, keepdims=True)
        g = (inverse * (out_grad - normed * along)).astype(BF)
        grad[:, at] = g
        qg[h, 0] = dot(q, g, 0, 0).astype(BF)


def forward(core, first, second, within, state, cot_own, cot_other):
    rows = head_rows()
    states = pl.BlockSpec((2, 1, HDIM, HDIM), lambda p, s, c: (p, s, 0, 0))
    queries = (BLOCK, 2 * HDIM)
    return pl.pallas_call(
        forward_kernel,
        name="forward",
        grid_spec=pltpu.PrefetchScalarGridSpec(
            num_scalar_prefetch=1,
            grid=(2, 2),
            in_specs=[
                pl.BlockSpec(queries, lambda p, s, c: (jnp.where(p == 0, s, 1), 0)),
                pl.BlockSpec(queries, lambda p, s, c: (jnp.where(p == 0, 0, s), 0)),
                rows,
                states,
                pl.BlockSpec((BLOCK, 256), lambda p, s, c: (0, 2 * c[0] + p)),
                pl.BlockSpec((BLOCK, 256), lambda p, s, c: (0, p)),
            ],
            out_specs=(rows, rows, states),
        ),
        out_shape=(
            shape((ROWS, WIDTH), BF),
            shape((ROWS, WIDTH), BF),
            shape((HEADS_CORE, 2, HDIM, HDIM), BF),
        ),
    )(core.reshape(1), first, second, within, state, cot_own, cot_other)


def backward_kernel(pair, qkv, grad, state, dq, dkv):
    @each_head
    def _(h):
        q, k, v = [head_of(qkv, h, j) for j in "qkv"]
        at = head_cols(h)
        g = grad[:, at]
        back = lower_scores(g, v)
        dq[:, at] = (times(back, k) + dot(g, state[h, 0], 1, 1)).astype(BF)
        dkv[0, :, at] = turned_times(back, q)
        dkv[1, :, at] = turned_times(lower_scores(q, k), g)


def backward(pair, qkv, grad, state):
    return pl.pallas_call(
        backward_kernel,
        name="backward",
        grid_spec=pltpu.PrefetchScalarGridSpec(
            num_scalar_prefetch=1,
            grid=(2,),
            in_specs=[
                pl.BlockSpec((BLOCK, 6 * HDIM), lambda s, p: (s, 0)),
                pl.BlockSpec((BLOCK, 256), lambda s, p: (s, p[0])),
                pl.BlockSpec((2, 1, HDIM, HDIM), lambda s, p: (p[0], s, 0, 0)),
            ],
            out_specs=(
                pl.BlockSpec((BLOCK, 256), lambda s, p: (s, 0)),
                pl.BlockSpec((2, BLOCK, 256), lambda s, p: (0, s, 0)),
            ),
        ),
        out_shape=(shape((ROWS, 256), BF), shape((2, ROWS, 256), F32)),
    )(jnp.full((1,), pair, jnp.int32), qkv, grad, state)


def multiply_blocks(turned, tokens, out):
    def block(i, carry):
        at = pl.ds(pl.multiple_of(i * 256, 256), 256)
        piece = dot(turned[...], tokens[:, at], 1, 0).astype(BF)
        out[0, 0, i] = piece[:256]
        out[0, 1, i] = piece[256:]
        return carry

    lax.fori_loop(0, tokens.shape[1] // 256, block, 0)


def query_gradient_kernel(q0, q1, tokens, out, turned):
    turned[:256, :] = q0[...].T
    turned[256:, :] = q1[...].T
    multiply_blocks(turned, tokens, out)


def gradient_kernel(first, second, d_first, d_second, state, tokens, out, turned):
    kind = pl.program_id(0)
    for pair, (rows, within) in enumerate(((first, d_first), (second, d_second))):

        @each_head
        def _(h):
            head = 2 * pair + h
            at = head_cols(h)
            for s in range(2):
                span = slice(s * BLOCK, (s + 1) * BLOCK)
                later = state[head, s]
                later = jnp.where(kind == 0, later.T, later)
                total = within[0, span, at] + dot(rows[span, at], later, 1, 0)
                turned[head_cols(head), span] = total.astype(BF).T

    multiply_blocks(turned, tokens, out)


def gradient_call(kernel, count, ins, specs, tokens):
    blocks = tokens.shape[1] // 256
    return pl.pallas_call(
        kernel,
        grid=(count,),
        in_specs=specs + [VMEM],
        out_specs=pl.BlockSpec((1, 2, blocks, 256, 256), lambda j: (j, 0, 0, 0, 0)),
        out_shape=shape((count, 2, blocks, 256, 256), BF),
        scratch_shapes=[pltpu.VMEM((WIDTH, ROWS), BF)],
    )(*ins, tokens)


def query_gradient(q0, q1, tokens):
    return gradient_call(query_gradient_kernel, 1, (q0, q1), [VMEM] * 2, tokens)


def key_value_gradient(first, second, d_first, d_second, state, tokens):
    rows = pl.BlockSpec((ROWS, 256), lambda j: (0, 2 - j))
    within = pl.BlockSpec((1, ROWS, 256), lambda j: (j, 0, 0))
    specs = [rows, rows, within, within, VMEM]
    ins = (first, second, d_first, d_second, state)
    return gradient_call(gradient_kernel, 2, ins, specs, tokens)


def parts_of(partial):
    return [
        partial[j, i].reshape(2, 2, 2, 256, 256) for j in range(partial.shape[0]) for i in range(2)
    ]


def wide(x):
    return x.astype(F32)


def add(a, b):
    return (wide(a) + wide(b)).astype(BF)


def reduce_part(part, order):
    left = ["z0", "z1", "flat"]
    for dim in order:
        name = dim if dim[0] == "z" else "flat"
        axis = left.index(name)
        left.remove(name)
        if name == "flat":
            keeps = colour() ^ place_bit(dim)
            send = lax.dynamic_index_in_dim(part, 1 - keeps, axis, False)
            keep = lax.dynamic_index_in_dim(part, keeps, axis, False)
        else:
            send = lax.index_in_dim(part, 1, axis, False)
            keep = lax.index_in_dim(part, 0, axis, False)
        part = add(keep, swap(send, dim))
    return part


def finish_group(parts, exchanged, last):
    total = jnp.stack(parts)
    for dim in exchanged:
        total = add(total, swap(total, dim))
    return total, swap(total, last)


def later_steps(total, later):
    total = wide(total)
    carried = jnp.zeros_like(total)
    for dim in ("y0", "y1", "x0", "x1"):
        received = yield swap(total.astype(BF), dim)
        received = wide(received)
        upper = (lax.axis_index(dim[0]) >> int(dim[1])) & 1
        carried = carried + jnp.where(upper == (0 if later else 1), received, 0.0)
        total = total + received
    yield carried.astype(BF)


def sort_kernel(holds, *refs):
    kept, sent = refs[-2:]

    def rows(i, carry):
        at = pl.ds(pl.multiple_of(i * 64, 64), 64)
        for g, (members, _, _) in enumerate(GROUPS):
            straight = holds[g] == 1
            for j, p in enumerate(members):
                here, there = refs[2 * g][j, at, :], refs[2 * g + 1][j, at, :]
                kept[p, at, :] = jnp.where(straight, here, there)
                sent[p, at, :] = jnp.where(straight, there, here)
        return carry

    lax.fori_loop(0, 4, rows, 0)


def sort_pieces(holds, finished):
    return pl.pallas_call(
        sort_kernel,
        name="sort_pieces",
        in_specs=[pl.BlockSpec(memory_space=pltpu.SMEM)] + [VMEM] * len(finished),
        out_specs=(VMEM, VMEM),
        out_shape=(shape((6, 256, 256), BF),) * 2,
    )(holds, *finished)


def adam_kernel(core, kept, received, weights, first, second, out_weights, out_first, out_second):
    straight = (pl.program_id(0) // 2) % 2 == core[0]
    gradient = jnp.where(straight, kept[0], received[0]).astype(F32).T
    new_first = BETA_ONE * first[...] + (1.0 - BETA_ONE) * gradient
    new_second = BETA_TWO * second[...] + (1.0 - BETA_TWO) * gradient * gradient
    first_hat = new_first / (1.0 - BETA_ONE**STEP)
    second_hat = new_second / (1.0 - BETA_TWO**STEP)
    out_first[...] = new_first
    out_second[...] = new_second
    out_weights[...] = weights[...] - LEARN_RATE * (
        first_hat / (jnp.sqrt(second_hat) + EPS_ADAM) + DECAY_WEIGHT * weights[...]
    )


def adam(core, kept, received, *arrays):
    piece = pl.BlockSpec((1, 256, 256), lambda n, c: (2 * (n // 4) + n % 2, 0, 0))
    block = pl.BlockSpec((256, 256), lambda n, c: (0, n))
    return pl.pallas_call(
        adam_kernel,
        name="adam",
        grid_spec=pltpu.PrefetchScalarGridSpec(
            num_scalar_prefetch=1,
            grid=(12,),
            in_specs=[piece, piece, block, block, block],
            out_specs=(block,) * 3,
        ),
        out_shape=tuple(shape(x.shape, F32) for x in arrays),
    )(core.reshape(1), kept, received, *arrays)


def gather_step(step, mine):
    got = []
    for h in range(2):
        got.append(swap(mine[h], GATHER_ORDERS[h][step]))
    return [jnp.concatenate([mine[h], got[h]], 0) for h in range(2)]


def exchange_colours(mine):
    pieces = []
    for h, axis in enumerate("xy"):
        pieces.append(mine[h])
        for side in range(2):
            pieces.append(swap(mine[h][2 * side : 2 * side + 2], f"{axis}{side}"))
    return pieces


def step(tokens, weights_master, adam_first, adam_second, cotangent):
    core = lax.axis_index("c")
    own = tokens[0]
    straight = colour() == core

    held, outgoing, cot_out = prepare(core, weights_master, cotangent[0])
    traded = swap(outgoing, "c")
    other = swap(own, "c")
    cot_other = swap(cot_out, "c")

    blocks = block_order()
    mine = jnp.where(straight, held, traded)
    first = gather_step(0, [mine[0][None], mine[1][None]])
    first = gather_step(1, first)
    both = arrange(blocks, own, other)
    first, mine, both = barrier((first, mine, both))
    pieces = exchange_colours(first)
    second = gather_step(0, [mine[2][None], mine[3][None]])
    second = gather_step(1, second)
    kv = jnp.zeros((HEADS_CORE, 2, HDIM, HDIM), F32)
    qkv_first, kv = project(0, both, pieces, kv)
    second, qkv_first, kv = barrier((second, qkv_first, kv))
    qkv_second, kv = project(1, both, exchange_colours(second), kv)

    state = earlier_states(kv)
    within = local_scores(qkv_first, qkv_second)
    attended, grad, qg = forward(
        core, qkv_first, qkv_second, within, state, cotangent[0], cot_other
    )

    steps = later_steps(qg, True)
    received = next(steps)
    q0, d0 = backward(0, qkv_first, grad, state)
    received, q0, d0, grad = barrier((received, q0, d0, grad))
    received = steps.send(received)
    q1, d1 = backward(1, qkv_second, grad, state)
    received, q0, q1, d1 = barrier((received, q0, q1, d1))
    received = steps.send(received)
    parts = parts_of(query_gradient(q0, q1, both))
    received, parts = barrier((received, parts))
    received = steps.send(received)
    later = steps.send(received)
    parts += parts_of(key_value_gradient(qkv_first, qkv_second, d0, d1, later, both))

    attended_other = swap(attended[BLOCK:], "c")
    low = jnp.where(core == 0, attended[:BLOCK], attended_other)
    high = jnp.where(core == 0, attended_other, attended[:BLOCK])
    attended_out = jnp.concatenate([low, high], 1)[None]

    reduced = [reduce_part(part, order) for part, order in zip(parts, HALVING)]
    holds, finished = [], []
    for members, exchanged, last in GROUPS:
        holds.append(place_bit(last) == core)
        finished += finish_group([reduced[p] for p in members], exchanged, last)
    kept, sent = sort_pieces(jnp.stack(holds).astype(jnp.int32), finished)
    received = swap(sent, "c")
    new_weights, new_first, new_second = adam(
        core, kept, received, weights_master, adam_first, adam_second
    )
    return (attended_out, new_weights, new_first, new_second)


def solution(mesh):
    torus = Mesh(mesh.devices.reshape(4, 4, 4, 2), ("x", "y", "z", "c"))
    rows = P(("z", "c"), ("x", "y"), None)
    shard = P(("z", "c"), None)
    return jax.shard_map(
        step,
        mesh=torus,
        in_specs=(rows, shard, shard, shard, rows),
        out_specs=(rows, shard, shard, shard),
        check_vma=False,
    )
```

profile of v0, /device:TPU:0, one launch (start us, length us, event | category | flops | bytes accessed | tf_op | source)
XLA Modules:
  0.0 287.3 jit_solution(7847424627926798153)
XLA Ops:
  0.6 3.1 %prepare.1 = (bf16[4,256,384]{2,1,0:T(8,128)(2,1)}, bf16[4,256,384]{2,1,0:T(8,128)(2,1)}, bf16[512,512]{1,0:T(8,128)(2,1)}) custom-call(s32[1]{0:T(128)} %bitcast.core, f32[256,3072]{1,0:T(8,128)} %weights.1, f32[256,3072]{1,0:T(8,128)} %weights.1, f32[256,3072]{1,0:T(8,128)} %weights.1, f32[256,3072]{1,0:T(8,128)} %weights.1, f32[256,3072]{1,0:T(8,128)} %weights.1, ...), custom_call_target="tpu_custom_call" | custom-call | tf_op jit(solution)/shard_map/prepare/pallas_call | solution.py:119
  7.6 4.2 %collective-permute-start.3 = (bf16[1,256,384]{2,1,0:T(8,128)(2,1)S(1)}, bf16[1,256,384]{2,1,0:T(8,128)(2,1)S(1)}, u32[]{:S(2)}, u32[]{:S(2)}) collective-permute-start(bf16[1,256,384]{2,1,0:T(8,128)(2,1)S(1)} %get-tuple-element.95), channel_id=1, source_target_pairs={{2,4},{4,2},{6,0},{0,6},{3,5},{5,3},{7,1},{1,7},{10,12},{12,10},{1... | collective-permute-start | bytes 589832 | tf_op jit(solution)/shard_map/ppermute | solution.py:55
  11.8 4.1 %collective-permute-done.3 = bf16[1,256,384]{2,1,0:T(8,128)(2,1)S(1)} collective-permute-done((bf16[1,256,384]{2,1,0:T(8,128)(2,1)S(1)}, bf16[1,256,384]{2,1,0:T(8,128)(2,1)S(1)}, u32[]{:S(2)}, u32[]{:S(2)}) %collective-permute-start.3) | collective-permute-done | bytes 196640 | tf_op jit(solution)/shard_map/ppermute | solution.py:55
  19.8 6.2 %collective-permute-done.4 = bf16[2,256,384]{2,1,0:T(8,128)(2,1)} collective-permute-done((bf16[2,256,384]{2,1,0:T(8,128)(2,1)S(1)}, bf16[2,256,384]{2,1,0:T(8,128)(2,1)}, u32[]{:S(2)}, u32[]{:S(2)}) %collective-permute-start.4) | collective-permute-done | bytes 393248 | tf_op jit(solution)/shard_map/ppermute | solution.py:55
  28.9 7.3 %arrange.1.tokens = bf16[1024,2048]{1,0:T(8,128)(2,1)} custom-call(s32[8]{0:T(128)} %stack.70.blocks, bf16[512,2048]{1,0:T(8,128)(2,1)} %bitcast.10.own, bf16[512,2048]{1,0:T(8,128)(2,1)} %collective-permute-done.5.other), custom_call_target="tpu_custom_call" | custom-call | tf_op jit(solution)/shard_map/arrange/pallas_call | solution.py:140
  36.3 4.8 %collective-permute-start.10 = (bf16[2,256,384]{2,1,0:T(8,128)(2,1)S(1)}, bf16[2,256,384]{2,1,0:T(8,128)(2,1)S(1)}, u32[]{:S(2)}, u32[]{:S(2)}) collective-permute-start(bf16[2,256,384]{2,1,0:T(8,128)(2,1)S(1)} %get-tuple-element.90), channel_id=1, source_target_pairs={{0,32},{32,0},{64,96},{96,64},{1,33},{33,1},{65,97},{97,65},{2,34}... | collective-permute-start | bytes 1179656 | tf_op jit(solution)/shard_map/ppermute | solution.py:55
  43.8 2.4 collective-permute-start.12
  54.1 4.6 %collective-permute-done.13 = bf16[2,256,384]{2,1,0:T(8,128)(2,1)S(1)} collective-permute-done((bf16[2,256,384]{2,1,0:T(8,128)(2,1)S(1)}, bf16[2,256,384]{2,1,0:T(8,128)(2,1)S(1)}, u32[]{:S(2)}, u32[]{:S(2)}) %collective-permute-start.13) | collective-permute-done | bytes 393248 | tf_op jit(solution)/shard_map/ppermute | solution.py:55
  58.8 4.5 %fusion.11.keys.values.first.qkv = bf16[1024,768]{1,0:T(8,128)(2,1)} fusion(bf16[1024,2048]{1,0:T(8,128)(2,1)S(1)} %copy-done, bf16[2048,384]{1,0:T(8,128)(2,1)S(1)} %fusion.47, bf16[2048,384]{1,0:T(8,128)(2,1)S(1)} %fusion.51), kind=kOutput, calls=%fused_computation.9 | convolution fusion | flops 3228303360 | bytes 8912896 | tf_op jit(solution)/shard_map/dot_general | solution.py:170
  69.4 2.7 collective-permute-start.15
  72.5 2.3 collective-permute-start.17
  81.7 4.5 %fusion.8.second.keys.values.qkv = bf16[1024,768]{1,0:T(8,128)(2,1)} fusion(bf16[1024,2048]{1,0:T(8,128)(2,1)S(1)} %copy-done.1, bf16[2048,384]{1,0:T(8,128)(2,1)S(1)} %fusion.39, bf16[2048,384]{1,0:T(8,128)(2,1)S(1)} %fusion.43), kind=kOutput, calls=%fused_computation.8 | convolution fusion | flops 3228303360 | bytes 8912896 | tf_op jit(solution)/shard_map/dot_general | solution.py:170
  88.5 5.4 %all-to-all-start = ((f32[16,64,128]{2,1,0:T(8,128)}), f32[16,64,128]{2,1,0:T(8,128)S(1)}, u32[]{:S(2)}, u32[]{:S(2)}) async-start(f32[16,64,128]{2,1,0:T(8,128)} %bitcast.250), calls=%async_computation | async-start | bytes 1048576 | tf_op jit(solution)/shard_map/all_to_all | solution.py:216
  94.1 10.0 %all-to-all-done.received = f32[16,64,128]{2,1,0:T(8,128)S(1)} async-done(((f32[16,64,128]{2,1,0:T(8,128)}), f32[16,64,128]{2,1,0:T(8,128)S(1)}, u32[]{:S(2)}, u32[]{:S(2)}) %all-to-all-start) | async-done | bytes 524320 | tf_op jit(solution)/shard_map/all_to_all | solution.py:216
  106.6 3.7 %all-to-all-start.1 = ((bf16[16,64,128]{2,1,0:T(8,128)(2,1)}), bf16[16,64,128]{2,1,0:T(8,128)(2,1)S(1)}, u32[]{:S(2)}, u32[]{:S(2)}) async-start(bf16[16,64,128]{2,1,0:T(8,128)(2,1)} %running.1), calls=%async_computation.1 | async-start | bytes 524288 | tf_op jit(solution)/shard_map/all_to_all | solution.py:224
  110.3 6.5 %within.1 = f32[1024,512]{1,0:T(8,128)} custom-call(bf16[1024,768]{1,0:T(8,128)(2,1)} %fusion.11.keys.values.first.qkv, bf16[1024,768]{1,0:T(8,128)(2,1)} %fusion.8.second.keys.values.qkv), custom_call_target="tpu_custom_call" | custom-call | tf_op jit(solution)/shard_map/within/pallas_call | solution.py:268
  119.3 6.9 %forward.1 = (bf16[1024,512]{1,0:T(8,128)(2,1)}, bf16[1024,512]{1,0:T(8,128)(2,1)}, bf16[4,2,128,128]{3,2,1,0:T(8,128)(2,1)}) custom-call(s32[1]{0:T(128)} %bitcast.core, bf16[1024,768]{1,0:T(8,128)(2,1)} %fusion.11.keys.values.first.qkv, bf16[1024,768]{1,0:T(8,128)(2,1)} %fusion.8.second.keys.values.qkv, f32[1024,512]{1,0:T(8,128)} %within.1, ...), custom_call_target="tpu_custom_call" | custom-call | tf_op jit(solution)/shard_map/forward/pallas_call | solution.py:300
  126.7 6.1 %backward.2 = (bf16[1024,256]{1,0:T(8,128)(2,1)}, f32[2,1024,256]{2,1,0:T(8,128)}) custom-call(s32[1]{0:T(128)} %constant.57.clone.1.pair, bf16[1024,768]{1,0:T(8,128)(2,1)} %fusion.11.keys.values.first.qkv, bf16[1024,512]{1,0:T(8,128)(2,1)} %get-tuple-element.56.grad, bf16[4,2,128,128]{3,2,1,0:T(8,128)(2,1)} %bitcast.252), custom_call_target="tpu_custom_call" | custom-call | tf_op jit(solution)/shard_map/backward/pallas_call | solution.py:337
  134.7 6.1 %backward.3 = (bf16[1024,256]{1,0:T(8,128)(2,1)}, f32[2,1024,256]{2,1,0:T(8,128)}) custom-call(s32[1]{0:T(128)} %constant.59.clone.1.pair, bf16[1024,768]{1,0:T(8,128)(2,1)} %fusion.8.second.keys.values.qkv, bf16[1024,512]{1,0:T(8,128)(2,1)} %get-tuple-element.56.grad, bf16[4,2,128,128]{3,2,1,0:T(8,128)(2,1)} %bitcast.253), custom_call_target="tpu_custom_call" | custom-call | tf_op jit(solution)/shard_map/backward/pallas_call | solution.py:337
  142.5 7.8 %shard_map.84 = bf16[1,2,8,256,256]{4,3,2,1,0:T(8,128)(2,1)} custom-call(bf16[1024,256]{1,0:T(8,128)(2,1)} %get-tuple-element.60.q0, bf16[1024,256]{1,0:T(8,128)(2,1)} %get-tuple-element.61.q1, bf16[1024,2048]{1,0:T(8,128)(2,1)} %arrange.1.tokens), custom_call_target="tpu_custom_call" | custom-call | tf_op jit(solution)/shard_map/pallas_call | solution.py:394
  162.6 14.9 %shard_map.85 = bf16[2,2,8,256,256]{4,3,2,1,0:T(8,128)(2,1)} custom-call(bf16[1024,768]{1,0:T(8,128)(2,1)} %fusion.11.keys.values.first.qkv, bf16[1024,768]{1,0:T(8,128)(2,1)} %fusion.8.second.keys.values.qkv, f32[2,1024,256]{2,1,0:T(8,128)} %get-tuple-element.63.d_first, f32[2,1024,256]{2,1,0:T(8,128)} %get-tuple-element.64.d_second, ...), custom_call_target="tpu_custom_call" | custom-call | tf_op jit(solution)/shard_map/pallas_call | solution.py:394
  188.7 5.0 %collective-permute-done.51 = bf16[2,2,256,256]{3,2,0,1:T(8,128)(2,1)S(1)} collective-permute-done((bf16[2,2,256,256]{3,2,0,1:T(8,128)(2,1)S(1)}, bf16[2,2,256,256]{3,2,0,1:T(8,128)(2,1)S(1)}, u32[]{:S(2)}, u32[]{:S(2)}) %collective-permute-start.51) | collective-permute-done | bytes 524320 | tf_op jit(solution)/shard_map/ppermute | solution.py:55
  195.3 7.6 %collective-permute-done.35 = bf16[2,256,256]{2,1,0:T(8,128)(2,1)S(1)} collective-permute-done((bf16[2,256,256]{2,1,0:T(8,128)(2,1)S(1)}, bf16[2,256,256]{2,1,0:T(8,128)(2,1)S(1)}, u32[]{:S(2)}, u32[]{:S(2)}) %collective-permute-start.35) | collective-permute-done | bytes 262176 | tf_op jit(solution)/shard_map/ppermute | solution.py:55
  207.5 5.8 %collective-permute-done.36 = bf16[256,256]{1,0:T(8,128)(2,1)S(1)} collective-permute-done((bf16[256,256]{1,0:T(8,128)(2,1)S(1)}, bf16[256,256]{1,0:T(8,128)(2,1)S(1)}, u32[]{:S(2)}, u32[]{:S(2)}) %collective-permute-start.36) | collective-permute-done | bytes 131104 | tf_op jit(solution)/shard_map/ppermute | solution.py:55
  215.4 4.0 %collective-permute-done.25 = bf16[256,256]{1,0:T(8,128)(2,1)S(1)} collective-permute-done((bf16[256,256]{1,0:T(8,128)(2,1)S(1)}, bf16[256,256]{1,0:T(8,128)(2,1)S(1)}, u32[]{:S(2)}, u32[]{:S(2)}) %collective-permute-start.25) | collective-permute-done | bytes 131104 | tf_op jit(solution)/shard_map/ppermute | solution.py:55
  226.2 3.2 %collective-permute-start.29 = (bf16[256,256]{1,0:T(8,128)(2,1)S(1)}, bf16[256,256]{1,0:T(8,128)(2,1)S(1)}, u32[]{:S(2)}, u32[]{:S(2)}) collective-permute-start(bf16[256,256]{1,0:T(8,128)(2,1)S(1)} %slice_bitcast_fusion.32), channel_id=1, source_target_pairs={{2,4},{4,2},{6,0},{0,6},{3,5},{5,3},{7,1},{1,7},{10,12},{12,10},{1... | collective-permute-start | bytes 393224 | tf_op jit(solution)/shard_map/ppermute | solution.py:55
  237.4 3.6 %collective-permute-done.55 = bf16[1,256,256]{2,1,0:T(8,128)(2,1)S(1)} collective-permute-done((bf16[1,256,256]{2,1,0:T(8,128)(2,1)S(1)}, bf16[1,256,256]{2,1,0:T(8,128)(2,1)S(1)}, u32[]{:S(2)}, u32[]{:S(2)}) %collective-permute-start.55) | collective-permute-done | bytes 131104 | tf_op jit(solution)/shard_map/ppermute | solution.py:55
  250.2 3.3 %collective-permute-done.31 = bf16[2,256,256]{2,1,0:T(8,128)(2,1)S(1)} collective-permute-done((bf16[2,256,256]{2,1,0:T(8,128)(2,1)S(1)}, bf16[2,256,256]{2,1,0:T(8,128)(2,1)S(1)}, u32[]{:S(2)}, u32[]{:S(2)}) %collective-permute-start.31) | collective-permute-done | bytes 262176 | tf_op jit(solution)/shard_map/ppermute | solution.py:55
  254.7 4.6 %collective-permute-done.42 = bf16[2,256,256]{2,1,0:T(8,128)(2,1)S(1)} collective-permute-done((bf16[2,256,256]{2,1,0:T(8,128)(2,1)S(1)}, bf16[2,256,256]{2,1,0:T(8,128)(2,1)S(1)}, u32[]{:S(2)}, u32[]{:S(2)}) %collective-permute-start.42) | collective-permute-done | bytes 262176 | tf_op jit(solution)/shard_map/ppermute | solution.py:55
  262.5 4.1 %collective-permute-done.50.refs_5_ = bf16[1,256,256]{2,1,0:T(8,128)(2,1)S(1)} collective-permute-done((bf16[1,256,256]{2,1,0:T(8,128)(2,1)S(1)}, bf16[1,256,256]{2,1,0:T(8,128)(2,1)S(1)}, u32[]{:S(2)}, u32[]{:S(2)}) %collective-permute-start.50) | collective-permute-done | bytes 131104 | tf_op jit(solution)/shard_map/ppermute | solution.py:55
  268.1 2.6 sort_pieces.1
  274.2 13.2 %adam.1 = (f32[256,3072]{1,0:T(8,128)}, f32[256,3072]{1,0:T(8,128)}, f32[256,3072]{1,0:T(8,128)}) custom-call(s32[1]{0:T(128)} %bitcast.core, bf16[6,256,256]{2,1,0:T(8,128)(2,1)} %get-tuple-element.67.kept, bf16[6,256,256]{2,1,0:T(8,128)(2,1)} %copy-done.8, f32[256,3072]{1,0:T(8,128)} %weights.1, f32[256,3072]{1,0:T(8,128)} %first.1, f32[256,3072]{1,0:T(8,128)} %second.1), custom_call_target="tpu_custom_call" | custom-call | tf_op jit(solution)/shard_map/adam/pallas_call | solution.py:509
  (250 shorter events, 110.5 us)
Async XLA Ops:
  3.8 25.1 %collective-permute-start.5 = (bf16[512,2048]{1,0:T(8,128)(2,1)}, bf16[512,2048]{1,0:T(8,128)(2,1)}, u32[]{:S(2)}, u32[]{:S(2)}) collective-permute-start(bf16[512,2048]{1,0:T(8,128)(2,1)} %bitcast.10.own), channel_id=1, source_target_pairs={{0,1},{1,0},{2,3},{3,2},{4,5},{5,4},{6,7},{7,6},{8,9},{9,8},{10,11... | collective-permute-start | bytes 6291464 | tf_op jit(solution)/shard_map/ppermute | solution.py:54
  15.9 10.1 %collective-permute-start.4 = (bf16[2,256,384]{2,1,0:T(8,128)(2,1)S(1)}, bf16[2,256,384]{2,1,0:T(8,128)(2,1)}, u32[]{:S(2)}, u32[]{:S(2)}) collective-permute-start(bf16[2,256,384]{2,1,0:T(8,128)(2,1)S(1)} %pad_maximum_fusion.5), channel_id=1, source_target_pairs={{0,2},{2,0},{4,6},{6,4},{1,3},{3,1},{5,7},{7,5},{8,10},{10,8},{12,... | collective-permute-start | bytes 1179656 | tf_op jit(solution)/shard_map/ppermute | solution.py:55
  17.9 9.8 %collective-permute-start.2 = (bf16[2,256,384]{2,1,0:T(8,128)(2,1)S(1)}, bf16[2,256,384]{2,1,0:T(8,128)(2,1)}, u32[]{:S(2)}, u32[]{:S(2)}) collective-permute-start(bf16[2,256,384]{2,1,0:T(8,128)(2,1)S(1)} %pad_maximum_fusion.4), channel_id=1, source_target_pairs={{2,4},{4,2},{6,0},{0,6},{3,5},{5,3},{7,1},{1,7},{10,12},{12,10},{1... | collective-permute-start | bytes 1179656 | tf_op jit(solution)/shard_map/ppermute | solution.py:55
  36.3 14.0 %collective-permute-start.10 = (bf16[2,256,384]{2,1,0:T(8,128)(2,1)S(1)}, bf16[2,256,384]{2,1,0:T(8,128)(2,1)S(1)}, u32[]{:S(2)}, u32[]{:S(2)}) collective-permute-start(bf16[2,256,384]{2,1,0:T(8,128)(2,1)S(1)} %get-tuple-element.90), channel_id=1, source_target_pairs={{0,32},{32,0},{64,96},{96,64},{1,33},{33,1},{65,97},{97,65},{2,34}... | collective-permute-start | bytes 1179656 | tf_op jit(solution)/shard_map/ppermute | solution.py:55
  42.4 11.0 %collective-permute-start.11 = (bf16[2,256,384]{2,1,0:T(8,128)(2,1)S(1)}, bf16[2,256,384]{2,1,0:T(8,128)(2,1)S(1)}, u32[]{:S(2)}, u32[]{:S(2)}) collective-permute-start(bf16[2,256,384]{2,1,0:T(8,128)(2,1)S(1)} %get-tuple-element.89), channel_id=1, source_target_pairs={{32,64},{64,32},{96,0},{0,96},{33,65},{65,33},{97,1},{1,97},{34,66... | collective-permute-start | bytes 1179656 | tf_op jit(solution)/shard_map/ppermute | solution.py:55
  43.8 10.1 %collective-permute-start.12 = (bf16[2,256,384]{2,1,0:T(8,128)(2,1)S(1)}, bf16[2,256,384]{2,1,0:T(8,128)(2,1)S(1)}, u32[]{:S(2)}, u32[]{:S(2)}) collective-permute-start(bf16[2,256,384]{2,1,0:T(8,128)(2,1)S(1)} %get-tuple-element.92), channel_id=1, source_target_pairs={{0,8},{8,0},{16,24},{24,16},{1,9},{9,1},{17,25},{25,17},{2,10},{10... | collective-permute-start | bytes 1179656 | tf_op jit(solution)/shard_map/ppermute | solution.py:55
  48.3 10.4 %collective-permute-start.13 = (bf16[2,256,384]{2,1,0:T(8,128)(2,1)S(1)}, bf16[2,256,384]{2,1,0:T(8,128)(2,1)S(1)}, u32[]{:S(2)}, u32[]{:S(2)}) collective-permute-start(bf16[2,256,384]{2,1,0:T(8,128)(2,1)S(1)} %get-tuple-element.91), channel_id=1, source_target_pairs={{8,16},{16,8},{24,0},{0,24},{9,17},{17,9},{25,1},{1,25},{10,18},{1... | collective-permute-start | bytes 1179656 | tf_op jit(solution)/shard_map/ppermute | solution.py:55
  50.2 16.2 %collective-permute-start.9 = (bf16[2,256,384]{2,1,0:T(8,128)(2,1)S(1)}, bf16[2,256,384]{2,1,0:T(8,128)(2,1)}, u32[]{:S(2)}, u32[]{:S(2)}) collective-permute-start(bf16[2,256,384]{2,1,0:T(8,128)(2,1)S(1)} %pad_maximum_fusion.7), channel_id=1, source_target_pairs={{0,2},{2,0},{4,6},{6,4},{1,3},{3,1},{5,7},{7,5},{8,10},{10,8},{12,... | collective-permute-start | bytes 1179656 | tf_op jit(solution)/shard_map/ppermute | solution.py:55
  50.3 17.2 %collective-permute-start.7 = (bf16[2,256,384]{2,1,0:T(8,128)(2,1)S(1)}, bf16[2,256,384]{2,1,0:T(8,128)(2,1)}, u32[]{:S(2)}, u32[]{:S(2)}) collective-permute-start(bf16[2,256,384]{2,1,0:T(8,128)(2,1)S(1)} %pad_maximum_fusion.6), channel_id=1, source_target_pairs={{2,4},{4,2},{6,0},{0,6},{3,5},{5,3},{7,1},{1,7},{10,12},{12,10},{1... | collective-permute-start | bytes 1179656 | tf_op jit(solution)/shard_map/ppermute | solution.py:55
  69.4 9.5 %collective-permute-start.15 = (bf16[2,256,384]{2,1,0:T(8,128)(2,1)S(1)}, bf16[2,256,384]{2,1,0:T(8,128)(2,1)S(1)}, u32[]{:S(2)}, u32[]{:S(2)}) collective-permute-start(bf16[2,256,384]{2,1,0:T(8,128)(2,1)S(1)} %get-tuple-element.85), channel_id=1, source_target_pairs={{32,64},{64,32},{96,0},{0,96},{33,65},{65,33},{97,1},{1,97},{34,66... | collective-permute-start | bytes 1179656 | tf_op jit(solution)/shard_map/ppermute | solution.py:55
  88.5 15.5 %all-to-all-start = ((f32[16,64,128]{2,1,0:T(8,128)}), f32[16,64,128]{2,1,0:T(8,128)S(1)}, u32[]{:S(2)}, u32[]{:S(2)}) async-start(f32[16,64,128]{2,1,0:T(8,128)} %bitcast.250), calls=%async_computation | async-start | bytes 1048576 | tf_op jit(solution)/shard_map/all_to_all | solution.py:216
  94.0 22.9 %collective-permute-start.18 = (bf16[512,512]{1,0:T(8,128)(2,1)S(1)}, bf16[512,512]{1,0:T(8,128)(2,1)S(1)}, u32[]{:S(2)}, u32[]{:S(2)}) collective-permute-start(bf16[512,512]{1,0:T(8,128)(2,1)S(1)} %copy-done.16), channel_id=1, source_target_pairs={{0,1},{1,0},{2,3},{3,2},{4,5},{5,4},{6,7},{7,6},{8,9},{9,8},{10,11... | collective-permute-start | bytes 1572872 | tf_op jit(solution)/shard_map/ppermute | solution.py:54
  106.6 12.0 %all-to-all-start.1 = ((bf16[16,64,128]{2,1,0:T(8,128)(2,1)}), bf16[16,64,128]{2,1,0:T(8,128)(2,1)S(1)}, u32[]{:S(2)}, u32[]{:S(2)}) async-start(bf16[16,64,128]{2,1,0:T(8,128)(2,1)} %running.1), calls=%async_computation.1 | async-start | bytes 524288 | tf_op jit(solution)/shard_map/all_to_all | solution.py:224
  140.9 11.0 %collective-permute-start.22 = (bf16[4,2,128,128]{3,2,1,0:T(8,128)(2,1)S(1)}, bf16[4,2,128,128]{3,2,1,0:T(8,128)(2,1)S(1)}, u32[]{:S(2)}, u32[]{:S(2)}) collective-permute-start(bf16[4,2,128,128]{3,2,1,0:T(8,128)(2,1)S(1)} %fusion.32), channel_id=1, source_target_pairs={{0,32},{32,0},{64,96},{96,64},{1,33},{33,1},{65,97},{97,65},{2,34}... | collective-permute-start | bytes 786440 | tf_op jit(solution)/shard_map/ppermute | solution.py:55
  156.8 114.0 %collective-permute-start.19 = (bf16[512,512]{1,0:T(8,128)(2,1)}, bf16[512,512]{1,0:T(8,128)(2,1)S(1)}, u32[]{:S(2)}, u32[]{:S(2)}) collective-permute-start(bf16[512,512]{1,0:T(8,128)(2,1)} %slice.276), channel_id=1, source_target_pairs={{0,1},{1,0},{2,3},{3,2},{4,5},{5,4},{6,7},{7,6},{8,9},{9,8},{10,11... | collective-permute-start | bytes 1572872 | tf_op jit(solution)/shard_map/ppermute | solution.py:54
  157.6 27.4 %collective-permute-start.34 = (bf16[2,2,256,256]{3,2,0,1:T(8,128)(2,1)}, bf16[2,2,256,256]{3,2,0,1:T(8,128)(2,1)}, u32[]{:S(2)}, u32[]{:S(2)}) collective-permute-start(bf16[2,2,256,256]{3,2,0,1:T(8,128)(2,1)} %copy_bitcast_fusion.4), channel_id=1, source_target_pairs={{0,8},{8,0},{16,24},{24,16},{1,9},{9,1},{17,25},{25,17},{2,10},{10... | collective-permute-start | bytes 1572872 | tf_op jit(solution)/shard_map/ppermute | solution.py:55
  159.0 28.3 %collective-permute-start.23 = (bf16[2,2,256,256]{3,2,1,0:T(8,128)(2,1)}, bf16[2,2,256,256]{3,2,1,0:T(8,128)(2,1)}, u32[]{:S(2)}, u32[]{:S(2)}) collective-permute-start(bf16[2,2,256,256]{3,2,1,0:T(8,128)(2,1)} %dynamic-slice_bitcast_fusion.1), channel_id=1, source_target_pairs={{0,32},{32,0},{64,96},{96,64},{1,33},{33,1},{65,97},{97,65},{2,34}... | collective-permute-start | bytes 1572872 | tf_op jit(solution)/shard_map/ppermute | solution.py:55
  179.7 14.0 %collective-permute-start.51 = (bf16[2,2,256,256]{3,2,0,1:T(8,128)(2,1)S(1)}, bf16[2,2,256,256]{3,2,0,1:T(8,128)(2,1)S(1)}, u32[]{:S(2)}, u32[]{:S(2)}) collective-permute-start(bf16[2,2,256,256]{3,2,0,1:T(8,128)(2,1)S(1)} %bitcast.267), channel_id=1, source_target_pairs={{8,16},{16,8},{24,0},{0,24},{9,17},{17,9},{25,1},{1,25},{10,18},{1... | collective-permute-start | bytes 1572872 | tf_op jit(solution)/shard_map/ppermute | solution.py:55
  181.3 13.6 %collective-permute-start.44 = (bf16[2,2,256,256]{3,2,1,0:T(8,128)(2,1)S(1)}, bf16[2,2,256,256]{3,2,1,0:T(8,128)(2,1)S(1)}, u32[]{:S(2)}, u32[]{:S(2)}) collective-permute-start(bf16[2,2,256,256]{3,2,1,0:T(8,128)(2,1)S(1)} %dynamic-slice_bitcast_fusion), channel_id=1, source_target_pairs={{32,64},{64,32},{96,0},{0,96},{33,65},{65,33},{97,1},{1,97},{34,66... | collective-permute-start | bytes 1572872 | tf_op jit(solution)/shard_map/ppermute | solution.py:55
  185.0 19.1 %collective-permute-start.37 = (bf16[2,2,256,256]{3,2,0,1:T(8,128)(2,1)S(1)}, bf16[2,2,256,256]{3,2,0,1:T(8,128)(2,1)S(1)}, u32[]{:S(2)}, u32[]{:S(2)}) collective-permute-start(bf16[2,2,256,256]{3,2,0,1:T(8,128)(2,1)S(1)} %bitcast.266), channel_id=1, source_target_pairs={{2,4},{4,2},{6,0},{0,6},{3,5},{5,3},{7,1},{1,7},{10,12},{12,10},{1... | collective-permute-start | bytes 1572872 | tf_op jit(solution)/shard_map/ppermute | solution.py:55
  187.3 19.1 %collective-permute-start.27 = (bf16[2,2,256,256]{3,2,0,1:T(8,128)(2,1)S(1)}, bf16[2,2,256,256]{3,2,0,1:T(8,128)(2,1)S(1)}, u32[]{:S(2)}, u32[]{:S(2)}) collective-permute-start(bf16[2,2,256,256]{3,2,0,1:T(8,128)(2,1)S(1)} %copy.12), channel_id=1, source_target_pairs={{0,2},{2,0},{4,6},{6,4},{1,3},{3,1},{5,7},{7,5},{8,10},{10,8},{12,... | collective-permute-start | bytes 1572872 | tf_op jit(solution)/shard_map/ppermute | solution.py:55
  195.0 9.3 %collective-permute-start.24 = (bf16[2,256,256]{2,1,0:T(8,128)(2,1)S(1)}, bf16[2,256,256]{2,1,0:T(8,128)(2,1)S(1)}, u32[]{:S(2)}, u32[]{:S(2)}) collective-permute-start(bf16[2,256,256]{2,1,0:T(8,128)(2,1)S(1)} %slice_bitcast_fusion.6), channel_id=1, source_target_pairs={{0,2},{2,0},{4,6},{6,4},{1,3},{3,1},{5,7},{7,5},{8,10},{10,8},{12,... | collective-permute-start | bytes 786440 | tf_op jit(solution)/shard_map/ppermute | solution.py:55
  202.9 17.3 %collective-permute-start.52 = (bf16[2,256,256]{2,1,0:T(8,128)(2,1)S(1)}, bf16[2,256,256]{2,1,0:T(8,128)(2,1)S(1)}, u32[]{:S(2)}, u32[]{:S(2)}) collective-permute-start(bf16[2,256,256]{2,1,0:T(8,128)(2,1)S(1)} %slice_bitcast_fusion), channel_id=1, source_target_pairs={{2,4},{4,2},{6,0},{0,6},{3,5},{5,3},{7,1},{1,7},{10,12},{12,10},{1... | collective-permute-start | bytes 786440 | tf_op jit(solution)/shard_map/ppermute | solution.py:55
  204.0 16.3 %collective-permute-start.45 = (bf16[2,256,256]{2,1,0:T(8,128)(2,1)S(1)}, bf16[2,256,256]{2,1,0:T(8,128)(2,1)S(1)}, u32[]{:S(2)}, u32[]{:S(2)}) collective-permute-start(bf16[2,256,256]{2,1,0:T(8,128)(2,1)S(1)} %slice_bitcast_fusion.2), channel_id=1, source_target_pairs={{0,2},{2,0},{4,6},{6,4},{1,3},{3,1},{5,7},{7,5},{8,10},{10,8},{12,... | collective-permute-start | bytes 786440 | tf_op jit(solution)/shard_map/ppermute | solution.py:55
  206.5 16.1 %collective-permute-start.38 = (bf16[2,256,256]{2,1,0:T(8,128)(2,1)S(1)}, bf16[2,256,256]{2,1,0:T(8,128)(2,1)S(1)}, u32[]{:S(2)}, u32[]{:S(2)}) collective-permute-start(bf16[2,256,256]{2,1,0:T(8,128)(2,1)S(1)} %dynamic-slice_bitcast_fusion.2), channel_id=1, source_target_pairs={{0,8},{8,0},{16,24},{24,16},{1,9},{9,1},{17,25},{25,17},{2,10},{10... | collective-permute-start | bytes 786440 | tf_op jit(solution)/shard_map/ppermute | solution.py:55
  220.4 9.9 %collective-permute-start.46 = (bf16[256,256]{1,0:T(8,128)(2,1)S(1)}, bf16[256,256]{1,0:T(8,128)(2,1)S(1)}, u32[]{:S(2)}, u32[]{:S(2)}) collective-permute-start(bf16[256,256]{1,0:T(8,128)(2,1)S(1)} %slice_bitcast_fusion.26), channel_id=1, source_target_pairs={{2,4},{4,2},{6,0},{0,6},{3,5},{5,3},{7,1},{1,7},{10,12},{12,10},{1... | collective-permute-start | bytes 393224 | tf_op jit(solution)/shard_map/ppermute | solution.py:55
  231.6 10.4 %collective-permute-start.40 = (bf16[2,256,256]{2,1,0:T(8,128)(2,1)S(1)}, bf16[2,256,256]{2,1,0:T(8,128)(2,1)S(1)}, u32[]{:S(2)}, u32[]{:S(2)}) collective-permute-start(bf16[2,256,256]{2,1,0:T(8,128)(2,1)S(1)} %pad_maximum_fusion.9), channel_id=1, source_target_pairs={{8,16},{16,8},{24,0},{0,24},{9,17},{17,9},{25,1},{1,25},{10,18},{1... | collective-permute-start | bytes 786440 | tf_op jit(solution)/shard_map/ppermute | solution.py:55
  233.5 10.9 %collective-permute-start.30 = (bf16[2,256,256]{2,1,0:T(8,128)(2,1)S(1)}, bf16[2,256,256]{2,1,0:T(8,128)(2,1)S(1)}, u32[]{:S(2)}, u32[]{:S(2)}) collective-permute-start(bf16[2,256,256]{2,1,0:T(8,128)(2,1)S(1)} %pad_maximum_fusion.8), channel_id=1, source_target_pairs={{32,64},{64,32},{96,0},{0,96},{33,65},{65,33},{97,1},{1,97},{34,66... | collective-permute-start | bytes 786440 | tf_op jit(solution)/shard_map/ppermute | solution.py:55
  236.4 9.5 %collective-permute-start.48 = (bf16[1,256,256]{2,1,0:T(8,128)(2,1)S(1)}, bf16[1,256,256]{2,1,0:T(8,128)(2,1)S(1)}, u32[]{:S(2)}, u32[]{:S(2)}) collective-permute-start(bf16[1,256,256]{2,1,0:T(8,128)(2,1)S(1)} %add_convert_fusion.11), channel_id=1, source_target_pairs={{0,32},{32,0},{64,96},{96,64},{1,33},{33,1},{65,97},{97,65},{2,34}... | collective-permute-start | bytes 393224 | tf_op jit(solution)/shard_map/ppermute | solution.py:55
  241.0 12.8 %collective-permute-start.56 = (bf16[1,256,256]{2,1,0:T(8,128)(2,1)S(1)}, bf16[1,256,256]{2,1,0:T(8,128)(2,1)S(1)}, u32[]{:S(2)}, u32[]{:S(2)}) collective-permute-start(bf16[1,256,256]{2,1,0:T(8,128)(2,1)S(1)} %add_convert_fusion.7), channel_id=1, source_target_pairs={{32,64},{64,32},{96,0},{0,96},{33,65},{65,33},{97,1},{1,97},{34,66... | collective-permute-start | bytes 393224 | tf_op jit(solution)/shard_map/ppermute | solution.py:55
  246.0 14.4 %collective-permute-start.49 = (bf16[1,256,256]{2,1,0:T(8,128)(2,1)S(1)}, bf16[1,256,256]{2,1,0:T(8,128)(2,1)S(1)}, u32[]{:S(2)}, u32[]{:S(2)}) collective-permute-start(bf16[1,256,256]{2,1,0:T(8,128)(2,1)S(1)} %add_convert_fusion.10), channel_id=1, source_target_pairs={{8,16},{16,8},{24,0},{0,24},{9,17},{17,9},{25,1},{1,25},{10,18},{1... | collective-permute-start | bytes 393224 | tf_op jit(solution)/shard_map/ppermute | solution.py:55
  250.1 9.2 %collective-permute-start.42 = (bf16[2,256,256]{2,1,0:T(8,128)(2,1)S(1)}, bf16[2,256,256]{2,1,0:T(8,128)(2,1)S(1)}, u32[]{:S(2)}, u32[]{:S(2)}) collective-permute-start(bf16[2,256,256]{2,1,0:T(8,128)(2,1)S(1)} %add_convert_fusion.1), channel_id=1, source_target_pairs={{0,32},{32,0},{64,96},{96,64},{1,33},{33,1},{65,97},{97,65},{2,34}... | collective-permute-start | bytes 786440 | tf_op jit(solution)/shard_map/ppermute | solution.py:55
  (46 other events, 285.1 us)
where the time goes:
time: 290 us; the launch traced here: 287 us
  waiting for transfers between devices  85.9 us (30%)
  Pallas kernels  80.9 us (28%)
  starting transfers between devices  79.3 us (27%)
  local copies, waits for them, and re-layouts  15.9 us (5%)
  other arithmetic  14.6 us (5%)
  matrix products  9.01 us (3%)
    ppermute x54, waiting for transfers between devices, swap(): return lax.ppermute(x, dim[0], PAIRS[dim[1]])  70.9 us
    ppermute x54, starting transfers between devices, swap(): return lax.ppermute(x, dim[0], PAIRS[dim[1]])  69.6 us
    pallas_call x2, Pallas kernels, gradient_call(): pl.pallas_call(kernel, grid=(count,), in_specs=specs + [VMEM], out_specs=...  22.7 us
    pallas_call x1, Pallas kernels, adam(): pl.pallas_call(adam_kernel, name='adam', grid_spec=pltpu.PrefetchScalarGr...  13.2 us
    pallas_call x2, Pallas kernels, backward(): pl.pallas_call(backward_kernel, name='backward', grid_spec=pltpu.Prefetch...  12.2 us
    all_to_all x1, waiting for transfers between devices, earlier_states(): received = lax.all_to_all(cut, ('x', 'y'), 0, 0, tiled=True)  9.99 us
    dot_general x2, matrix products, project(): qkv = jnp.dot(tokens, weights, preferred_element_type=F32).astype(BF)  9.01 us
    pallas_call x1, Pallas kernels, arrange(): pl.pallas_call(arrange_kernel, name='arrange', grid_spec=pltpu.PrefetchSc...  7.33 us
  transfers between devices with their start and end apart: 61, of which 29 were waited for; matrix products, arithmetic and copies ran while one was open for 10% of the time, Pallas kernels for 17%

commit v1 on v0

--- a/solution.py
+++ b/solution.py
@@ -1,3 +1,5 @@
+import functools
+
 import jax
 import jax.numpy as jnp
 from jax import lax
@@ -32,8 +34,8 @@
 HALVING = [
     ("x0", "z0", "z1"),
     ("y0", "z1", "z0"),
-    ("z0", "x0", "z1"),
-    ("z1", "y0", "z0"),
+    ("x0", "z0", "z1"),
+    ("y0", "z1", "z0"),
     ("x1", "z0", "z1"),
     ("y1", "z1", "z0"),
 ]
@@ -150,12 +152,26 @@
     )(blocks, own, other)
 
 
-def outer_kernel(pair, keys, values, before, kv):
-    for h in range(2):
-        kv[h, 0] = dot(keys[:, cols(h)], values[:, cols(h)], 0, 0)
-
-
-def project(pair, tokens, pieces, before):
+def outer_kernel(k0, v0, k1, v1, kv):
+    for pair, (keys, values) in enumerate(((k0, v0), (k1, v1))):
+        for h in range(2):
+            kv[2 * pair + h, 0] = dot(keys[:, cols(h)], values[:, cols(h)], 0, 0)
+
+
+def own_states(first, second):
+    keys = pl.BlockSpec((BLOCK, 256), lambda s: (s, 1))
+    values = pl.BlockSpec((BLOCK, 256), lambda s: (s, 2))
+    return pl.pallas_call(
+        outer_kernel,
+        name="outer",
+        grid=(2,),
+        in_specs=[keys, values, keys, values],
+        out_specs=pl.BlockSpec((HEADS_CORE, 1, HDIM, HDIM), lambda s: (0, s, 0, 0)),
+        out_shape=shape((HEADS_CORE, 2, HDIM, HDIM), F32),
+    )(first, first, second, second)
+
+
+def project(tokens, pieces):
     chunks = []
     for h, order in enumerate(GATHER_ORDERS):
         mine, low, high = pieces[3 * h : 3 * h + 3]
@@ -167,24 +183,7 @@
             rows.append(theirs[place // 2][place % 2] if i & 1 else mine[place])
         chunks.append(jnp.concatenate(rows, 0))
     weights = jnp.concatenate(chunks, 1)
-    qkv = jnp.dot(tokens, weights, preferred_element_type=F32).astype(BF)
-    kv = pl.pallas_call(
-        outer_kernel,
-        name="outer",
-        grid_spec=pltpu.PrefetchScalarGridSpec(
-            num_scalar_prefetch=1,
-            grid=(2,),
-            in_specs=[
-                pl.BlockSpec((BLOCK, 256), lambda s, p: (s, 1)),
-                pl.BlockSpec((BLOCK, 256), lambda s, p: (s, 2)),
-                pl.BlockSpec(memory_space=pl.ANY),
-            ],
-            out_specs=pl.BlockSpec((2, 1, HDIM, HDIM), lambda s, p: (p[0], s, 0, 0)),
-        ),
-        out_shape=shape((HEADS_CORE, 2, HDIM, HDIM), F32),
-        input_output_aliases={3: 0},
-    )(jnp.full((1,), pair, jnp.int32), qkv, qkv, before)
-    return qkv, kv
+    return jnp.dot(tokens, weights, preferred_element_type=F32).astype(BF)
 
 
 def lower_scores(a, b):
@@ -322,10 +321,9 @@
 
 
 def backward_kernel(pair, qkv, grad, state, dq, dkv):
-    @each_head
-    def _(h):
-        q, k, v = [head_of(qkv, h, j) for j in "qkv"]
-        at = head_cols(h)
+    for h in range(2):
+        q, k, v = [qkv[:, cols(2 * j + h)] for j in range(3)]
+        at = cols(h)
         g = grad[:, at]
         back = lower_scores(g, v)
         dq[:, at] = (times(back, k) + dot(g, state[h, 0], 1, 1)).astype(BF)
@@ -355,14 +353,15 @@
 
 
 def multiply_blocks(turned, tokens, out):
-    def block(i, carry):
-        at = pl.ds(pl.multiple_of(i * 256, 256), 256)
+    def blocks(i, carry):
+        at = pl.ds(pl.multiple_of(i * 512, 512), 512)
         piece = dot(turned[...], tokens[:, at], 1, 0).astype(BF)
-        out[0, 0, i] = piece[:256]
-        out[0, 1, i] = piece[256:]
+        for half in range(2):
+            for j in range(2):
+                out[half, 2 * i + j] = piece[half * 256 : (half + 1) * 256, j * 256 : (j + 1) * 256]
         return carry
 
-    lax.fori_loop(0, tokens.shape[1] // 256, block, 0)
+    lax.fori_loop(0, tokens.shape[1] // 512, blocks, 0)
 
 
 def query_gradient_kernel(q0, q1, tokens, out, turned):
@@ -371,52 +370,46 @@
     multiply_blocks(turned, tokens, out)
 
 
-def gradient_kernel(first, second, d_first, d_second, state, tokens, out, turned):
-    kind = pl.program_id(0)
+def gradient_kernel(kind, first, second, d_first, d_second, state, tokens, out, turned):
     for pair, (rows, within) in enumerate(((first, d_first), (second, d_second))):
-
-        @each_head
-        def _(h):
+        for h in range(2):
             head = 2 * pair + h
-            at = head_cols(h)
             for s in range(2):
                 span = slice(s * BLOCK, (s + 1) * BLOCK)
-                later = state[head, s]
-                later = jnp.where(kind == 0, later.T, later)
-                total = within[0, span, at] + dot(rows[span, at], later, 1, 0)
-                turned[head_cols(head), span] = total.astype(BF).T
+                later = dot(rows[span, cols(h)], state[head, s], 1, 1 - kind)
+                total = within[0, span, cols(h)] + later
+                turned[cols(head), span] = total.astype(BF).T
 
     multiply_blocks(turned, tokens, out)
 
 
-def gradient_call(kernel, count, ins, specs, tokens):
+def gradient_call(kernel, ins, specs, tokens):
     blocks = tokens.shape[1] // 256
     return pl.pallas_call(
         kernel,
-        grid=(count,),
+        grid=(1,),
         in_specs=specs + [VMEM],
-        out_specs=pl.BlockSpec((1, 2, blocks, 256, 256), lambda j: (j, 0, 0, 0, 0)),
-        out_shape=shape((count, 2, blocks, 256, 256), BF),
+        out_specs=VMEM,
+        out_shape=shape((2, blocks, 256, 256), BF),
         scratch_shapes=[pltpu.VMEM((WIDTH, ROWS), BF)],
     )(*ins, tokens)
 
 
 def query_gradient(q0, q1, tokens):
-    return gradient_call(query_gradient_kernel, 1, (q0, q1), [VMEM] * 2, tokens)
-
-
-def key_value_gradient(first, second, d_first, d_second, state, tokens):
-    rows = pl.BlockSpec((ROWS, 256), lambda j: (0, 2 - j))
-    within = pl.BlockSpec((1, ROWS, 256), lambda j: (j, 0, 0))
+    return gradient_call(query_gradient_kernel, (q0, q1), [VMEM] * 2, tokens)
+
+
+def key_value_gradient(kind, first, second, d_first, d_second, state, tokens):
+    rows = pl.BlockSpec((ROWS, 256), lambda _: (0, 2 - kind))
+    within = pl.BlockSpec((1, ROWS, 256), lambda _: (kind, 0, 0))
     specs = [rows, rows, within, within, VMEM]
     ins = (first, second, d_first, d_second, state)
-    return gradient_call(gradient_kernel, 2, ins, specs, tokens)
+    kernel = functools.partial(gradient_kernel, kind)
+    return gradient_call(kernel, ins, specs, tokens)
 
 
 def parts_of(partial):
-    return [
-        partial[j, i].reshape(2, 2, 2, 256, 256) for j in range(partial.shape[0]) for i in range(2)
-    ]
+    return [partial[i].reshape(2, 2, 2, 256, 256) for i in range(2)]
 
 
 def wide(x):
@@ -427,7 +420,7 @@
     return (wide(a) + wide(b)).astype(BF)
 
 
-def reduce_part(part, order):
+def reduce_steps(part, order):
     left = ["z0", "z1", "flat"]
     for dim in order:
         name = dim if dim[0] == "z" else "flat"
@@ -440,8 +433,9 @@
         else:
             send = lax.index_in_dim(part, 1, axis, False)
             keep = lax.index_in_dim(part, 0, axis, False)
-        part = add(keep, swap(send, dim))
-    return part
+        received = yield swap(send, dim)
+        part = add(keep, received)
+    yield part
 
 
 def finish_group(parts, exchanged, last):
@@ -465,18 +459,13 @@
 
 def sort_kernel(holds, *refs):
     kept, sent = refs[-2:]
-
-    def rows(i, carry):
-        at = pl.ds(pl.multiple_of(i * 64, 64), 64)
-        for g, (members, _, _) in enumerate(GROUPS):
-            straight = holds[g] == 1
-            for j, p in enumerate(members):
-                here, there = refs[2 * g][j, at, :], refs[2 * g + 1][j, at, :]
-                kept[p, at, :] = jnp.where(straight, here, there)
-                sent[p, at, :] = jnp.where(straight, there, here)
-        return carry
-
-    lax.fori_loop(0, 4, rows, 0)
+    for g, (members, _, _) in enumerate(GROUPS):
+        straight = holds[g] == 1
+        for j, p in enumerate(members):
+            at = slice(p * 256, (p + 1) * 256)
+            here, there = refs[2 * g][j].T, refs[2 * g + 1][j].T
+            kept[:, at] = jnp.where(straight, here, there)
+            sent[:, at] = jnp.where(straight, there, here)
 
 
 def sort_pieces(holds, finished):
@@ -485,33 +474,35 @@
         name="sort_pieces",
         in_specs=[pl.BlockSpec(memory_space=pltpu.SMEM)] + [VMEM] * len(finished),
         out_specs=(VMEM, VMEM),
-        out_shape=(shape((6, 256, 256), BF),) * 2,
+        out_shape=(shape((256, 3 * WIDTH), BF),) * 2,
     )(holds, *finished)
 
 
 def adam_kernel(core, kept, received, weights, first, second, out_weights, out_first, out_second):
-    straight = (pl.program_id(0) // 2) % 2 == core[0]
-    gradient = jnp.where(straight, kept[0], received[0]).astype(F32).T
-    new_first = BETA_ONE * first[...] + (1.0 - BETA_ONE) * gradient
-    new_second = BETA_TWO * second[...] + (1.0 - BETA_TWO) * gradient * gradient
-    first_hat = new_first / (1.0 - BETA_ONE**STEP)
-    second_hat = new_second / (1.0 - BETA_TWO**STEP)
-    out_first[...] = new_first
-    out_second[...] = new_second
-    out_weights[...] = weights[...] - LEARN_RATE * (
-        first_hat / (jnp.sqrt(second_hat) + EPS_ADAM) + DECAY_WEIGHT * weights[...]
-    )
+    for block in range(6):
+        at = slice(block * WIDTH, (block + 1) * WIDTH)
+        source = slice((block // 2) * WIDTH, (block // 2 + 1) * WIDTH)
+        gradient = jnp.where(block % 2 == core[0], kept[:, source], received[:, source]).astype(F32)
+        new_first = BETA_ONE * first[:, at] + (1.0 - BETA_ONE) * gradient
+        new_second = BETA_TWO * second[:, at] + (1.0 - BETA_TWO) * gradient * gradient
+        first_hat = new_first / (1.0 - BETA_ONE**STEP)
+        second_hat = new_second / (1.0 - BETA_TWO**STEP)
+        out_first[:, at] = new_first
+        out_second[:, at] = new_second
+        out_weights[:, at] = weights[:, at] - LEARN_RATE * (
+            first_hat / (jnp.sqrt(second_hat) + EPS_ADAM) + DECAY_WEIGHT * weights[:, at]
+        )
 
 
 def adam(core, kept, received, *arrays):
-    piece = pl.BlockSpec((1, 256, 256), lambda n, c: (2 * (n // 4) + n % 2, 0, 0))
-    block = pl.BlockSpec((256, 256), lambda n, c: (0, n))
+    piece = pl.BlockSpec((32, 3 * WIDTH), lambda i, c: (i, 0))
+    block = pl.BlockSpec((32, 6 * WIDTH), lambda i, c: (i, 0))
     return pl.pallas_call(
         adam_kernel,
         name="adam",
         grid_spec=pltpu.PrefetchScalarGridSpec(
             num_scalar_prefetch=1,
-            grid=(12,),
+            grid=(8,),
             in_specs=[piece, piece, block, block, block],
             out_specs=(block,) * 3,
         ),
@@ -554,12 +545,11 @@
     pieces = exchange_colours(first)
     second = gather_step(0, [mine[2][None], mine[3][None]])
     second = gather_step(1, second)
-    kv = jnp.zeros((HEADS_CORE, 2, HDIM, HDIM), F32)
-    qkv_first, kv = project(0, both, pieces, kv)
-    second, qkv_first, kv = barrier((second, qkv_first, kv))
-    qkv_second, kv = project(1, both, exchange_colours(second), kv)
-
-    state = earlier_states(kv)
+    qkv_first = project(both, pieces)
+    second, qkv_first = barrier((second, qkv_first))
+    qkv_second = project(both, exchange_colours(second))
+
+    state = earlier_states(own_states(qkv_first, qkv_second))
     within = local_scores(qkv_first, qkv_second)
     attended, grad, qg = forward(
         core, qkv_first, qkv_second, within, state, cotangent[0], cot_other
@@ -576,15 +566,31 @@
     parts = parts_of(query_gradient(q0, q1, both))
     received, parts = barrier((received, parts))
     received = steps.send(received)
+    queries = [reduce_steps(part, order) for part, order in zip(parts, HALVING)]
+    arrived = [next(part) for part in queries]
     later = steps.send(received)
-    parts += parts_of(key_value_gradient(qkv_first, qkv_second, d0, d1, later, both))
+
+    operands = (qkv_first, qkv_second, d0, d1, later, both)
+    parts = parts_of(key_value_gradient(0, *operands))
+    parts, arrived, operands = barrier((parts, arrived, operands))
+    arrived = [part.send(x) for part, x in zip(queries, arrived)]
+    others = [reduce_steps(part, order) for part, order in zip(parts, HALVING[2:])]
+    moving = [next(part) for part in others]
+    parts = parts_of(key_value_gradient(1, *operands))
+    parts, arrived = barrier((parts, arrived))
+    arrived = [part.send(x) for part, x in zip(queries, arrived)]
+    others += [reduce_steps(part, order) for part, order in zip(parts, HALVING[4:])]
+    moving += [next(part) for part in others[2:]]
+    reduced = [part.send(x) for part, x in zip(queries, arrived)]
+    for _ in range(3):
+        moving = [part.send(x) for part, x in zip(others, moving)]
+    reduced += moving
 
     attended_other = swap(attended[BLOCK:], "c")
     low = jnp.where(core == 0, attended[:BLOCK], attended_other)
     high = jnp.where(core == 0, attended_other, attended[:BLOCK])
     attended_out = jnp.concatenate([low, high], 1)[None]
 
-    reduced = [reduce_part(part, order) for part, order in zip(parts, HALVING)]
     holds, finished = [], []
     for members, exchanged, last in GROUPS:
         holds.append(place_bit(last) == core)

time: 290 us -> 277 us (0.955)
  Pallas kernels: 80.9 us -> 75.2 us
  starting transfers between devices: 79.3 us -> 76 us
  waiting for transfers between devices: 85.9 us -> 82.9 us
    squeeze x16 -> x18, local copies, waits for them, and re-layouts: 1.95 us -> 5.04 us  [the longest x6 3.39 us: reduce_steps(): send = lax.dynamic_index_in_dim(part, 1 - keeps, axis, False)]
    pallas_call x1, Pallas kernels: 13.2 us -> 10.2 us  [adam(): pl.pallas_call(adam_kernel, name='adam', grid_spec=pltpu.PrefetchScalarGr...]
    concatenate x8, other arithmetic: 4.56 us -> 1.58 us  [gather_step(): return [jnp.concatenate([mine[h], got[h]], 0) for h in range(2)]]
  transfers between devices with their start and end apart: 61 -> 61, of which waited for: 29 -> 32; matrix products, arithmetic and copies ran while one was open for 10% -> 11% of each run, Pallas kernels for 17% -> 16%
where the time goes in v1:
time: 277 us; the launch traced here: 275 us
  waiting for transfers between devices  82.9 us (30%)
  starting transfers between devices  76 us (27%)
  Pallas kernels  75.2 us (27%)
  local copies, waits for them, and re-layouts  17.9 us (6%)
  other arithmetic  12 us (4%)
  matrix products  9.08 us (3%)
    ppermute x54, waiting for transfers between devices, swap(): return lax.ppermute(x, dim[0], PAIRS[dim[1]])  68.9 us
    ppermute x54, starting transfers between devices, swap(): return lax.ppermute(x, dim[0], PAIRS[dim[1]])  67.3 us
    pallas_call x3, Pallas kernels, gradient_call(): pl.pallas_call(kernel, grid=(1,), in_specs=specs + [VMEM], out_specs=VMEM...  22.9 us
    pallas_call x2, Pallas kernels, backward(): pl.pallas_call(backward_kernel, name='backward', grid_spec=pltpu.Prefetch...  10.8 us
    pallas_call x1, Pallas kernels, adam(): pl.pallas_call(adam_kernel, name='adam', grid_spec=pltpu.PrefetchScalarGr...  10.2 us
    all_to_all x1, waiting for transfers between devices, earlier_states(): received = lax.all_to_all(cut, ('x', 'y'), 0, 0, tiled=True)  9.99 us
    dot_general x2, matrix products, project(): return jnp.dot(tokens, weights, preferred_element_type=F32).astype(BF)  9.08 us
    pallas_call x1, Pallas kernels, arrange(): pl.pallas_call(arrange_kernel, name='arrange', grid_spec=pltpu.PrefetchSc...  7.34 us
  transfers between devices with their start and end apart: 61, of which 32 were waited for; matrix products, arithmetic and copies ran while one was open for 11% of the time, Pallas kernels for 16%

profile of v1, /device:TPU:0, one launch (start us, length us, event | category | flops | bytes accessed | tf_op | source)
XLA Modules:
  0.0 274.6 jit_solution(10677273675160740770)
XLA Ops:
  0.6 3.1 %prepare.1 = (bf16[4,256,384]{2,1,0:T(8,128)(2,1)}, bf16[4,256,384]{2,1,0:T(8,128)(2,1)}, bf16[512,512]{1,0:T(8,128)(2,1)}) custom-call(s32[1]{0:T(128)} %bitcast.core, f32[256,3072]{1,0:T(8,128)} %weights.1, f32[256,3072]{1,0:T(8,128)} %weights.1, f32[256,3072]{1,0:T(8,128)} %weights.1, f32[256,3072]{1,0:T(8,128)} %weights.1, f32[256,3072]{1,0:T(8,128)} %weights.1, ...), custom_call_target="tpu_custom_call" | custom-call | tf_op jit(solution)/shard_map/prepare/pallas_call | solution.py:121
  7.6 4.2 %collective-permute-start.3 = (bf16[1,256,384]{2,1,0:T(8,128)(2,1)S(1)}, bf16[1,256,384]{2,1,0:T(8,128)(2,1)S(1)}, u32[]{:S(2)}, u32[]{:S(2)}) collective-permute-start(bf16[1,256,384]{2,1,0:T(8,128)(2,1)S(1)} %get-tuple-element.116), channel_id=1, source_target_pairs={{2,4},{4,2},{6,0},{0,6},{3,5},{5,3},{7,1},{1,7},{10,12},{12,10},{1... | collective-permute-start | bytes 589832 | tf_op jit(solution)/shard_map/ppermute | solution.py:57
  11.8 4.1 %collective-permute-done.3 = bf16[1,256,384]{2,1,0:T(8,128)(2,1)S(1)} collective-permute-done((bf16[1,256,384]{2,1,0:T(8,128)(2,1)S(1)}, bf16[1,256,384]{2,1,0:T(8,128)(2,1)S(1)}, u32[]{:S(2)}, u32[]{:S(2)}) %collective-permute-start.3) | collective-permute-done | bytes 196640 | tf_op jit(solution)/shard_map/ppermute | solution.py:57
  19.8 6.1 %collective-permute-done.4 = bf16[2,256,384]{2,1,0:T(8,128)(2,1)S(1)} collective-permute-done((bf16[2,256,384]{2,1,0:T(8,128)(2,1)S(1)}, bf16[2,256,384]{2,1,0:T(8,128)(2,1)S(1)}, u32[]{:S(2)}, u32[]{:S(2)}) %collective-permute-start.4) | collective-permute-done | bytes 393248 | tf_op jit(solution)/shard_map/ppermute | solution.py:57
  28.9 7.3 %arrange.1.tokens = bf16[1024,2048]{1,0:T(8,128)(2,1)} custom-call(s32[8]{0:T(128)} %stack.70.blocks, bf16[512,2048]{1,0:T(8,128)(2,1)} %bitcast.10.own, bf16[512,2048]{1,0:T(8,128)(2,1)} %collective-permute-done.5.other), custom_call_target="tpu_custom_call" | custom-call | tf_op jit(solution)/shard_map/arrange/pallas_call | solution.py:142
  36.3 4.8 %collective-permute-start.10 = (bf16[2,256,384]{2,1,0:T(8,128)(2,1)S(1)}, bf16[2,256,384]{2,1,0:T(8,128)(2,1)S(1)}, u32[]{:S(2)}, u32[]{:S(2)}) collective-permute-start(bf16[2,256,384]{2,1,0:T(8,128)(2,1)S(1)} %get-tuple-element.111), channel_id=1, source_target_pairs={{0,32},{32,0},{64,96},{96,64},{1,33},{33,1},{65,97},{97,65},{2,34}... | collective-permute-start | bytes 1179656 | tf_op jit(solution)/shard_map/ppermute | solution.py:57
  43.8 2.4 collective-permute-start.12
  54.1 4.6 %collective-permute-done.13 = bf16[2,256,384]{2,1,0:T(8,128)(2,1)S(1)} collective-permute-done((bf16[2,256,384]{2,1,0:T(8,128)(2,1)S(1)}, bf16[2,256,384]{2,1,0:T(8,128)(2,1)S(1)}, u32[]{:S(2)}, u32[]{:S(2)}) %collective-permute-start.13) | collective-permute-done | bytes 393248 | tf_op jit(solution)/shard_map/ppermute | solution.py:57
  58.8 4.5 %fusion.11.first.k0.v0.qkv = bf16[1024,768]{1,0:T(8,128)(2,1)} fusion(bf16[1024,2048]{1,0:T(8,128)(2,1)S(1)} %copy-done, bf16[2048,384]{1,0:T(8,128)(2,1)S(1)} %fusion.47, bf16[2048,384]{1,0:T(8,128)(2,1)S(1)} %fusion.51), kind=kOutput, calls=%fused_computation.9 | convolution fusion | flops 3228303360 | bytes 8912896 | tf_op jit(solution)/shard_map/dot_general | solution.py:186
  64.4 2.7 collective-permute-start.15
  76.6 4.5 %fusion.8.second.k1.v1.qkv = bf16[1024,768]{1,0:T(8,128)(2,1)} fusion(bf16[1024,2048]{1,0:T(8,128)(2,1)S(1)} %copy-done, bf16[2048,384]{1,0:T(8,128)(2,1)S(1)} %fusion.39, bf16[2048,384]{1,0:T(8,128)(2,1)S(1)} %fusion.43), kind=kOutput, calls=%fused_computation.8 | convolution fusion | flops 3228303360 | bytes 8912896 | tf_op jit(solution)/shard_map/dot_general | solution.py:186
  81.1 2.7 outer.1
  83.8 4.4 %all-to-all-start = ((f32[16,64,128]{2,1,0:T(8,128)}), f32[16,64,128]{2,1,0:T(8,128)S(1)}, u32[]{:S(2)}, u32[]{:S(2)}) async-start(f32[16,64,128]{2,1,0:T(8,128)} %bitcast.266), calls=%async_computation | async-start | bytes 1048576 | tf_op jit(solution)/shard_map/all_to_all | solution.py:215
  88.3 10.0 %all-to-all-done.received = f32[16,64,128]{2,1,0:T(8,128)S(1)} async-done(((f32[16,64,128]{2,1,0:T(8,128)}), f32[16,64,128]{2,1,0:T(8,128)S(1)}, u32[]{:S(2)}, u32[]{:S(2)}) %all-to-all-start) | async-done | bytes 524320 | tf_op jit(solution)/shard_map/all_to_all | solution.py:215
  100.8 3.7 %all-to-all-start.1 = ((bf16[16,64,128]{2,1,0:T(8,128)(2,1)}), bf16[16,64,128]{2,1,0:T(8,128)(2,1)S(1)}, u32[]{:S(2)}, u32[]{:S(2)}) async-start(bf16[16,64,128]{2,1,0:T(8,128)(2,1)} %running.1), calls=%async_computation.1 | async-start | bytes 524288 | tf_op jit(solution)/shard_map/all_to_all | solution.py:223
  104.6 6.5 %within.1 = f32[1024,512]{1,0:T(8,128)} custom-call(bf16[1024,768]{1,0:T(8,128)(2,1)} %fusion.11.first.k0.v0.qkv, bf16[1024,768]{1,0:T(8,128)(2,1)} %fusion.8.second.k1.v1.qkv), custom_call_target="tpu_custom_call" | custom-call | tf_op jit(solution)/shard_map/within/pallas_call | solution.py:267
  113.5 6.9 %forward.1 = (bf16[1024,512]{1,0:T(8,128)(2,1)}, bf16[1024,512]{1,0:T(8,128)(2,1)}, bf16[4,2,128,128]{3,2,1,0:T(8,128)(2,1)}) custom-call(s32[1]{0:T(128)} %bitcast.core, bf16[1024,768]{1,0:T(8,128)(2,1)} %fusion.11.first.k0.v0.qkv, bf16[1024,768]{1,0:T(8,128)(2,1)} %fusion.8.second.k1.v1.qkv, f32[1024,512]{1,0:T(8,128)} %within.1, ...), custom_call_target="tpu_custom_call" | custom-call | tf_op jit(solution)/shard_map/forward/pallas_call | solution.py:299
  120.9 5.4 %backward.2 = (bf16[1024,256]{1,0:T(8,128)(2,1)}, f32[2,1024,256]{2,1,0:T(8,128)}) custom-call(s32[1]{0:T(128)} %constant.54.clone.1.pair, bf16[1024,768]{1,0:T(8,128)(2,1)} %fusion.11.first.k0.v0.qkv, bf16[1024,512]{1,0:T(8,128)(2,1)} %get-tuple-element.68.grad, bf16[4,2,128,128]{3,2,1,0:T(8,128)(2,1)} %bitcast.250), custom_call_target="tpu_custom_call" | custom-call | tf_op jit(solution)/shard_map/backward/pallas_call | solution.py:335
  128.5 5.4 %backward.3 = (bf16[1024,256]{1,0:T(8,128)(2,1)}, f32[2,1024,256]{2,1,0:T(8,128)}) custom-call(s32[1]{0:T(128)} %constant.55.clone.1.pair, bf16[1024,768]{1,0:T(8,128)(2,1)} %fusion.8.second.k1.v1.qkv, bf16[1024,512]{1,0:T(8,128)(2,1)} %get-tuple-element.68.grad, bf16[4,2,128,128]{3,2,1,0:T(8,128)(2,1)} %bitcast.251), custom_call_target="tpu_custom_call" | custom-call | tf_op jit(solution)/shard_map/backward/pallas_call | solution.py:335
  135.6 7.1 %shard_map.84 = bf16[2,8,256,256]{3,2,1,0:T(8,128)(2,1)} custom-call(bf16[1024,256]{1,0:T(8,128)(2,1)} %get-tuple-element.72.q0, bf16[1024,256]{1,0:T(8,128)(2,1)} %get-tuple-element.73.q1, bf16[1024,2048]{1,0:T(8,128)(2,1)} %arrange.1.tokens), custom_call_target="tpu_custom_call" | custom-call | tf_op jit(solution)/shard_map/pallas_call | solution.py:388
  153.1 7.9 %shard_map.85 = bf16[2,8,256,256]{3,2,1,0:T(8,128)(2,1)} custom-call(bf16[1024,768]{1,0:T(8,128)(2,1)} %fusion.11.first.k0.v0.qkv, bf16[1024,768]{1,0:T(8,128)(2,1)} %fusion.8.second.k1.v1.qkv, f32[2,1024,256]{2,1,0:T(8,128)} %get-tuple-element.82.d_first, f32[2,1024,256]{2,1,0:T(8,128)} %get-tuple-element.83.d_second, ...), custom_call_target="tpu_custom_call" | custom-call | tf_op jit(solution)/shard_map/pallas_call | solution.py:388
  173.5 7.9 %shard_map.86 = bf16[2,8,256,256]{3,2,1,0:T(8,128)(2,1)} custom-call(bf16[1024,768]{1,0:T(8,128)(2,1)} %fusion.11.first.k0.v0.qkv, bf16[1024,768]{1,0:T(8,128)(2,1)} %fusion.8.second.k1.v1.qkv, f32[2,1024,256]{2,1,0:T(8,128)} %get-tuple-element.82.d_first, f32[2,1024,256]{2,1,0:T(8,128)} %get-tuple-element.83.d_second, ...), custom_call_target="tpu_custom_call" | custom-call | tf_op jit(solution)/shard_map/pallas_call | solution.py:388
  188.8 2.8 %collective-permute-done.36 = bf16[256,256]{1,0:T(8,128)(2,1)S(1)} collective-permute-done((bf16[256,256]{1,0:T(8,128)(2,1)S(1)}, bf16[256,256]{1,0:T(8,128)(2,1)S(1)}, u32[]{:S(2)}, u32[]{:S(2)}) %collective-permute-start.36) | collective-permute-done | bytes 131104 | tf_op jit(solution)/shard_map/ppermute | solution.py:57
  193.8 4.0 %collective-permute-done.28 = bf16[256,256]{1,0:T(8,128)(2,1)S(1)} collective-permute-done((bf16[256,256]{1,0:T(8,128)(2,1)S(1)}, bf16[256,256]{1,0:T(8,128)(2,1)S(1)}, u32[]{:S(2)}, u32[]{:S(2)}) %collective-permute-start.28) | collective-permute-done | bytes 131104 | tf_op jit(solution)/shard_map/ppermute | solution.py:57
  203.2 6.5 %collective-permute-done.44 = bf16[2,2,256,256]{3,2,1,0:T(8,128)(2,1)S(1)} collective-permute-done((bf16[2,2,256,256]{3,2,1,0:T(8,128)(2,1)S(1)}, bf16[2,2,256,256]{3,2,1,0:T(8,128)(2,1)S(1)}, u32[]{:S(2)}, u32[]{:S(2)}) %collective-permute-start.44) | collective-permute-done | bytes 524320 | tf_op jit(solution)/shard_map/ppermute | solution.py:57
  214.4 3.3 %collective-permute-done.39 = bf16[256,256]{1,0:T(8,128)(2,1)S(1)} collective-permute-done((bf16[256,256]{1,0:T(8,128)(2,1)S(1)}, bf16[256,256]{1,0:T(8,128)(2,1)S(1)}, u32[]{:S(2)}, u32[]{:S(2)}) %collective-permute-start.39) | collective-permute-done | bytes 131104 | tf_op jit(solution)/shard_map/ppermute | solution.py:57
  229.8 2.7 collective-permute-start.33
  233.6 5.4 %collective-permute-done.55 = bf16[1,256,256]{2,1,0:T(8,128)(2,1)S(1)} collective-permute-done((bf16[1,256,256]{2,1,0:T(8,128)(2,1)S(1)}, bf16[1,256,256]{2,1,0:T(8,128)(2,1)S(1)}, u32[]{:S(2)}, u32[]{:S(2)}) %collective-permute-start.55) | collective-permute-done | bytes 131104 | tf_op jit(solution)/shard_map/ppermute | solution.py:57
  241.8 4.3 %collective-permute-done.56 = bf16[1,256,256]{2,1,0:T(8,128)(2,1)S(1)} collective-permute-done((bf16[1,256,256]{2,1,0:T(8,128)(2,1)S(1)}, bf16[1,256,256]{2,1,0:T(8,128)(2,1)S(1)}, u32[]{:S(2)}, u32[]{:S(2)}) %collective-permute-start.56) | collective-permute-done | bytes 131104 | tf_op jit(solution)/shard_map/ppermute | solution.py:57
  252.7 3.9 %collective-permute-done.50.refs_5_ = bf16[1,256,256]{2,1,0:T(8,128)(2,1)S(1)} collective-permute-done((bf16[1,256,256]{2,1,0:T(8,128)(2,1)S(1)}, bf16[1,256,256]{2,1,0:T(8,128)(2,1)S(1)}, u32[]{:S(2)}, u32[]{:S(2)}) %collective-permute-start.50) | collective-permute-done | bytes 131104 | tf_op jit(solution)/shard_map/ppermute | solution.py:57
  258.1 3.0 %sort_pieces.1 = (bf16[256,1536]{1,0:T(8,128)(2,1)}, bf16[256,1536]{1,0:T(8,128)(2,1)}) custom-call(s32[4]{0:T(128)} %add_convert_fusion.12.holds, bf16[2,256,256]{2,1,0:T(8,128)(2,1)} %copy-done.10, bf16[2,256,256]{2,1,0:T(8,128)(2,1)} %copy-done.16, bf16[2,256,256]{2,1,0:T(8,128)(2,1)} %copy-done.9, bf16[2,256,256]{2,1,0:T(8,128)(2,1)} %copy-done.15, ...), custom_call_target="tpu_custom_call" | custom-call | tf_op jit(solution)/shard_map/sort_pieces/pallas_call | solution.py:472
  264.4 10.2 %adam.1 = (f32[256,3072]{1,0:T(8,128)}, f32[256,3072]{1,0:T(8,128)}, f32[256,3072]{1,0:T(8,128)}) custom-call(s32[1]{0:T(128)} %bitcast.core, bf16[256,1536]{1,0:T(8,128)(2,1)} %get-tuple-element.93.kept, bf16[256,1536]{1,0:T(8,128)(2,1)} %copy-done.11, f32[256,3072]{1,0:T(8,128)} %weights.1, f32[256,3072]{1,0:T(8,128)} %first.1, f32[256,3072]{1,0:T(8,128)} %second.1), custom_call_target="tpu_custom_call" | custom-call | tf_op jit(solution)/shard_map/adam/pallas_call | solution.py:500
  (253 shorter events, 110.8 us)
Async XLA Ops:
  3.8 25.1 %collective-permute-start.5 = (bf16[512,2048]{1,0:T(8,128)(2,1)}, bf16[512,2048]{1,0:T(8,128)(2,1)}, u32[]{:S(2)}, u32[]{:S(2)}) collective-permute-start(bf16[512,2048]{1,0:T(8,128)(2,1)} %bitcast.10.own), channel_id=1, source_target_pairs={{0,1},{1,0},{2,3},{3,2},{4,5},{5,4},{6,7},{7,6},{8,9},{9,8},{10,11... | collective-permute-start | bytes 6291464 | tf_op jit(solution)/shard_map/ppermute | solution.py:56
  15.9 10.0 %collective-permute-start.4 = (bf16[2,256,384]{2,1,0:T(8,128)(2,1)S(1)}, bf16[2,256,384]{2,1,0:T(8,128)(2,1)S(1)}, u32[]{:S(2)}, u32[]{:S(2)}) collective-permute-start(bf16[2,256,384]{2,1,0:T(8,128)(2,1)S(1)} %pad_maximum_fusion.5), channel_id=1, source_target_pairs={{0,2},{2,0},{4,6},{6,4},{1,3},{3,1},{5,7},{7,5},{8,10},{10,8},{12,... | collective-permute-start | bytes 1179656 | tf_op jit(solution)/shard_map/ppermute | solution.py:57
  17.9 9.8 %collective-permute-start.2 = (bf16[2,256,384]{2,1,0:T(8,128)(2,1)S(1)}, bf16[2,256,384]{2,1,0:T(8,128)(2,1)}, u32[]{:S(2)}, u32[]{:S(2)}) collective-permute-start(bf16[2,256,384]{2,1,0:T(8,128)(2,1)S(1)} %pad_maximum_fusion.4), channel_id=1, source_target_pairs={{2,4},{4,2},{6,0},{0,6},{3,5},{5,3},{7,1},{1,7},{10,12},{12,10},{1... | collective-permute-start | bytes 1179656 | tf_op jit(solution)/shard_map/ppermute | solution.py:57
  36.3 14.0 %collective-permute-start.10 = (bf16[2,256,384]{2,1,0:T(8,128)(2,1)S(1)}, bf16[2,256,384]{2,1,0:T(8,128)(2,1)S(1)}, u32[]{:S(2)}, u32[]{:S(2)}) collective-permute-start(bf16[2,256,384]{2,1,0:T(8,128)(2,1)S(1)} %get-tuple-element.111), channel_id=1, source_target_pairs={{0,32},{32,0},{64,96},{96,64},{1,33},{33,1},{65,97},{97,65},{2,34}... | collective-permute-start | bytes 1179656 | tf_op jit(solution)/shard_map/ppermute | solution.py:57
  42.5 11.0 %collective-permute-start.11 = (bf16[2,256,384]{2,1,0:T(8,128)(2,1)S(1)}, bf16[2,256,384]{2,1,0:T(8,128)(2,1)S(1)}, u32[]{:S(2)}, u32[]{:S(2)}) collective-permute-start(bf16[2,256,384]{2,1,0:T(8,128)(2,1)S(1)} %get-tuple-element.110), channel_id=1, source_target_pairs={{32,64},{64,32},{96,0},{0,96},{33,65},{65,33},{97,1},{1,97},{34,66... | collective-permute-start | bytes 1179656 | tf_op jit(solution)/shard_map/ppermute | solution.py:57
  43.8 10.1 %collective-permute-start.12 = (bf16[2,256,384]{2,1,0:T(8,128)(2,1)S(1)}, bf16[2,256,384]{2,1,0:T(8,128)(2,1)S(1)}, u32[]{:S(2)}, u32[]{:S(2)}) collective-permute-start(bf16[2,256,384]{2,1,0:T(8,128)(2,1)S(1)} %get-tuple-element.113), channel_id=1, source_target_pairs={{0,8},{8,0},{16,24},{24,16},{1,9},{9,1},{17,25},{25,17},{2,10},{10... | collective-permute-start | bytes 1179656 | tf_op jit(solution)/shard_map/ppermute | solution.py:57
  48.3 10.4 %collective-permute-start.13 = (bf16[2,256,384]{2,1,0:T(8,128)(2,1)S(1)}, bf16[2,256,384]{2,1,0:T(8,128)(2,1)S(1)}, u32[]{:S(2)}, u32[]{:S(2)}) collective-permute-start(bf16[2,256,384]{2,1,0:T(8,128)(2,1)S(1)} %get-tuple-element.112), channel_id=1, source_target_pairs={{8,16},{16,8},{24,0},{0,24},{9,17},{17,9},{25,1},{1,25},{10,18},{1... | collective-permute-start | bytes 1179656 | tf_op jit(solution)/shard_map/ppermute | solution.py:57
  50.2 13.2 %collective-permute-start.9 = (bf16[2,256,384]{2,1,0:T(8,128)(2,1)S(1)}, bf16[2,256,384]{2,1,0:T(8,128)(2,1)S(1)}, u32[]{:S(2)}, u32[]{:S(2)}) collective-permute-start(bf16[2,256,384]{2,1,0:T(8,128)(2,1)S(1)} %pad_maximum_fusion.7), channel_id=1, source_target_pairs={{0,2},{2,0},{4,6},{6,4},{1,3},{3,1},{5,7},{7,5},{8,10},{10,8},{12,... | collective-permute-start | bytes 1179656 | tf_op jit(solution)/shard_map/ppermute | solution.py:57
  50.4 13.1 %collective-permute-start.7 = (bf16[2,256,384]{2,1,0:T(8,128)(2,1)S(1)}, bf16[2,256,384]{2,1,0:T(8,128)(2,1)S(1)}, u32[]{:S(2)}, u32[]{:S(2)}) collective-permute-start(bf16[2,256,384]{2,1,0:T(8,128)(2,1)S(1)} %pad_maximum_fusion.6), channel_id=1, source_target_pairs={{2,4},{4,2},{6,0},{0,6},{3,5},{5,3},{7,1},{1,7},{10,12},{12,10},{1... | collective-permute-start | bytes 1179656 | tf_op jit(solution)/shard_map/ppermute | solution.py:57
  64.4 9.5 %collective-permute-start.15 = (bf16[2,256,384]{2,1,0:T(8,128)(2,1)S(1)}, bf16[2,256,384]{2,1,0:T(8,128)(2,1)S(1)}, u32[]{:S(2)}, u32[]{:S(2)}) collective-permute-start(bf16[2,256,384]{2,1,0:T(8,128)(2,1)S(1)} %get-tuple-element.106), channel_id=1, source_target_pairs={{32,64},{64,32},{96,0},{0,96},{33,65},{65,33},{97,1},{1,97},{34,66... | collective-permute-start | bytes 1179656 | tf_op jit(solution)/shard_map/ppermute | solution.py:57
  83.8 14.5 %all-to-all-start = ((f32[16,64,128]{2,1,0:T(8,128)}), f32[16,64,128]{2,1,0:T(8,128)S(1)}, u32[]{:S(2)}, u32[]{:S(2)}) async-start(f32[16,64,128]{2,1,0:T(8,128)} %bitcast.266), calls=%async_computation | async-start | bytes 1048576 | tf_op jit(solution)/shard_map/all_to_all | solution.py:215
  88.2 22.9 %collective-permute-start.18 = (bf16[512,512]{1,0:T(8,128)(2,1)S(1)}, bf16[512,512]{1,0:T(8,128)(2,1)S(1)}, u32[]{:S(2)}, u32[]{:S(2)}) collective-permute-start(bf16[512,512]{1,0:T(8,128)(2,1)S(1)} %copy-done.19), channel_id=1, source_target_pairs={{0,1},{1,0},{2,3},{3,2},{4,5},{5,4},{6,7},{7,6},{8,9},{9,8},{10,11... | collective-permute-start | bytes 1572872 | tf_op jit(solution)/shard_map/ppermute | solution.py:56
  100.8 12.0 %all-to-all-start.1 = ((bf16[16,64,128]{2,1,0:T(8,128)(2,1)}), bf16[16,64,128]{2,1,0:T(8,128)(2,1)S(1)}, u32[]{:S(2)}, u32[]{:S(2)}) async-start(bf16[16,64,128]{2,1,0:T(8,128)(2,1)} %running.1), calls=%async_computation.1 | async-start | bytes 524288 | tf_op jit(solution)/shard_map/all_to_all | solution.py:223
  134.9 9.4 %collective-permute-start.22 = (bf16[4,2,128,128]{3,2,1,0:T(8,128)(2,1)S(1)}, bf16[4,2,128,128]{3,2,1,0:T(8,128)(2,1)S(1)}, u32[]{:S(2)}, u32[]{:S(2)}) collective-permute-start(bf16[4,2,128,128]{3,2,1,0:T(8,128)(2,1)S(1)} %fusion.32), channel_id=1, source_target_pairs={{0,32},{32,0},{64,96},{96,64},{1,33},{33,1},{65,97},{97,65},{2,34}... | collective-permute-start | bytes 786440 | tf_op jit(solution)/shard_map/ppermute | solution.py:57
  148.5 112.5 %collective-permute-start.19 = (bf16[512,512]{1,0:T(8,128)(2,1)}, bf16[512,512]{1,0:T(8,128)(2,1)}, u32[]{:S(2)}, u32[]{:S(2)}) collective-permute-start(bf16[512,512]{1,0:T(8,128)(2,1)} %slice.274), channel_id=1, source_target_pairs={{0,1},{1,0},{2,3},{3,2},{4,5},{5,4},{6,7},{7,6},{8,9},{9,8},{10,11... | collective-permute-start | bytes 1572872 | tf_op jit(solution)/shard_map/ppermute | solution.py:56
  149.4 14.7 %collective-permute-start.24 = (bf16[2,2,256,256]{3,2,1,0:T(8,128)(2,1)}, bf16[2,2,256,256]{3,2,1,0:T(8,128)(2,1)}, u32[]{:S(2)}, u32[]{:S(2)}) collective-permute-start(bf16[2,2,256,256]{3,2,1,0:T(8,128)(2,1)} %dynamic-slice_bitcast_fusion.2), channel_id=1, source_target_pairs={{0,32},{32,0},{64,96},{96,64},{1,33},{33,1},{65,97},{97,65},{2,34}... | collective-permute-start | bytes 1572872 | tf_op jit(solution)/shard_map/ppermute | solution.py:57
  150.8 14.4 %collective-permute-start.25 = (bf16[2,2,256,256]{3,2,0,1:T(8,128)(2,1)}, bf16[2,2,256,256]{3,2,0,1:T(8,128)(2,1)}, u32[]{:S(2)}, u32[]{:S(2)}) collective-permute-start(bf16[2,2,256,256]{3,2,0,1:T(8,128)(2,1)} %copy_bitcast_fusion.2), channel_id=1, source_target_pairs={{0,8},{8,0},{16,24},{24,16},{1,9},{9,1},{17,25},{25,17},{2,10},{10... | collective-permute-start | bytes 1572872 | tf_op jit(solution)/shard_map/ppermute | solution.py:57
  167.1 16.1 %collective-permute-start.27 = (bf16[2,256,256]{2,1,0:T(8,128)(2,1)}, bf16[2,256,256]{2,1,0:T(8,128)(2,1)}, u32[]{:S(2)}, u32[]{:S(2)}) collective-permute-start(bf16[2,256,256]{2,1,0:T(8,128)(2,1)} %slice_bitcast_fusion.9), channel_id=1, source_target_pairs={{2,4},{4,2},{6,0},{0,6},{3,5},{5,3},{7,1},{1,7},{10,12},{12,10},{1... | collective-permute-start | bytes 786440 | tf_op jit(solution)/shard_map/ppermute | solution.py:57
  170.1 13.1 %collective-permute-start.26 = (bf16[2,256,256]{2,1,0:T(8,128)(2,1)}, bf16[2,256,256]{2,1,0:T(8,128)(2,1)S(1)}, u32[]{:S(2)}, u32[]{:S(2)}) collective-permute-start(bf16[2,256,256]{2,1,0:T(8,128)(2,1)} %slice_bitcast_fusion.10), channel_id=1, source_target_pairs={{0,2},{2,0},{4,6},{6,4},{1,3},{3,1},{5,7},{7,5},{8,10},{10,8},{12,... | collective-permute-start | bytes 786440 | tf_op jit(solution)/shard_map/ppermute | solution.py:57
  170.9 28.0 %collective-permute-start.37 = (bf16[2,2,256,256]{3,2,0,1:T(8,128)(2,1)}, bf16[2,2,256,256]{3,2,0,1:T(8,128)(2,1)S(1)}, u32[]{:S(2)}, u32[]{:S(2)}) collective-permute-start(bf16[2,2,256,256]{3,2,0,1:T(8,128)(2,1)} %copy_bitcast_fusion.1), channel_id=1, source_target_pairs={{0,8},{8,0},{16,24},{24,16},{1,9},{9,1},{17,25},{25,17},{2,10},{10... | collective-permute-start | bytes 1572872 | tf_op jit(solution)/shard_map/ppermute | solution.py:57
  172.0 29.3 %collective-permute-start.29 = (bf16[2,2,256,256]{3,2,1,0:T(8,128)(2,1)}, bf16[2,2,256,256]{3,2,1,0:T(8,128)(2,1)S(1)}, u32[]{:S(2)}, u32[]{:S(2)}) collective-permute-start(bf16[2,2,256,256]{3,2,1,0:T(8,128)(2,1)} %dynamic-slice_bitcast_fusion.1), channel_id=1, source_target_pairs={{0,32},{32,0},{64,96},{96,64},{1,33},{33,1},{65,97},{97,65},{2,34}... | collective-permute-start | bytes 1572872 | tf_op jit(solution)/shard_map/ppermute | solution.py:57
  183.2 18.6 %collective-permute-start.51 = (bf16[2,2,256,256]{3,2,0,1:T(8,128)(2,1)S(1)}, bf16[2,2,256,256]{3,2,0,1:T(8,128)(2,1)S(1)}, u32[]{:S(2)}, u32[]{:S(2)}) collective-permute-start(bf16[2,2,256,256]{3,2,0,1:T(8,128)(2,1)S(1)} %copy_bitcast_fusion), channel_id=1, source_target_pairs={{8,16},{16,8},{24,0},{0,24},{9,17},{17,9},{25,1},{1,25},{10,18},{1... | collective-permute-start | bytes 1572872 | tf_op jit(solution)/shard_map/ppermute | solution.py:57
  197.8 11.9 %collective-permute-start.44 = (bf16[2,2,256,256]{3,2,1,0:T(8,128)(2,1)S(1)}, bf16[2,2,256,256]{3,2,1,0:T(8,128)(2,1)S(1)}, u32[]{:S(2)}, u32[]{:S(2)}) collective-permute-start(bf16[2,2,256,256]{3,2,1,0:T(8,128)(2,1)S(1)} %dynamic-slice_bitcast_fusion), channel_id=1, source_target_pairs={{32,64},{64,32},{96,0},{0,96},{33,65},{65,33},{97,1},{1,97},{34,66... | collective-permute-start | bytes 1572872 | tf_op jit(solution)/shard_map/ppermute | solution.py:57
  199.1 11.3 %collective-permute-start.38 = (bf16[2,256,256]{2,1,0:T(8,128)(2,1)S(1)}, bf16[2,256,256]{2,1,0:T(8,128)(2,1)S(1)}, u32[]{:S(2)}, u32[]{:S(2)}) collective-permute-start(bf16[2,256,256]{2,1,0:T(8,128)(2,1)S(1)} %slice_bitcast_fusion.4), channel_id=1, source_target_pairs={{2,4},{4,2},{6,0},{0,6},{3,5},{5,3},{7,1},{1,7},{10,12},{12,10},{1... | collective-permute-start | bytes 786440 | tf_op jit(solution)/shard_map/ppermute | solution.py:57
  201.5 10.6 %collective-permute-start.30 = (bf16[2,256,256]{2,1,0:T(8,128)(2,1)S(1)}, bf16[2,256,256]{2,1,0:T(8,128)(2,1)S(1)}, u32[]{:S(2)}, u32[]{:S(2)}) collective-permute-start(bf16[2,256,256]{2,1,0:T(8,128)(2,1)S(1)} %slice_bitcast_fusion.7), channel_id=1, source_target_pairs={{0,2},{2,0},{4,6},{6,4},{1,3},{3,1},{5,7},{7,5},{8,10},{10,8},{12,... | collective-permute-start | bytes 786440 | tf_op jit(solution)/shard_map/ppermute | solution.py:57
  202.0 17.9 %collective-permute-start.52 = (bf16[2,256,256]{2,1,0:T(8,128)(2,1)S(1)}, bf16[2,256,256]{2,1,0:T(8,128)(2,1)S(1)}, u32[]{:S(2)}, u32[]{:S(2)}) collective-permute-start(bf16[2,256,256]{2,1,0:T(8,128)(2,1)S(1)} %slice_bitcast_fusion), channel_id=1, source_target_pairs={{2,4},{4,2},{6,0},{0,6},{3,5},{5,3},{7,1},{1,7},{10,12},{12,10},{1... | collective-permute-start | bytes 786440 | tf_op jit(solution)/shard_map/ppermute | solution.py:57
  209.8 10.6 %collective-permute-start.45 = (bf16[2,256,256]{2,1,0:T(8,128)(2,1)S(1)}, bf16[2,256,256]{2,1,0:T(8,128)(2,1)S(1)}, u32[]{:S(2)}, u32[]{:S(2)}) collective-permute-start(bf16[2,256,256]{2,1,0:T(8,128)(2,1)S(1)} %slice_bitcast_fusion.2), channel_id=1, source_target_pairs={{0,2},{2,0},{4,6},{6,4},{1,3},{3,1},{5,7},{7,5},{8,10},{10,8},{12,... | collective-permute-start | bytes 786440 | tf_op jit(solution)/shard_map/ppermute | solution.py:57
  217.7 10.0 %collective-permute-start.40 = (bf16[2,256,256]{2,1,0:T(8,128)(2,1)S(1)}, bf16[2,256,256]{2,1,0:T(8,128)(2,1)S(1)}, u32[]{:S(2)}, u32[]{:S(2)}) collective-permute-start(bf16[2,256,256]{2,1,0:T(8,128)(2,1)S(1)} %pad_maximum_fusion.9), channel_id=1, source_target_pairs={{8,16},{16,8},{24,0},{0,24},{9,17},{17,9},{25,1},{1,25},{10,18},{1... | collective-permute-start | bytes 786440 | tf_op jit(solution)/shard_map/ppermute | solution.py:57
  218.5 11.2 %collective-permute-start.32 = (bf16[2,256,256]{2,1,0:T(8,128)(2,1)S(1)}, bf16[2,256,256]{2,1,0:T(8,128)(2,1)S(1)}, u32[]{:S(2)}, u32[]{:S(2)}) collective-permute-start(bf16[2,256,256]{2,1,0:T(8,128)(2,1)S(1)} %pad_maximum_fusion.8), channel_id=1, source_target_pairs={{32,64},{64,32},{96,0},{0,96},{33,65},{65,33},{97,1},{1,97},{34,66... | collective-permute-start | bytes 786440 | tf_op jit(solution)/shard_map/ppermute | solution.py:57
  227.8 13.6 %collective-permute-start.41 = (bf16[2,256,256]{2,1,0:T(8,128)(2,1)S(1)}, bf16[2,256,256]{2,1,0:T(8,128)(2,1)S(1)}, u32[]{:S(2)}, u32[]{:S(2)}) collective-permute-start(bf16[2,256,256]{2,1,0:T(8,128)(2,1)S(1)} %add_convert_fusion.2), channel_id=1, source_target_pairs={{32,64},{64,32},{96,0},{0,96},{33,65},{65,33},{97,1},{1,97},{34,66... | collective-permute-start | bytes 786440 | tf_op jit(solution)/shard_map/ppermute | solution.py:57
  229.8 11.8 %collective-permute-start.33 = (bf16[2,256,256]{2,1,0:T(8,128)(2,1)S(1)}, bf16[2,256,256]{2,1,0:T(8,128)(2,1)S(1)}, u32[]{:S(2)}, u32[]{:S(2)}) collective-permute-start(bf16[2,256,256]{2,1,0:T(8,128)(2,1)S(1)} %add_convert_fusion.5), channel_id=1, source_target_pairs={{8,16},{16,8},{24,0},{0,24},{9,17},{17,9},{25,1},{1,25},{10,18},{1... | collective-permute-start | bytes 786440 | tf_op jit(solution)/shard_map/ppermute | solution.py:57
  239.8 10.5 %collective-permute-start.49 = (bf16[1,256,256]{2,1,0:T(8,128)(2,1)S(1)}, bf16[1,256,256]{2,1,0:T(8,128)(2,1)S(1)}, u32[]{:S(2)}, u32[]{:S(2)}) collective-permute-start(bf16[1,256,256]{2,1,0:T(8,128)(2,1)S(1)} %add_convert_fusion.10), channel_id=1, source_target_pairs={{8,16},{16,8},{24,0},{0,24},{9,17},{17,9},{25,1},{1,25},{10,18},{1... | collective-permute-start | bytes 393224 | tf_op jit(solution)/shard_map/ppermute | solution.py:57
  (49 other events, 298.5 us)

commit v2 on v1

--- a/solution.py
+++ b/solution.py
@@ -1,5 +1,3 @@
-import functools
-
 import jax
 import jax.numpy as jnp
 from jax import lax
@@ -352,64 +350,66 @@
     )(jnp.full((1,), pair, jnp.int32), qkv, grad, state)
 
 
-def multiply_blocks(turned, tokens, out):
+def multiply_blocks(keeps, turned, tokens, outs):
     def blocks(i, carry):
         at = pl.ds(pl.multiple_of(i * 512, 512), 512)
         piece = dot(turned[...], tokens[:, at], 1, 0).astype(BF)
-        for half in range(2):
-            for j in range(2):
-                out[half, 2 * i + j] = piece[half * 256 : (half + 1) * 256, j * 256 : (j + 1) * 256]
+        for part in range(2):
+            sent, kept = outs[2 * part], outs[2 * part + 1]
+            first = piece[part * 256 : (part + 1) * 256, :256]
+            second = piece[part * 256 : (part + 1) * 256, 256:]
+            kept[i] = jnp.where(keeps[part] == 0, first, second)
+            sent[i] = jnp.where(keeps[part] == 0, second, first)
         return carry
 
     lax.fori_loop(0, tokens.shape[1] // 512, blocks, 0)
 
 
-def query_gradient_kernel(q0, q1, tokens, out, turned):
+def query_gradient_kernel(keeps, q0, q1, tokens, s0, k0, s1, k1, turned):
     turned[:256, :] = q0[...].T
     turned[256:, :] = q1[...].T
-    multiply_blocks(turned, tokens, out)
-
-
-def gradient_kernel(kind, first, second, d_first, d_second, state, tokens, out, turned):
-    for pair, (rows, within) in enumerate(((first, d_first), (second, d_second))):
-        for h in range(2):
-            head = 2 * pair + h
-            for s in range(2):
-                span = slice(s * BLOCK, (s + 1) * BLOCK)
-                later = dot(rows[span, cols(h)], state[head, s], 1, 1 - kind)
-                total = within[0, span, cols(h)] + later
-                turned[cols(head), span] = total.astype(BF).T
-
-    multiply_blocks(turned, tokens, out)
-
-
-def gradient_call(kernel, ins, specs, tokens):
-    blocks = tokens.shape[1] // 256
+    multiply_blocks(keeps, turned, tokens, (s0, k0, s1, k1))
+
+
+def gradient_kernel(keeps, first, second, d_first, d_second, state, tokens, *refs):
+    turned = refs[-1]
+    for kind in range(2):
+        sides = ((first, d_first), (second, d_second))
+        for pair, (qkv, within) in enumerate(sides):
+
+            @each_head
+            def _(h):
+                head = 2 * pair + h
+                at = head_cols(h)
+                for s in range(2):
+                    span = slice(s * BLOCK, (s + 1) * BLOCK)
+                    source = qkv[span, head_cols(4 - 2 * kind + h)]
+                    later = dot(source, state[head, s], 1, 1 - kind)
+                    total = within[kind, span, at] + later
+                    turned[head_cols(head), span] = total.astype(BF).T
+
+        multiply_blocks(keeps.at[pl.ds(2 * kind, 2)], turned, tokens, refs[4 * kind : 4 * kind + 4])
+
+
+def gradient_call(kernel, first, ins, specs, tokens):
+    count = len(first)
+    keeps = jnp.stack([colour() ^ place_bit(HALVING[p][0]) for p in first]).astype(jnp.int32)
     return pl.pallas_call(
         kernel,
-        grid=(1,),
-        in_specs=specs + [VMEM],
-        out_specs=VMEM,
-        out_shape=shape((2, blocks, 256, 256), BF),
+        in_specs=[pl.BlockSpec(memory_space=pltpu.SMEM)] + specs + [VMEM],
+        out_specs=(VMEM,) * (2 * count),
+        out_shape=(shape((4, 256, 256), BF),) * (2 * count),
         scratch_shapes=[pltpu.VMEM((WIDTH, ROWS), BF)],
-    )(*ins, tokens)
+    )(keeps, *ins, tokens)
 
 
 def query_gradient(q0, q1, tokens):
-    return gradient_call(query_gradient_kernel, (q0, q1), [VMEM] * 2, tokens)
-
-
-def key_value_gradient(kind, first, second, d_first, d_second, state, tokens):
-    rows = pl.BlockSpec((ROWS, 256), lambda _: (0, 2 - kind))
-    within = pl.BlockSpec((1, ROWS, 256), lambda _: (kind, 0, 0))
-    specs = [rows, rows, within, within, VMEM]
+    return gradient_call(query_gradient_kernel, (0, 1), (q0, q1), [VMEM] * 2, tokens)
+
+
+def key_value_gradient(first, second, d_first, d_second, state, tokens):
     ins = (first, second, d_first, d_second, state)
-    kernel = functools.partial(gradient_kernel, kind)
-    return gradient_call(kernel, ins, specs, tokens)
-
-
-def parts_of(partial):
-    return [partial[i].reshape(2, 2, 2, 256, 256) for i in range(2)]
+    return gradient_call(gradient_kernel, (2, 3, 4, 5), ins, [VMEM] * 5, tokens)
 
 
 def wide(x):
@@ -420,22 +420,13 @@
     return (wide(a) + wide(b)).astype(BF)
 
 
-def reduce_steps(part, order):
-    left = ["z0", "z1", "flat"]
-    for dim in order:
-        name = dim if dim[0] == "z" else "flat"
-        axis = left.index(name)
-        left.remove(name)
-        if name == "flat":
-            keeps = colour() ^ place_bit(dim)
-            send = lax.dynamic_index_in_dim(part, 1 - keeps, axis, False)
-            keep = lax.dynamic_index_in_dim(part, keeps, axis, False)
-        else:
-            send = lax.index_in_dim(part, 1, axis, False)
-            keep = lax.index_in_dim(part, 0, axis, False)
-        received = yield swap(send, dim)
-        part = add(keep, received)
-    yield part
+def reduce_part(sent, kept, order):
+    part = add(kept, swap(sent, order[0])).reshape(2, 2, 256, 256)
+    for i, dim in enumerate(order[1:]):
+        axis = int(dim[1]) if i == 0 else 0
+        send = lax.index_in_dim(part, 1, axis, False)
+        part = add(lax.index_in_dim(part, 0, axis, False), swap(send, dim))
+    return part
 
 
 def finish_group(parts, exchanged, last):
@@ -478,6 +469,27 @@
     )(holds, *finished)
 
 
+def join_kernel(core, own, other, out):
+    straight = core[0] == 0
+    out[0, :, :WIDTH] = jnp.where(straight, own[...], other[...])
+    out[0, :, WIDTH:] = jnp.where(straight, other[...], own[...])
+
+
+def join_heads(core, own, other):
+    half = pl.BlockSpec((256, WIDTH), lambda i, c: (i, 0))
+    return pl.pallas_call(
+        join_kernel,
+        name="join_heads",
+        grid_spec=pltpu.PrefetchScalarGridSpec(
+            num_scalar_prefetch=1,
+            grid=(2,),
+            in_specs=[half, half],
+            out_specs=pl.BlockSpec((1, 256, 2 * WIDTH), lambda i, c: (0, i, 0)),
+        ),
+        out_shape=shape((1, BLOCK, 2 * WIDTH), BF),
+    )(core.reshape(1), own, other)
+
+
 def adam_kernel(core, kept, received, weights, first, second, out_weights, out_first, out_second):
     for block in range(6):
         at = slice(block * WIDTH, (block + 1) * WIDTH)
@@ -485,8 +497,8 @@
         gradient = jnp.where(block % 2 == core[0], kept[:, source], received[:, source]).astype(F32)
         new_first = BETA_ONE * first[:, at] + (1.0 - BETA_ONE) * gradient
         new_second = BETA_TWO * second[:, at] + (1.0 - BETA_TWO) * gradient * gradient
-        first_hat = new_first / (1.0 - BETA_ONE**STEP)
-        second_hat = new_second / (1.0 - BETA_TWO**STEP)
+        first_hat = new_first * (1.0 / (1.0 - BETA_ONE**STEP))
+        second_hat = new_second * (1.0 / (1.0 - BETA_TWO**STEP))
         out_first[:, at] = new_first
         out_second[:, at] = new_second
         out_weights[:, at] = weights[:, at] - LEARN_RATE * (
@@ -563,33 +575,17 @@
     q1, d1 = backward(1, qkv_second, grad, state)
     received, q0, q1, d1 = barrier((received, q0, q1, d1))
     received = steps.send(received)
-    parts = parts_of(query_gradient(q0, q1, both))
+    parts = query_gradient(q0, q1, both)
     received, parts = barrier((received, parts))
     received = steps.send(received)
-    queries = [reduce_steps(part, order) for part, order in zip(parts, HALVING)]
-    arrived = [next(part) for part in queries]
     later = steps.send(received)
-
-    operands = (qkv_first, qkv_second, d0, d1, later, both)
-    parts = parts_of(key_value_gradient(0, *operands))
-    parts, arrived, operands = barrier((parts, arrived, operands))
-    arrived = [part.send(x) for part, x in zip(queries, arrived)]
-    others = [reduce_steps(part, order) for part, order in zip(parts, HALVING[2:])]
-    moving = [next(part) for part in others]
-    parts = parts_of(key_value_gradient(1, *operands))
-    parts, arrived = barrier((parts, arrived))
-    arrived = [part.send(x) for part, x in zip(queries, arrived)]
-    others += [reduce_steps(part, order) for part, order in zip(parts, HALVING[4:])]
-    moving += [next(part) for part in others[2:]]
-    reduced = [part.send(x) for part, x in zip(queries, arrived)]
-    for _ in range(3):
-        moving = [part.send(x) for part, x in zip(others, moving)]
-    reduced += moving
+    parts += key_value_gradient(qkv_first, qkv_second, d0, d1, later, both)
+    reduced = [
+        reduce_part(parts[2 * p], parts[2 * p + 1], order) for p, order in enumerate(HALVING)
+    ]
 
     attended_other = swap(attended[BLOCK:], "c")
-    low = jnp.where(core == 0, attended[:BLOCK], attended_other)
-    high = jnp.where(core == 0, attended_other, attended[:BLOCK])
-    attended_out = jnp.concatenate([low, high], 1)[None]
+    attended_out = join_heads(core, attended, attended_other)
 
     holds, finished = [], []
     for members, exchanged, last in GROUPS:

time: 277 us -> 268 us (0.968)
  local copies, waits for them, and re-layouts: 17.9 us -> 6.88 us
  other arithmetic: 12 us -> 7.97 us
  starting transfers between devices: 76 us -> 79.3 us
  waiting for transfers between devices: 82.9 us -> 86.2 us
    slice x3, local copies, waits for them, and re-layouts: 5.09 us -> 0.06 us  [reduce_part(): send = lax.index_in_dim(part, 1, axis, False)]
    squeeze x18 -> x9, local copies, waits for them, and re-layouts: 5.04 us -> 0.12 us  [reduce_part(): send = lax.index_in_dim(part, 1, axis, False)]
    ppermute x54, starting transfers between devices: 67.3 us -> 70.6 us  [swap(): return lax.ppermute(x, dim[0], PAIRS[dim[1]])]
    convert_element_type x24, other arithmetic: 4.9 us -> 1.79 us  [add(): return (wide(a) + wide(b)).astype(BF)]
  transfers between devices with their start and end apart: 61 -> 61, of which waited for: 32 -> 27; matrix products, arithmetic and copies ran while one was open for 11% -> 5% of each run, Pallas kernels for 16% -> 16%
where the time goes in v2:
time: 268 us; the launch traced here: 266 us
  waiting for transfers between devices  86.2 us (32%)
  starting transfers between devices  79.3 us (30%)
  Pallas kernels  75.2 us (28%)
  matrix products  9 us (3%)
  other arithmetic  7.97 us (3%)
  local copies, waits for them, and re-layouts  6.88 us (3%)
    ppermute x54, starting transfers between devices, swap(): return lax.ppermute(x, dim[0], PAIRS[dim[1]])  70.6 us
    ppermute x54, waiting for transfers between devices, swap(): return lax.ppermute(x, dim[0], PAIRS[dim[1]])  69.9 us
    pallas_call x2, Pallas kernels, gradient_call(): pl.pallas_call(kernel, in_specs=[pl.BlockSpec(memory_space=pltpu.SMEM)] +...  20.9 us
    pallas_call x2, Pallas kernels, backward(): pl.pallas_call(backward_kernel, name='backward', grid_spec=pltpu.Prefetch...  10.8 us
    pallas_call x1, Pallas kernels, adam(): pl.pallas_call(adam_kernel, name='adam', grid_spec=pltpu.PrefetchScalarGr...  10.2 us
    all_to_all x1, waiting for transfers between devices, earlier_states(): received = lax.all_to_all(cut, ('x', 'y'), 0, 0, tiled=True)  9.99 us
    dot_general x2, matrix products, project(): return jnp.dot(tokens, weights, preferred_element_type=F32).astype(BF)  9 us
    pallas_call x1, Pallas kernels, arrange(): pl.pallas_call(arrange_kernel, name='arrange', grid_spec=pltpu.PrefetchSc...  7.34 us
  transfers between devices with their start and end apart: 61, of which 27 were waited for; matrix products, arithmetic and copies ran while one was open for 5% of the time, Pallas kernels for 16%

profile of v2, /device:TPU:0, one launch (start us, length us, event | category | flops | bytes accessed | tf_op | source)
XLA Modules:
  0.0 266.1 jit_solution(16979959057957813450)
XLA Ops:
  0.6 3.1 %prepare.1 = (bf16[4,256,384]{2,1,0:T(8,128)(2,1)}, bf16[4,256,384]{2,1,0:T(8,128)(2,1)}, bf16[512,512]{1,0:T(8,128)(2,1)}) custom-call(s32[1]{0:T(128)} %bitcast.core, f32[256,3072]{1,0:T(8,128)} %weights.1, f32[256,3072]{1,0:T(8,128)} %weights.1, f32[256,3072]{1,0:T(8,128)} %weights.1, f32[256,3072]{1,0:T(8,128)} %weights.1, f32[256,3072]{1,0:T(8,128)} %weights.1, ...), custom_call_target="tpu_custom_call" | custom-call | tf_op jit(solution)/shard_map/prepare/pallas_call | solution.py:119
  7.6 4.2 %collective-permute-start.3 = (bf16[1,256,384]{2,1,0:T(8,128)(2,1)S(1)}, bf16[1,256,384]{2,1,0:T(8,128)(2,1)S(1)}, u32[]{:S(2)}, u32[]{:S(2)}) collective-permute-start(bf16[1,256,384]{2,1,0:T(8,128)(2,1)S(1)} %get-tuple-element.108), channel_id=1, source_target_pairs={{2,4},{4,2},{6,0},{0,6},{3,5},{5,3},{7,1},{1,7},{10,12},{12,10},{1... | collective-permute-start | bytes 589832 | tf_op jit(solution)/shard_map/ppermute | solution.py:55
  11.8 4.1 %collective-permute-done.3 = bf16[1,256,384]{2,1,0:T(8,128)(2,1)S(1)} collective-permute-done((bf16[1,256,384]{2,1,0:T(8,128)(2,1)S(1)}, bf16[1,256,384]{2,1,0:T(8,128)(2,1)S(1)}, u32[]{:S(2)}, u32[]{:S(2)}) %collective-permute-start.3) | collective-permute-done | bytes 196640 | tf_op jit(solution)/shard_map/ppermute | solution.py:55
  19.7 6.2 %collective-permute-done.4 = bf16[2,256,384]{2,1,0:T(8,128)(2,1)S(1)} collective-permute-done((bf16[2,256,384]{2,1,0:T(8,128)(2,1)S(1)}, bf16[2,256,384]{2,1,0:T(8,128)(2,1)S(1)}, u32[]{:S(2)}, u32[]{:S(2)}) %collective-permute-start.4) | collective-permute-done | bytes 393248 | tf_op jit(solution)/shard_map/ppermute | solution.py:55
  28.9 7.3 %arrange.1.tokens = bf16[1024,2048]{1,0:T(8,128)(2,1)} custom-call(s32[8]{0:T(128)} %stack.90.blocks, bf16[512,2048]{1,0:T(8,128)(2,1)} %bitcast.10.own, bf16[512,2048]{1,0:T(8,128)(2,1)} %collective-permute-done.5.other), custom_call_target="tpu_custom_call" | custom-call | tf_op jit(solution)/shard_map/arrange/pallas_call | solution.py:140
  38.3 4.2 %collective-permute-start.12 = (bf16[2,256,384]{2,1,0:T(8,128)(2,1)S(1)}, bf16[2,256,384]{2,1,0:T(8,128)(2,1)S(1)}, u32[]{:S(2)}, u32[]{:S(2)}) collective-permute-start(bf16[2,256,384]{2,1,0:T(8,128)(2,1)S(1)} %get-tuple-element.105), channel_id=1, source_target_pairs={{0,8},{8,0},{16,24},{24,16},{1,9},{9,1},{17,25},{25,17},{2,10},{10... | collective-permute-start | bytes 1179656 | tf_op jit(solution)/shard_map/ppermute | solution.py:55
  45.6 4.3 %collective-permute-start.13 = (bf16[2,256,384]{2,1,0:T(8,128)(2,1)S(1)}, bf16[2,256,384]{2,1,0:T(8,128)(2,1)S(1)}, u32[]{:S(2)}, u32[]{:S(2)}) collective-permute-start(bf16[2,256,384]{2,1,0:T(8,128)(2,1)S(1)} %get-tuple-element.104), channel_id=1, source_target_pairs={{8,16},{16,8},{24,0},{0,24},{9,17},{17,9},{25,1},{1,25},{10,18},{1... | collective-permute-start | bytes 1179656 | tf_op jit(solution)/shard_map/ppermute | solution.py:55
  53.1 4.5 %collective-permute-done.13 = bf16[2,256,384]{2,1,0:T(8,128)(2,1)S(1)} collective-permute-done((bf16[2,256,384]{2,1,0:T(8,128)(2,1)S(1)}, bf16[2,256,384]{2,1,0:T(8,128)(2,1)S(1)}, u32[]{:S(2)}, u32[]{:S(2)}) %collective-permute-start.13) | collective-permute-done | bytes 393248 | tf_op jit(solution)/shard_map/ppermute | solution.py:55
  58.0 4.5 %fusion.11.first.k0.v0.qkv = bf16[1024,768]{1,0:T(8,128)(2,1)} fusion(bf16[1024,2048]{1,0:T(8,128)(2,1)S(1)} %copy-done, bf16[2048,384]{1,0:T(8,128)(2,1)S(1)} %fusion.38, bf16[2048,384]{1,0:T(8,128)(2,1)S(1)} %fusion.42), kind=kOutput, calls=%fused_computation.9 | convolution fusion | flops 3228303360 | bytes 8912896 | tf_op jit(solution)/shard_map/dot_general | solution.py:184
  65.9 3.0 %collective-permute-start.17 = (bf16[2,256,384]{2,1,0:T(8,128)(2,1)S(1)}, bf16[2,256,384]{2,1,0:T(8,128)(2,1)S(1)}, u32[]{:S(2)}, u32[]{:S(2)}) collective-permute-start(bf16[2,256,384]{2,1,0:T(8,128)(2,1)S(1)} %get-tuple-element.100), channel_id=1, source_target_pairs={{8,16},{16,8},{24,0},{0,24},{9,17},{17,9},{25,1},{1,25},{10,18},{1... | collective-permute-start | bytes 1179656 | tf_op jit(solution)/shard_map/ppermute | solution.py:55
  69.0 4.8 %collective-permute-done.14 = bf16[2,256,384]{2,1,0:T(8,128)(2,1)S(1)} collective-permute-done((bf16[2,256,384]{2,1,0:T(8,128)(2,1)S(1)}, bf16[2,256,384]{2,1,0:T(8,128)(2,1)S(1)}, u32[]{:S(2)}, u32[]{:S(2)}) %collective-permute-start.14) | collective-permute-done | bytes 393248 | tf_op jit(solution)/shard_map/ppermute | solution.py:55
  77.1 4.5 %fusion.8.second.k1.v1.qkv = bf16[1024,768]{1,0:T(8,128)(2,1)} fusion(bf16[1024,2048]{1,0:T(8,128)(2,1)S(1)} %copy-done, bf16[2048,384]{1,0:T(8,128)(2,1)S(1)} %fusion.30, bf16[2048,384]{1,0:T(8,128)(2,1)S(1)} %fusion.34), kind=kOutput, calls=%fused_computation.8 | convolution fusion | flops 3228303360 | bytes 8912896 | tf_op jit(solution)/shard_map/dot_general | solution.py:184
  84.3 3.8 %all-to-all-start = ((f32[16,64,128]{2,1,0:T(8,128)}), f32[16,64,128]{2,1,0:T(8,128)S(1)}, u32[]{:S(2)}, u32[]{:S(2)}) async-start(f32[16,64,128]{2,1,0:T(8,128)} %bitcast.220), calls=%async_computation | async-start | bytes 1048576 | tf_op jit(solution)/shard_map/all_to_all | solution.py:213
  88.2 10.0 %all-to-all-done.received = f32[16,64,128]{2,1,0:T(8,128)S(1)} async-done(((f32[16,64,128]{2,1,0:T(8,128)}), f32[16,64,128]{2,1,0:T(8,128)S(1)}, u32[]{:S(2)}, u32[]{:S(2)}) %all-to-all-start) | async-done | bytes 524320 | tf_op jit(solution)/shard_map/all_to_all | solution.py:213
  100.8 3.7 %all-to-all-start.1 = ((bf16[16,64,128]{2,1,0:T(8,128)(2,1)}), bf16[16,64,128]{2,1,0:T(8,128)(2,1)S(1)}, u32[]{:S(2)}, u32[]{:S(2)}) async-start(bf16[16,64,128]{2,1,0:T(8,128)(2,1)} %running.1), calls=%async_computation.1 | async-start | bytes 524288 | tf_op jit(solution)/shard_map/all_to_all | solution.py:221
  104.5 6.5 %within.1 = f32[1024,512]{1,0:T(8,128)} custom-call(bf16[1024,768]{1,0:T(8,128)(2,1)} %fusion.11.first.k0.v0.qkv, bf16[1024,768]{1,0:T(8,128)(2,1)} %fusion.8.second.k1.v1.qkv), custom_call_target="tpu_custom_call" | custom-call | tf_op jit(solution)/shard_map/within/pallas_call | solution.py:265
  113.5 6.9 %forward.1 = (bf16[1024,512]{1,0:T(8,128)(2,1)}, bf16[1024,512]{1,0:T(8,128)(2,1)}, bf16[4,2,128,128]{3,2,1,0:T(8,128)(2,1)}) custom-call(s32[1]{0:T(128)} %bitcast.core, bf16[1024,768]{1,0:T(8,128)(2,1)} %fusion.11.first.k0.v0.qkv, bf16[1024,768]{1,0:T(8,128)(2,1)} %fusion.8.second.k1.v1.qkv, f32[1024,512]{1,0:T(8,128)} %within.1, ...), custom_call_target="tpu_custom_call" | custom-call | tf_op jit(solution)/shard_map/forward/pallas_call | solution.py:297
  120.8 5.4 %backward.2 = (bf16[1024,256]{1,0:T(8,128)(2,1)}, f32[2,1024,256]{2,1,0:T(8,128)}) custom-call(s32[1]{0:T(128)} %constant.24.clone.1.pair, bf16[1024,768]{1,0:T(8,128)(2,1)} %fusion.11.first.k0.v0.qkv, bf16[1024,512]{1,0:T(8,128)(2,1)} %get-tuple-element.68.grad, bf16[4,2,128,128]{3,2,1,0:T(8,128)(2,1)} %bitcast.210), custom_call_target="tpu_custom_call" | custom-call | tf_op jit(solution)/shard_map/backward/pallas_call | solution.py:333
  128.5 5.4 %backward.3 = (bf16[1024,256]{1,0:T(8,128)(2,1)}, f32[2,1024,256]{2,1,0:T(8,128)}) custom-call(s32[1]{0:T(128)} %constant.25.clone.1.pair, bf16[1024,768]{1,0:T(8,128)(2,1)} %fusion.8.second.k1.v1.qkv, bf16[1024,512]{1,0:T(8,128)(2,1)} %get-tuple-element.68.grad, bf16[4,2,128,128]{3,2,1,0:T(8,128)(2,1)} %bitcast.211), custom_call_target="tpu_custom_call" | custom-call | tf_op jit(solution)/shard_map/backward/pallas_call | solution.py:333
  136.1 7.0 %shard_map.84 = (bf16[4,256,256]{2,1,0:T(8,128)(2,1)}, bf16[4,256,256]{2,1,0:T(8,128)(2,1)}, bf16[4,256,256]{2,1,0:T(8,128)(2,1)}, bf16[4,256,256]{2,1,0:T(8,128)(2,1)}) custom-call(s32[2]{0:T(128)} %pad_add_fusion.keeps, bf16[1024,256]{1,0:T(8,128)(2,1)} %get-tuple-element.72.q0, bf16[1024,256]{1,0:T(8,128)(2,1)} %get-tuple-element.73.q1, ...), custom_call_target="tpu_custom_call" | custom-call | tf_op jit(solution)/shard_map/pallas_call | solution.py:397
  147.5 4.8 %collective-permute-done.26 = bf16[4,2,128,128]{3,2,1,0:T(8,128)(2,1)S(1)} collective-permute-done((bf16[4,2,128,128]{3,2,1,0:T(8,128)(2,1)S(1)}, bf16[4,2,128,128]{3,2,1,0:T(8,128)(2,1)S(1)}, u32[]{:S(2)}, u32[]{:S(2)}) %collective-permute-start.26) | collective-permute-done | bytes 262176 | tf_op jit(solution)/shard_map/ppermute | solution.py:55
  153.3 13.9 %shard_map.85 = (bf16[4,256,256]{2,1,0:T(8,128)(2,1)}, bf16[4,256,256]{2,1,0:T(8,128)(2,1)}, bf16[4,256,256]{2,1,0:T(8,128)(2,1)}, bf16[4,256,256]{2,1,0:T(8,128...) custom-call(s32[4]{0:T(128)} %pad_add_fusion.1.keeps, ...), custom_call_target="tpu_custom_call" | custom-call | tf_op jit(solution)/shard_map/pallas_call | solution.py:397
  171.9 4.7 %collective-permute-done.27 = bf16[4,256,256]{2,1,0:T(8,128)(2,1)S(1)} collective-permute-done((bf16[4,256,256]{2,1,0:T(8,128)(2,1)}, bf16[4,256,256]{2,1,0:T(8,128)(2,1)S(1)}, u32[]{:S(2)}, u32[]{:S(2)}) %collective-permute-start.27) | collective-permute-done | bytes 524320 | tf_op jit(solution)/shard_map/ppermute | solution.py:55
  186.0 7.3 %collective-permute-done.25 = bf16[256,256]{1,0:T(8,128)(2,1)S(1)} collective-permute-done((bf16[256,256]{1,0:T(8,128)(2,1)S(1)}, bf16[256,256]{1,0:T(8,128)(2,1)S(1)}, u32[]{:S(2)}, u32[]{:S(2)}) %collective-permute-start.25) | collective-permute-done | bytes 131104 | tf_op jit(solution)/shard_map/ppermute | solution.py:55
  193.3 4.9 %collective-permute-done.36 = bf16[256,256]{1,0:T(8,128)(2,1)S(1)} collective-permute-done((bf16[256,256]{1,0:T(8,128)(2,1)S(1)}, bf16[256,256]{1,0:T(8,128)(2,1)S(1)}, u32[]{:S(2)}, u32[]{:S(2)}) %collective-permute-start.36) | collective-permute-done | bytes 131104 | tf_op jit(solution)/shard_map/ppermute | solution.py:55
  209.6 3.3 %collective-permute-start.40 = (bf16[2,256,256]{2,1,0:T(8,128)(2,1)S(1)}, bf16[2,256,256]{2,1,0:T(8,128)(2,1)S(1)}, u32[]{:S(2)}, u32[]{:S(2)}) collective-permute-start(bf16[2,256,256]{2,1,0:T(8,128)(2,1)S(1)} %pad_maximum_fusion.9), channel_id=1, source_target_pairs={{8,16},{16,8},{24,0},{0,24},{9,17},{17,9},{25,1},{1,25},{10,18},{1... | collective-permute-start | bytes 786440 | tf_op jit(solution)/shard_map/ppermute | solution.py:55
  214.2 4.8 %collective-permute-done.48 = bf16[1,256,256]{2,1,0:T(8,128)(2,1)S(1)} collective-permute-done((bf16[1,256,256]{2,1,0:T(8,128)(2,1)S(1)}, bf16[1,256,256]{2,1,0:T(8,128)(2,1)S(1)}, u32[]{:S(2)}, u32[]{:S(2)}) %collective-permute-start.48) | collective-permute-done | bytes 131104 | tf_op jit(solution)/shard_map/ppermute | solution.py:55
  226.0 3.4 %collective-permute-done.31 = bf16[2,256,256]{2,1,0:T(8,128)(2,1)S(1)} collective-permute-done((bf16[2,256,256]{2,1,0:T(8,128)(2,1)S(1)}, bf16[2,256,256]{2,1,0:T(8,128)(2,1)S(1)}, u32[]{:S(2)}, u32[]{:S(2)}) %collective-permute-start.31) | collective-permute-done | bytes 262176 | tf_op jit(solution)/shard_map/ppermute | solution.py:55
  232.3 3.7 %collective-permute-done.32 = bf16[2,256,256]{2,1,0:T(8,128)(2,1)S(1)} collective-permute-done((bf16[2,256,256]{2,1,0:T(8,128)(2,1)S(1)}, bf16[2,256,256]{2,1,0:T(8,128)(2,1)S(1)}, u32[]{:S(2)}, u32[]{:S(2)}) %collective-permute-start.32) | collective-permute-done | bytes 262176 | tf_op jit(solution)/shard_map/ppermute | solution.py:55
  240.9 3.7 %collective-permute-done.57.refs_7_ = bf16[1,256,256]{2,1,0:T(8,128)(2,1)S(1)} collective-permute-done((bf16[1,256,256]{2,1,0:T(8,128)(2,1)S(1)}, bf16[1,256,256]{2,1,0:T(8,128)(2,1)S(1)}, u32[]{:S(2)}, u32[]{:S(2)}) %collective-permute-start.57) | collective-permute-done | bytes 131104 | tf_op jit(solution)/shard_map/ppermute | solution.py:55
  246.0 3.0 %sort_pieces.1 = (bf16[256,1536]{1,0:T(8,128)(2,1)}, bf16[256,1536]{1,0:T(8,128)(2,1)}) custom-call(s32[4]{0:T(128)} %add_convert_fusion.21.holds, bf16[2,256,256]{2,1,0:T(8,128)(2,1)} %copy-done.5, bf16[2,256,256]{2,1,0:T(8,128)(2,1)} %copy-done.18, bf16[2,256,256]{2,1,0:T(8,128)(2,1)} %copy-done.6, bf16[2,256,256]{2,1,0:T(8,128)(2,1)} %copy-done.19, ...), custom_call_target="tpu_custom_call" | custom-call | tf_op jit(solution)/shard_map/sort_pieces/pallas_call | solution.py:463
  256.0 10.2 %adam.1 = (f32[256,3072]{1,0:T(8,128)}, f32[256,3072]{1,0:T(8,128)}, f32[256,3072]{1,0:T(8,128)}) custom-call(s32[1]{0:T(128)} %bitcast.core, bf16[256,1536]{1,0:T(8,128)(2,1)} %get-tuple-element.93.kept, bf16[256,1536]{1,0:T(8,128)(2,1)} %copy-done.7, f32[256,3072]{1,0:T(8,128)} %weights.1, f32[256,3072]{1,0:T(8,128)} %first.1, f32[256,3072]{1,0:T(8,128)} %second.1), custom_call_target="tpu_custom_call" | custom-call | tf_op jit(solution)/shard_map/adam/pallas_call | solution.py:512
  (250 shorter events, 93.5 us)
Async XLA Ops:
  3.8 25.1 %collective-permute-start.5 = (bf16[512,2048]{1,0:T(8,128)(2,1)}, bf16[512,2048]{1,0:T(8,128)(2,1)}, u32[]{:S(2)}, u32[]{:S(2)}) collective-permute-start(bf16[512,2048]{1,0:T(8,128)(2,1)} %bitcast.10.own), channel_id=1, source_target_pairs={{0,1},{1,0},{2,3},{3,2},{4,5},{5,4},{6,7},{7,6},{8,9},{9,8},{10,11... | collective-permute-start | bytes 6291464 | tf_op jit(solution)/shard_map/ppermute | solution.py:54
  15.9 10.0 %collective-permute-start.4 = (bf16[2,256,384]{2,1,0:T(8,128)(2,1)S(1)}, bf16[2,256,384]{2,1,0:T(8,128)(2,1)S(1)}, u32[]{:S(2)}, u32[]{:S(2)}) collective-permute-start(bf16[2,256,384]{2,1,0:T(8,128)(2,1)S(1)} %pad_maximum_fusion.5), channel_id=1, source_target_pairs={{0,2},{2,0},{4,6},{6,4},{1,3},{3,1},{5,7},{7,5},{8,10},{10,8},{12,... | collective-permute-start | bytes 1179656 | tf_op jit(solution)/shard_map/ppermute | solution.py:55
  17.9 9.8 %collective-permute-start.2 = (bf16[2,256,384]{2,1,0:T(8,128)(2,1)S(1)}, bf16[2,256,384]{2,1,0:T(8,128)(2,1)}, u32[]{:S(2)}, u32[]{:S(2)}) collective-permute-start(bf16[2,256,384]{2,1,0:T(8,128)(2,1)S(1)} %pad_maximum_fusion.4), channel_id=1, source_target_pairs={{2,4},{4,2},{6,0},{0,6},{3,5},{5,3},{7,1},{1,7},{10,12},{12,10},{1... | collective-permute-start | bytes 1179656 | tf_op jit(solution)/shard_map/ppermute | solution.py:55
  38.2 11.8 %collective-permute-start.6 = (bf16[1,256,384]{2,1,0:T(8,128)(2,1)S(1)}, bf16[1,256,384]{2,1,0:T(8,128)(2,1)S(1)}, u32[]{:S(2)}, u32[]{:S(2)}) collective-permute-start(bf16[1,256,384]{2,1,0:T(8,128)(2,1)S(1)} %get-tuple-element.107), channel_id=1, source_target_pairs={{0,2},{2,0},{4,6},{6,4},{1,3},{3,1},{5,7},{7,5},{8,10},{10,8},{12,... | collective-permute-start | bytes 589832 | tf_op jit(solution)/shard_map/ppermute | solution.py:55
  38.3 12.4 %collective-permute-start.12 = (bf16[2,256,384]{2,1,0:T(8,128)(2,1)S(1)}, bf16[2,256,384]{2,1,0:T(8,128)(2,1)S(1)}, u32[]{:S(2)}, u32[]{:S(2)}) collective-permute-start(bf16[2,256,384]{2,1,0:T(8,128)(2,1)S(1)} %get-tuple-element.105), channel_id=1, source_target_pairs={{0,8},{8,0},{16,24},{24,16},{1,9},{9,1},{17,25},{25,17},{2,10},{10... | collective-permute-start | bytes 1179656 | tf_op jit(solution)/shard_map/ppermute | solution.py:55
  42.5 15.2 %collective-permute-start.11 = (bf16[2,256,384]{2,1,0:T(8,128)(2,1)S(1)}, bf16[2,256,384]{2,1,0:T(8,128)(2,1)S(1)}, u32[]{:S(2)}, u32[]{:S(2)}) collective-permute-start(bf16[2,256,384]{2,1,0:T(8,128)(2,1)S(1)} %get-tuple-element.102), channel_id=1, source_target_pairs={{32,64},{64,32},{96,0},{0,96},{33,65},{65,33},{97,1},{1,97},{34,66... | collective-permute-start | bytes 1179656 | tf_op jit(solution)/shard_map/ppermute | solution.py:55
  43.8 13.8 %collective-permute-start.10 = (bf16[2,256,384]{2,1,0:T(8,128)(2,1)S(1)}, bf16[2,256,384]{2,1,0:T(8,128)(2,1)S(1)}, u32[]{:S(2)}, u32[]{:S(2)}) collective-permute-start(bf16[2,256,384]{2,1,0:T(8,128)(2,1)S(1)} %get-tuple-element.103), channel_id=1, source_target_pairs={{0,32},{32,0},{64,96},{96,64},{1,33},{33,1},{65,97},{97,65},{2,34}... | collective-permute-start | bytes 1179656 | tf_op jit(solution)/shard_map/ppermute | solution.py:55
  45.6 11.9 %collective-permute-start.13 = (bf16[2,256,384]{2,1,0:T(8,128)(2,1)S(1)}, bf16[2,256,384]{2,1,0:T(8,128)(2,1)S(1)}, u32[]{:S(2)}, u32[]{:S(2)}) collective-permute-start(bf16[2,256,384]{2,1,0:T(8,128)(2,1)S(1)} %get-tuple-element.104), channel_id=1, source_target_pairs={{8,16},{16,8},{24,0},{0,24},{9,17},{17,9},{25,1},{1,25},{10,18},{1... | collective-permute-start | bytes 1179656 | tf_op jit(solution)/shard_map/ppermute | solution.py:55
  49.9 12.5 %collective-permute-start.9 = (bf16[2,256,384]{2,1,0:T(8,128)(2,1)S(1)}, bf16[2,256,384]{2,1,0:T(8,128)(2,1)S(1)}, u32[]{:S(2)}, u32[]{:S(2)}) collective-permute-start(bf16[2,256,384]{2,1,0:T(8,128)(2,1)S(1)} %pad_maximum_fusion.7), channel_id=1, source_target_pairs={{0,2},{2,0},{4,6},{6,4},{1,3},{3,1},{5,7},{7,5},{8,10},{10,8},{12,... | collective-permute-start | bytes 1179656 | tf_op jit(solution)/shard_map/ppermute | solution.py:55
  50.8 11.8 %collective-permute-start.7 = (bf16[2,256,384]{2,1,0:T(8,128)(2,1)S(1)}, bf16[2,256,384]{2,1,0:T(8,128)(2,1)S(1)}, u32[]{:S(2)}, u32[]{:S(2)}) collective-permute-start(bf16[2,256,384]{2,1,0:T(8,128)(2,1)S(1)} %pad_maximum_fusion.6), channel_id=1, source_target_pairs={{2,4},{4,2},{6,0},{0,6},{3,5},{5,3},{7,1},{1,7},{10,12},{12,10},{1... | collective-permute-start | bytes 1179656 | tf_op jit(solution)/shard_map/ppermute | solution.py:55
  62.8 11.1 %collective-permute-start.15 = (bf16[2,256,384]{2,1,0:T(8,128)(2,1)S(1)}, bf16[2,256,384]{2,1,0:T(8,128)(2,1)S(1)}, u32[]{:S(2)}, u32[]{:S(2)}) collective-permute-start(bf16[2,256,384]{2,1,0:T(8,128)(2,1)S(1)} %get-tuple-element.98), channel_id=1, source_target_pairs={{32,64},{64,32},{96,0},{0,96},{33,65},{65,33},{97,1},{1,97},{34,66... | collective-permute-start | bytes 1179656 | tf_op jit(solution)/shard_map/ppermute | solution.py:55
  65.9 11.0 %collective-permute-start.17 = (bf16[2,256,384]{2,1,0:T(8,128)(2,1)S(1)}, bf16[2,256,384]{2,1,0:T(8,128)(2,1)S(1)}, u32[]{:S(2)}, u32[]{:S(2)}) collective-permute-start(bf16[2,256,384]{2,1,0:T(8,128)(2,1)S(1)} %get-tuple-element.100), channel_id=1, source_target_pairs={{8,16},{16,8},{24,0},{0,24},{9,17},{17,9},{25,1},{1,25},{10,18},{1... | collective-permute-start | bytes 1179656 | tf_op jit(solution)/shard_map/ppermute | solution.py:55
  84.3 13.9 %all-to-all-start = ((f32[16,64,128]{2,1,0:T(8,128)}), f32[16,64,128]{2,1,0:T(8,128)S(1)}, u32[]{:S(2)}, u32[]{:S(2)}) async-start(f32[16,64,128]{2,1,0:T(8,128)} %bitcast.220), calls=%async_computation | async-start | bytes 1048576 | tf_op jit(solution)/shard_map/all_to_all | solution.py:213
  88.1 22.9 %collective-permute-start.18 = (bf16[512,512]{1,0:T(8,128)(2,1)S(1)}, bf16[512,512]{1,0:T(8,128)(2,1)S(1)}, u32[]{:S(2)}, u32[]{:S(2)}) collective-permute-start(bf16[512,512]{1,0:T(8,128)(2,1)S(1)} %copy-done.22), channel_id=1, source_target_pairs={{0,1},{1,0},{2,3},{3,2},{4,5},{5,4},{6,7},{7,6},{8,9},{9,8},{10,11... | collective-permute-start | bytes 1572872 | tf_op jit(solution)/shard_map/ppermute | solution.py:54
  100.8 12.0 %all-to-all-start.1 = ((bf16[16,64,128]{2,1,0:T(8,128)(2,1)}), bf16[16,64,128]{2,1,0:T(8,128)(2,1)S(1)}, u32[]{:S(2)}, u32[]{:S(2)}) async-start(bf16[16,64,128]{2,1,0:T(8,128)(2,1)} %running.1), calls=%async_computation.1 | async-start | bytes 524288 | tf_op jit(solution)/shard_map/all_to_all | solution.py:221
  143.3 26.0 %collective-permute-start.23 = (bf16[4,256,256]{2,1,0:T(8,128)(2,1)}, bf16[4,256,256]{2,1,0:T(8,128)(2,1)S(1)}, u32[]{:S(2)}, u32[]{:S(2)}) collective-permute-start(bf16[4,256,256]{2,1,0:T(8,128)(2,1)} %get-tuple-element.79), channel_id=1, source_target_pairs={{0,32},{32,0},{64,96},{96,64},{1,33},{33,1},{65,97},{97,65},{2,34}... | collective-permute-start | bytes 1572872 | tf_op jit(solution)/shard_map/ppermute | solution.py:55
  146.6 25.0 %collective-permute-start.34 = (bf16[4,256,256]{2,1,0:T(8,128)(2,1)}, bf16[4,256,256]{2,1,0:T(8,128)(2,1)S(1)}, u32[]{:S(2)}, u32[]{:S(2)}) collective-permute-start(bf16[4,256,256]{2,1,0:T(8,128)(2,1)} %get-tuple-element.86), channel_id=1, source_target_pairs={{0,8},{8,0},{16,24},{24,16},{1,9},{9,1},{17,25},{25,17},{2,10},{10... | collective-permute-start | bytes 1572872 | tf_op jit(solution)/shard_map/ppermute | solution.py:55
  167.2 10.7 %collective-permute-start.37 = (bf16[4,256,256]{2,1,0:T(8,128)(2,1)}, bf16[4,256,256]{2,1,0:T(8,128)(2,1)S(1)}, u32[]{:S(2)}, u32[]{:S(2)}) collective-permute-start(bf16[4,256,256]{2,1,0:T(8,128)(2,1)} %get-tuple-element.88), channel_id=1, source_target_pairs={{0,8},{8,0},{16,24},{24,16},{1,9},{9,1},{17,25},{25,17},{2,10},{10... | collective-permute-start | bytes 1572872 | tf_op jit(solution)/shard_map/ppermute | solution.py:55
  167.3 10.8 %collective-permute-start.44 = (bf16[4,256,256]{2,1,0:T(8,128)(2,1)}, bf16[4,256,256]{2,1,0:T(8,128)(2,1)S(1)}, u32[]{:S(2)}, u32[]{:S(2)}) collective-permute-start(bf16[4,256,256]{2,1,0:T(8,128)(2,1)} %get-tuple-element.90), channel_id=1, source_target_pairs={{32,64},{64,32},{96,0},{0,96},{33,65},{65,33},{97,1},{1,97},{34,66... | collective-permute-start | bytes 1572872 | tf_op jit(solution)/shard_map/ppermute | solution.py:55
  169.4 11.1 %collective-permute-start.51 = (bf16[4,256,256]{2,1,0:T(8,128)(2,1)}, bf16[4,256,256]{2,1,0:T(8,128)(2,1)S(1)}, u32[]{:S(2)}, u32[]{:S(2)}) collective-permute-start(bf16[4,256,256]{2,1,0:T(8,128)(2,1)} %get-tuple-element.92), channel_id=1, source_target_pairs={{8,16},{16,8},{24,0},{0,24},{9,17},{17,9},{25,1},{1,25},{10,18},{1... | collective-permute-start | bytes 1572872 | tf_op jit(solution)/shard_map/ppermute | solution.py:55
  171.6 10.7 %collective-permute-start.24 = (bf16[2,256,256]{2,1,0:T(8,128)(2,1)S(1)}, bf16[2,256,256]{2,1,0:T(8,128)(2,1)S(1)}, u32[]{:S(2)}, u32[]{:S(2)}) collective-permute-start(bf16[2,256,256]{2,1,0:T(8,128)(2,1)S(1)} %slice.301), channel_id=1, source_target_pairs={{0,2},{2,0},{4,6},{6,4},{1,3},{3,1},{5,7},{7,5},{8,10},{10,8},{12,... | collective-permute-start | bytes 786440 | tf_op jit(solution)/shard_map/ppermute | solution.py:55
  177.8 20.4 %collective-permute-start.28 = (bf16[2,256,256]{2,1,0:T(8,128)(2,1)S(1)}, bf16[2,256,256]{2,1,0:T(8,128)(2,1)S(1)}, u32[]{:S(2)}, u32[]{:S(2)}) collective-permute-start(bf16[2,256,256]{2,1,0:T(8,128)(2,1)S(1)} %slice.305), channel_id=1, source_target_pairs={{0,2},{2,0},{4,6},{6,4},{1,3},{3,1},{5,7},{7,5},{8,10},{10,8},{12,... | collective-permute-start | bytes 786440 | tf_op jit(solution)/shard_map/ppermute | solution.py:55
  178.1 21.4 %collective-permute-start.38 = (bf16[2,256,256]{2,1,0:T(8,128)(2,1)S(1)}, bf16[2,256,256]{2,1,0:T(8,128)(2,1)S(1)}, u32[]{:S(2)}, u32[]{:S(2)}) collective-permute-start(bf16[2,256,256]{2,1,0:T(8,128)(2,1)S(1)} %slice_bitcast_fusion.2), channel_id=1, source_target_pairs={{2,4},{4,2},{6,0},{0,6},{3,5},{5,3},{7,1},{1,7},{10,12},{12,10},{1... | collective-permute-start | bytes 786440 | tf_op jit(solution)/shard_map/ppermute | solution.py:55
  180.5 19.5 %collective-permute-start.45 = (bf16[2,256,256]{2,1,0:T(8,128)(2,1)S(1)}, bf16[2,256,256]{2,1,0:T(8,128)(2,1)S(1)}, u32[]{:S(2)}, u32[]{:S(2)}) collective-permute-start(bf16[2,256,256]{2,1,0:T(8,128)(2,1)S(1)} %slice.317), channel_id=1, source_target_pairs={{0,2},{2,0},{4,6},{6,4},{1,3},{3,1},{5,7},{7,5},{8,10},{10,8},{12,... | collective-permute-start | bytes 786440 | tf_op jit(solution)/shard_map/ppermute | solution.py:55
  182.4 19.7 %collective-permute-start.52 = (bf16[2,256,256]{2,1,0:T(8,128)(2,1)S(1)}, bf16[2,256,256]{2,1,0:T(8,128)(2,1)S(1)}, u32[]{:S(2)}, u32[]{:S(2)}) collective-permute-start(bf16[2,256,256]{2,1,0:T(8,128)(2,1)S(1)} %slice_bitcast_fusion), channel_id=1, source_target_pairs={{2,4},{4,2},{6,0},{0,6},{3,5},{5,3},{7,1},{1,7},{10,12},{12,10},{1... | collective-permute-start | bytes 786440 | tf_op jit(solution)/shard_map/ppermute | solution.py:55
  199.6 9.8 %collective-permute-start.39 = (bf16[256,256]{1,0:T(8,128)(2,1)S(1)}, bf16[256,256]{1,0:T(8,128)(2,1)S(1)}, u32[]{:S(2)}, u32[]{:S(2)}) collective-permute-start(bf16[256,256]{1,0:T(8,128)(2,1)S(1)} %slice_bitcast_fusion.26), channel_id=1, source_target_pairs={{0,2},{2,0},{4,6},{6,4},{1,3},{3,1},{5,7},{7,5},{8,10},{10,8},{12,... | collective-permute-start | bytes 393224 | tf_op jit(solution)/shard_map/ppermute | solution.py:55
  208.2 13.0 %collective-permute-start.30 = (bf16[2,256,256]{2,1,0:T(8,128)(2,1)S(1)}, bf16[2,256,256]{2,1,0:T(8,128)(2,1)S(1)}, u32[]{:S(2)}, u32[]{:S(2)}) collective-permute-start(bf16[2,256,256]{2,1,0:T(8,128)(2,1)S(1)} %pad_maximum_fusion.8), channel_id=1, source_target_pairs={{32,64},{64,32},{96,0},{0,96},{33,65},{65,33},{97,1},{1,97},{34,66... | collective-permute-start | bytes 786440 | tf_op jit(solution)/shard_map/ppermute | solution.py:55
  209.6 12.9 %collective-permute-start.40 = (bf16[2,256,256]{2,1,0:T(8,128)(2,1)S(1)}, bf16[2,256,256]{2,1,0:T(8,128)(2,1)S(1)}, u32[]{:S(2)}, u32[]{:S(2)}) collective-permute-start(bf16[2,256,256]{2,1,0:T(8,128)(2,1)S(1)} %pad_maximum_fusion.9), channel_id=1, source_target_pairs={{8,16},{16,8},{24,0},{0,24},{9,17},{17,9},{25,1},{1,25},{10,18},{1... | collective-permute-start | bytes 786440 | tf_op jit(solution)/shard_map/ppermute | solution.py:55
  213.9 10.5 %collective-permute-start.55 = (bf16[1,256,256]{2,1,0:T(8,128)(2,1)S(1)}, bf16[1,256,256]{2,1,0:T(8,128)(2,1)S(1)}, u32[]{:S(2)}, u32[]{:S(2)}) collective-permute-start(bf16[1,256,256]{2,1,0:T(8,128)(2,1)S(1)} %add_convert_fusion.17), channel_id=1, source_target_pairs={{0,8},{8,0},{16,24},{24,16},{1,9},{9,1},{17,25},{25,17},{2,10},{10... | collective-permute-start | bytes 393224 | tf_op jit(solution)/shard_map/ppermute | solution.py:55
  219.0 11.4 %collective-permute-start.49 = (bf16[1,256,256]{2,1,0:T(8,128)(2,1)S(1)}, bf16[1,256,256]{2,1,0:T(8,128)(2,1)S(1)}, u32[]{:S(2)}, u32[]{:S(2)}) collective-permute-start(bf16[1,256,256]{2,1,0:T(8,128)(2,1)S(1)} %add_convert_fusion.19), channel_id=1, source_target_pairs={{8,16},{16,8},{24,0},{0,24},{9,17},{17,9},{25,1},{1,25},{10,18},{1... | collective-permute-start | bytes 393224 | tf_op jit(solution)/shard_map/ppermute | solution.py:55
  224.4 13.9 %collective-permute-start.56 = (bf16[1,256,256]{2,1,0:T(8,128)(2,1)S(1)}, bf16[1,256,256]{2,1,0:T(8,128)(2,1)S(1)}, u32[]{:S(2)}, u32[]{:S(2)}) collective-permute-start(bf16[1,256,256]{2,1,0:T(8,128)(2,1)S(1)} %add_convert_fusion.16), channel_id=1, source_target_pairs={{32,64},{64,32},{96,0},{0,96},{33,65},{65,33},{97,1},{1,97},{34,66... | collective-permute-start | bytes 393224 | tf_op jit(solution)/shard_map/ppermute | solution.py:55
  230.5 10.4 %collective-permute-start.50 = (bf16[1,256,256]{2,1,0:T(8,128)(2,1)S(1)}, bf16[1,256,256]{2,1,0:T(8,128)(2,1)S(1)}, u32[]{:S(2)}, u32[]{:S(2)}) collective-permute-start(bf16[1,256,256]{2,1,0:T(8,128)(2,1)S(1)} %add_convert_fusion.18.refs_4_), channel_id=1, source_target_pairs={{32,64},{64,32},{96,0},{0,96},{33,65},{65,33},{97,1},{1,97},{34,66... | collective-permute-start | bytes 393224 | tf_op jit(solution)/shard_map/ppermute | solution.py:55
  (52 other events, 325.0 us)

commit v3 on v2

--- a/solution.py
+++ b/solution.py
@@ -350,32 +350,47 @@
     )(jnp.full((1,), pair, jnp.int32), qkv, grad, state)
 
 
-def multiply_blocks(keeps, turned, tokens, outs):
+def token_copy(i, tokens, held, sems):
+    at = pl.ds(pl.multiple_of(i * 512, 512), 512)
+    return pltpu.make_async_copy(tokens.at[:, at], held.at[:, at], sems.at[i])
+
+
+def fetch_tokens(tokens, held, sems):
+    for i in range(4):
+        token_copy(i, tokens, held, sems).start()
+
+
+def multiply_blocks(keeps, offset, turned, held, arriving, outs):
     def blocks(i, carry):
+        if arriving is not None:
+            token_copy(i, *arriving).wait()
         at = pl.ds(pl.multiple_of(i * 512, 512), 512)
-        piece = dot(turned[...], tokens[:, at], 1, 0).astype(BF)
+        piece = dot(turned[...], held[:, at], 1, 0).astype(BF)
         for part in range(2):
             sent, kept = outs[2 * part], outs[2 * part + 1]
             first = piece[part * 256 : (part + 1) * 256, :256]
             second = piece[part * 256 : (part + 1) * 256, 256:]
-            kept[i] = jnp.where(keeps[part] == 0, first, second)
-            sent[i] = jnp.where(keeps[part] == 0, second, first)
+            straight = keeps[offset + part] == 0
+            kept[i] = jnp.where(straight, first, second)
+            sent[i] = jnp.where(straight, second, first)
         return carry
 
-    lax.fori_loop(0, tokens.shape[1] // 512, blocks, 0)
-
-
-def query_gradient_kernel(keeps, q0, q1, tokens, s0, k0, s1, k1, turned):
+    lax.fori_loop(0, 4, blocks, 0)
+
+
+def query_gradient_kernel(keeps, q0, q1, tokens, s0, k0, s1, k1, turned, held, sems):
+    fetch_tokens(tokens, held, sems)
     turned[:256, :] = q0[...].T
     turned[256:, :] = q1[...].T
-    multiply_blocks(keeps, turned, tokens, (s0, k0, s1, k1))
-
-
-def gradient_kernel(keeps, first, second, d_first, d_second, state, tokens, *refs):
-    turned = refs[-1]
+    multiply_blocks(keeps, 0, turned, held, (tokens, held, sems), (s0, k0, s1, k1))
+
+
+def gradient_kernel(keeps, k0, v0, k1, v1, d0, d1, state, tokens, *refs):
+    outs, (turned, held, sems) = refs[:8], refs[8:]
+    fetch_tokens(tokens, held, sems)
     for kind in range(2):
-        sides = ((first, d_first), (second, d_second))
-        for pair, (qkv, within) in enumerate(sides):
+        sides = ((v0 if kind == 0 else k0, d0), (v1 if kind == 0 else k1, d1))
+        for pair, (source, within) in enumerate(sides):
 
             @each_head
             def _(h):
@@ -383,12 +398,12 @@
                 at = head_cols(h)
                 for s in range(2):
                     span = slice(s * BLOCK, (s + 1) * BLOCK)
-                    source = qkv[span, head_cols(4 - 2 * kind + h)]
-                    later = dot(source, state[head, s], 1, 1 - kind)
+                    later = dot(source[span, at], state[head, s], 1, 1 - kind)
                     total = within[kind, span, at] + later
                     turned[head_cols(head), span] = total.astype(BF).T
 
-        multiply_blocks(keeps.at[pl.ds(2 * kind, 2)], turned, tokens, refs[4 * kind : 4 * kind + 4])
+        arriving = (tokens, held, sems) if kind == 0 else None
+        multiply_blocks(keeps, 2 * kind, turned, held, arriving, outs[4 * kind : 4 * kind + 4])
 
 
 def gradient_call(kernel, first, ins, specs, tokens):
@@ -396,10 +411,17 @@
     keeps = jnp.stack([colour() ^ place_bit(HALVING[p][0]) for p in first]).astype(jnp.int32)
     return pl.pallas_call(
         kernel,
-        in_specs=[pl.BlockSpec(memory_space=pltpu.SMEM)] + specs + [VMEM],
+        grid=(1,),
+        in_specs=[pl.BlockSpec(memory_space=pltpu.SMEM)]
+        + specs
+        + [pl.BlockSpec(memory_space=pl.ANY)],
         out_specs=(VMEM,) * (2 * count),
         out_shape=(shape((4, 256, 256), BF),) * (2 * count),
-        scratch_shapes=[pltpu.VMEM((WIDTH, ROWS), BF)],
+        scratch_shapes=[
+            pltpu.VMEM((WIDTH, ROWS), BF),
+            pltpu.VMEM((ROWS, 2048), BF),
+            pltpu.SemaphoreType.DMA((4,)),
+        ],
     )(keeps, *ins, tokens)
 
 
@@ -408,8 +430,9 @@
 
 
 def key_value_gradient(first, second, d_first, d_second, state, tokens):
-    ins = (first, second, d_first, d_second, state)
-    return gradient_call(gradient_kernel, (2, 3, 4, 5), ins, [VMEM] * 5, tokens)
+    specs = [pl.BlockSpec((ROWS, 256), lambda _, j=j: (0, j)) for j in (1, 2)] * 2 + [VMEM] * 3
+    ins = (first, first, second, second, d_first, d_second, state)
+    return gradient_call(gradient_kernel, (2, 3, 4, 5), ins, specs, tokens)
 
 
 def wide(x):
@@ -421,7 +444,8 @@
 
 
 def reduce_part(sent, kept, order):
-    part = add(kept, swap(sent, order[0])).reshape(2, 2, 256, 256)
+    received = swap(sent, order[0])
+    part = add(kept, received).reshape(2, 2, 256, 256)
     for i, dim in enumerate(order[1:]):
         axis = int(dim[1]) if i == 0 else 0
         send = lax.index_in_dim(part, 1, axis, False)
@@ -440,7 +464,8 @@
     total = wide(total)
     carried = jnp.zeros_like(total)
     for dim in ("y0", "y1", "x0", "x1"):
-        received = yield swap(total.astype(BF), dim)
+        moving = swap(total.astype(BF), dim)
+        received = yield moving
         received = wide(received)
         upper = (lax.axis_index(dim[0]) >> int(dim[1])) & 1
         carried = carried + jnp.where(upper == (0 if later else 1), received, 0.0)
@@ -454,9 +479,9 @@
         straight = holds[g] == 1
         for j, p in enumerate(members):
             at = slice(p * 256, (p + 1) * 256)
-            here, there = refs[2 * g][j].T, refs[2 * g + 1][j].T
-            kept[:, at] = jnp.where(straight, here, there)
-            sent[:, at] = jnp.where(straight, there, here)
+            here, there = refs[2 * g][j], refs[2 * g + 1][j]
+            kept[:, at] = jnp.where(straight, here, there).T
+            sent[:, at] = jnp.where(straight, there, here).T
 
 
 def sort_pieces(holds, finished):
@@ -490,36 +515,21 @@
     )(core.reshape(1), own, other)
 
 
-def adam_kernel(core, kept, received, weights, first, second, out_weights, out_first, out_second):
-    for block in range(6):
-        at = slice(block * WIDTH, (block + 1) * WIDTH)
-        source = slice((block // 2) * WIDTH, (block // 2 + 1) * WIDTH)
-        gradient = jnp.where(block % 2 == core[0], kept[:, source], received[:, source]).astype(F32)
-        new_first = BETA_ONE * first[:, at] + (1.0 - BETA_ONE) * gradient
-        new_second = BETA_TWO * second[:, at] + (1.0 - BETA_TWO) * gradient * gradient
-        first_hat = new_first * (1.0 / (1.0 - BETA_ONE**STEP))
-        second_hat = new_second * (1.0 / (1.0 - BETA_TWO**STEP))
-        out_first[:, at] = new_first
-        out_second[:, at] = new_second
-        out_weights[:, at] = weights[:, at] - LEARN_RATE * (
-            first_hat / (jnp.sqrt(second_hat) + EPS_ADAM) + DECAY_WEIGHT * weights[:, at]
-        )
-
-
-def adam(core, kept, received, *arrays):
-    piece = pl.BlockSpec((32, 3 * WIDTH), lambda i, c: (i, 0))
-    block = pl.BlockSpec((32, 6 * WIDTH), lambda i, c: (i, 0))
-    return pl.pallas_call(
-        adam_kernel,
-        name="adam",
-        grid_spec=pltpu.PrefetchScalarGridSpec(
-            num_scalar_prefetch=1,
-            grid=(8,),
-            in_specs=[piece, piece, block, block, block],
-            out_specs=(block,) * 3,
-        ),
-        out_shape=tuple(shape(x.shape, F32) for x in arrays),
-    )(core.reshape(1), kept, received, *arrays)
+def adam(core, kept, received, weights, first, second):
+    pieces = []
+    for kind in range(3):
+        at = slice(kind * WIDTH, (kind + 1) * WIDTH)
+        pieces.append(jnp.where(core == 0, kept[:, at], received[:, at]))
+        pieces.append(jnp.where(core == 0, received[:, at], kept[:, at]))
+    gradient = jnp.concatenate(pieces, 1).astype(F32)
+    new_first = BETA_ONE * first + (1.0 - BETA_ONE) * gradient
+    new_second = BETA_TWO * second + (1.0 - BETA_TWO) * gradient * gradient
+    first_hat = new_first * (1.0 / (1.0 - BETA_ONE**STEP))
+    second_hat = new_second * (1.0 / (1.0 - BETA_TWO**STEP))
+    new_weights = weights - LEARN_RATE * (
+        first_hat / (jnp.sqrt(second_hat) + EPS_ADAM) + DECAY_WEIGHT * weights
+    )
+    return new_weights, new_first, new_second
 
 
 def gather_step(step, mine):

time: 268 us -> 268 us (level)
  other arithmetic: 7.97 us -> 20.4 us
  Pallas kernels: 75.2 us -> 63.3 us
    pallas_call x3 -> x2, Pallas kernels: 31.1 us -> 19 us  [gradient_call(): pl.pallas_call(kernel, grid=(1,), in_specs=[pl.BlockSpec(memory_space=plt...]
    sub x0 -> x1, other arithmetic: none -> 5.91 us  [adam(): weights - LEARN_RATE * (first_hat / (jnp.sqrt(second_hat) + EPS_ADAM) + D...]
    unnamed x0 -> x5, other arithmetic: none -> 5.49 us
    unnamed x73 -> x75, local copies, waits for them, and re-layouts: 5.51 us -> 3.84 us
  transfers between devices with their start and end apart: 61 -> 61, of which waited for: 27 -> 27; matrix products, arithmetic and copies ran while one was open for 5% -> 5% of each run, Pallas kernels for 16% -> 15%
where the time goes in v3:
time: 268 us; the launch traced here: 266 us
  waiting for transfers between devices  86.5 us (32%)
  starting transfers between devices  79.6 us (30%)
  Pallas kernels  63.3 us (24%)
  other arithmetic  20.4 us (8%)
  matrix products  9 us (3%)
  local copies, waits for them, and re-layouts  5.27 us (2%)
    ppermute x54, starting transfers between devices, swap(): return lax.ppermute(x, dim[0], PAIRS[dim[1]])  70.9 us
    ppermute x54, waiting for transfers between devices, swap(): return lax.ppermute(x, dim[0], PAIRS[dim[1]])  70 us
    pallas_call x2, Pallas kernels, gradient_call(): pl.pallas_call(kernel, grid=(1,), in_specs=[pl.BlockSpec(memory_space=plt...  19 us
    pallas_call x2, Pallas kernels, backward(): pl.pallas_call(backward_kernel, name='backward', grid_spec=pltpu.Prefetch...  10.8 us
    all_to_all x1, waiting for transfers between devices, earlier_states(): received = lax.all_to_all(cut, ('x', 'y'), 0, 0, tiled=True)  9.99 us
    dot_general x2, matrix products, project(): return jnp.dot(tokens, weights, preferred_element_type=F32).astype(BF)  9 us
    pallas_call x1, Pallas kernels, arrange(): pl.pallas_call(arrange_kernel, name='arrange', grid_spec=pltpu.PrefetchSc...  7.34 us
    pallas_call x1, Pallas kernels, forward(): pl.pallas_call(forward_kernel, name='forward', grid_spec=pltpu.PrefetchSc...  6.87 us
  transfers between devices with their start and end apart: 61, of which 27 were waited for; matrix products, arithmetic and copies ran while one was open for 5% of the time, Pallas kernels for 15%

profile of v3, /device:TPU:0, one launch (start us, length us, event | category | flops | bytes accessed | tf_op | source)
XLA Modules:
  0.0 265.6 jit_solution(14156377275749095329)
XLA Ops:
  0.6 3.1 %prepare.1 = (bf16[4,256,384]{2,1,0:T(8,128)(2,1)}, bf16[4,256,384]{2,1,0:T(8,128)(2,1)}, bf16[512,512]{1,0:T(8,128)(2,1)}) custom-call(s32[1]{0:T(128)} %bitcast.core, f32[256,3072]{1,0:T(8,128)} %refs_5_.1, f32[256,3072]{1,0:T(8,128)} %refs_5_.1, f32[256,3072]{1,0:T(8,128)} %refs_5_.1, f32[256,3072]{1,0:T(8,128)} %refs_5_.1, f32[256,3072]{1,0:T(8,128)} %refs_5_.1, ...), custom_call_target="tpu_custom_call" | custom-call | tf_op jit(solution)/shard_map/prepare/pallas_call | solution.py:119
  7.6 4.2 %collective-permute-start.3 = (bf16[1,256,384]{2,1,0:T(8,128)(2,1)S(1)}, bf16[1,256,384]{2,1,0:T(8,128)(2,1)S(1)}, u32[]{:S(2)}, u32[]{:S(2)}) collective-permute-start(bf16[1,256,384]{2,1,0:T(8,128)(2,1)S(1)} %get-tuple-element.105), channel_id=1, source_target_pairs={{2,4},{4,2},{6,0},{0,6},{3,5},{5,3},{7,1},{1,7},{10,12},{12,10},{1... | collective-permute-start | bytes 589832 | tf_op jit(solution)/shard_map/ppermute | solution.py:55
  11.8 4.1 %collective-permute-done.3 = bf16[1,256,384]{2,1,0:T(8,128)(2,1)S(1)} collective-permute-done((bf16[1,256,384]{2,1,0:T(8,128)(2,1)S(1)}, bf16[1,256,384]{2,1,0:T(8,128)(2,1)S(1)}, u32[]{:S(2)}, u32[]{:S(2)}) %collective-permute-start.3) | collective-permute-done | bytes 196640 | tf_op jit(solution)/shard_map/ppermute | solution.py:55
  19.8 6.1 %collective-permute-done.4 = bf16[2,256,384]{2,1,0:T(8,128)(2,1)S(1)} collective-permute-done((bf16[2,256,384]{2,1,0:T(8,128)(2,1)S(1)}, bf16[2,256,384]{2,1,0:T(8,128)(2,1)S(1)}, u32[]{:S(2)}, u32[]{:S(2)}) %collective-permute-start.4) | collective-permute-done | bytes 393248 | tf_op jit(solution)/shard_map/ppermute | solution.py:55
  28.9 7.3 %arrange.1.tokens = bf16[1024,2048]{1,0:T(8,128)(2,1)} custom-call(s32[8]{0:T(128)} %stack.90.blocks, bf16[512,2048]{1,0:T(8,128)(2,1)} %bitcast.10.own, bf16[512,2048]{1,0:T(8,128)(2,1)} %collective-permute-done.5.other), custom_call_target="tpu_custom_call" | custom-call | tf_op jit(solution)/shard_map/arrange/pallas_call | solution.py:140
  38.3 4.2 %collective-permute-start.12 = (bf16[2,256,384]{2,1,0:T(8,128)(2,1)S(1)}, bf16[2,256,384]{2,1,0:T(8,128)(2,1)S(1)}, u32[]{:S(2)}, u32[]{:S(2)}) collective-permute-start(bf16[2,256,384]{2,1,0:T(8,128)(2,1)S(1)} %get-tuple-element.102), channel_id=1, source_target_pairs={{0,8},{8,0},{16,24},{24,16},{1,9},{9,1},{17,25},{25,17},{2,10},{10... | collective-permute-start | bytes 1179656 | tf_op jit(solution)/shard_map/ppermute | solution.py:55
  45.6 4.3 %collective-permute-start.13 = (bf16[2,256,384]{2,1,0:T(8,128)(2,1)S(1)}, bf16[2,256,384]{2,1,0:T(8,128)(2,1)S(1)}, u32[]{:S(2)}, u32[]{:S(2)}) collective-permute-start(bf16[2,256,384]{2,1,0:T(8,128)(2,1)S(1)} %get-tuple-element.101), channel_id=1, source_target_pairs={{8,16},{16,8},{24,0},{0,24},{9,17},{17,9},{25,1},{1,25},{10,18},{1... | collective-permute-start | bytes 1179656 | tf_op jit(solution)/shard_map/ppermute | solution.py:55
  53.1 4.5 %collective-permute-done.13 = bf16[2,256,384]{2,1,0:T(8,128)(2,1)S(1)} collective-permute-done((bf16[2,256,384]{2,1,0:T(8,128)(2,1)S(1)}, bf16[2,256,384]{2,1,0:T(8,128)(2,1)S(1)}, u32[]{:S(2)}, u32[]{:S(2)}) %collective-permute-start.13) | collective-permute-done | bytes 393248 | tf_op jit(solution)/shard_map/ppermute | solution.py:55
  58.0 4.5 %fusion.13.first.k0.v0.qkv = bf16[1024,768]{1,0:T(8,128)(2,1)} fusion(bf16[1024,2048]{1,0:T(8,128)(2,1)S(1)} %copy-done.1, bf16[2048,384]{1,0:T(8,128)(2,1)S(1)} %fusion.40, bf16[2048,384]{1,0:T(8,128)(2,1)S(1)} %fusion.44), kind=kOutput, calls=%fused_computation.14 | convolution fusion | flops 3228303360 | bytes 8912896 | tf_op jit(solution)/shard_map/dot_general | solution.py:184
  65.9 3.0 %collective-permute-start.17 = (bf16[2,256,384]{2,1,0:T(8,128)(2,1)S(1)}, bf16[2,256,384]{2,1,0:T(8,128)(2,1)S(1)}, u32[]{:S(2)}, u32[]{:S(2)}) collective-permute-start(bf16[2,256,384]{2,1,0:T(8,128)(2,1)S(1)} %get-tuple-element.97), channel_id=1, source_target_pairs={{8,16},{16,8},{24,0},{0,24},{9,17},{17,9},{25,1},{1,25},{10,18},{1... | collective-permute-start | bytes 1179656 | tf_op jit(solution)/shard_map/ppermute | solution.py:55
  69.0 4.8 %collective-permute-done.14 = bf16[2,256,384]{2,1,0:T(8,128)(2,1)S(1)} collective-permute-done((bf16[2,256,384]{2,1,0:T(8,128)(2,1)S(1)}, bf16[2,256,384]{2,1,0:T(8,128)(2,1)S(1)}, u32[]{:S(2)}, u32[]{:S(2)}) %collective-permute-start.14) | collective-permute-done | bytes 393248 | tf_op jit(solution)/shard_map/ppermute | solution.py:55
  77.1 4.5 %fusion.10.second.k1.v1.qkv = bf16[1024,768]{1,0:T(8,128)(2,1)} fusion(bf16[1024,2048]{1,0:T(8,128)(2,1)S(1)} %copy-done.1, bf16[2048,384]{1,0:T(8,128)(2,1)S(1)} %fusion.32, bf16[2048,384]{1,0:T(8,128)(2,1)S(1)} %fusion.36), kind=kOutput, calls=%fused_computation.13 | convolution fusion | flops 3228303360 | bytes 8912896 | tf_op jit(solution)/shard_map/dot_general | solution.py:184
  84.3 3.8 %all-to-all-start = ((f32[16,64,128]{2,1,0:T(8,128)}), f32[16,64,128]{2,1,0:T(8,128)S(1)}, u32[]{:S(2)}, u32[]{:S(2)}) async-start(f32[16,64,128]{2,1,0:T(8,128)} %bitcast.220), calls=%async_computation | async-start | bytes 1048576 | tf_op jit(solution)/shard_map/all_to_all | solution.py:213
  88.2 10.0 %all-to-all-done.received = f32[16,64,128]{2,1,0:T(8,128)S(1)} async-done(((f32[16,64,128]{2,1,0:T(8,128)}), f32[16,64,128]{2,1,0:T(8,128)S(1)}, u32[]{:S(2)}, u32[]{:S(2)}) %all-to-all-start) | async-done | bytes 524320 | tf_op jit(solution)/shard_map/all_to_all | solution.py:213
  100.7 3.7 %all-to-all-start.1 = ((bf16[16,64,128]{2,1,0:T(8,128)(2,1)}), bf16[16,64,128]{2,1,0:T(8,128)(2,1)S(1)}, u32[]{:S(2)}, u32[]{:S(2)}) async-start(bf16[16,64,128]{2,1,0:T(8,128)(2,1)} %running.1), calls=%async_computation.1 | async-start | bytes 524288 | tf_op jit(solution)/shard_map/all_to_all | solution.py:221
  104.5 6.5 %within.1 = f32[1024,512]{1,0:T(8,128)} custom-call(bf16[1024,768]{1,0:T(8,128)(2,1)} %fusion.13.first.k0.v0.qkv, bf16[1024,768]{1,0:T(8,128)(2,1)} %fusion.10.second.k1.v1.qkv), custom_call_target="tpu_custom_call" | custom-call | tf_op jit(solution)/shard_map/within/pallas_call | solution.py:265
  113.5 6.9 %forward.1 = (bf16[1024,512]{1,0:T(8,128)(2,1)}, bf16[1024,512]{1,0:T(8,128)(2,1)}, bf16[4,2,128,128]{3,2,1,0:T(8,128)(2,1)}) custom-call(s32[1]{0:T(128)} %bitcast.core, bf16[1024,768]{1,0:T(8,128)(2,1)} %fusion.13.first.k0.v0.qkv, bf16[1024,768]{1,0:T(8,128)(2,1)} %fusion.10.second.k1.v1.qkv, f32[1024,512]{1,0:T(8,128)} %within.1, ...), custom_call_target="tpu_custom_call" | custom-call | tf_op jit(solution)/shard_map/forward/pallas_call | solution.py:297
  120.8 5.4 %backward.2 = (bf16[1024,256]{1,0:T(8,128)(2,1)}, f32[2,1024,256]{2,1,0:T(8,128)}) custom-call(s32[1]{0:T(128)} %constant.12.clone.1.pair, bf16[1024,768]{1,0:T(8,128)(2,1)} %fusion.13.first.k0.v0.qkv, bf16[1024,512]{1,0:T(8,128)(2,1)} %get-tuple-element.65.grad, bf16[4,2,128,128]{3,2,1,0:T(8,128)(2,1)} %bitcast.210), custom_call_target="tpu_custom_call" | custom-call | tf_op jit(solution)/shard_map/backward/pallas_call | solution.py:333
  128.5 5.4 %backward.3 = (bf16[1024,256]{1,0:T(8,128)(2,1)}, f32[2,1024,256]{2,1,0:T(8,128)}) custom-call(s32[1]{0:T(128)} %constant.13.clone.1.pair, bf16[1024,768]{1,0:T(8,128)(2,1)} %fusion.10.second.k1.v1.qkv, bf16[1024,512]{1,0:T(8,128)(2,1)} %get-tuple-element.65.grad, bf16[4,2,128,128]{3,2,1,0:T(8,128)(2,1)} %bitcast.211), custom_call_target="tpu_custom_call" | custom-call | tf_op jit(solution)/shard_map/backward/pallas_call | solution.py:333
  136.1 6.6 %shard_map.84 = (bf16[4,256,256]{2,1,0:T(8,128)(2,1)}, bf16[4,256,256]{2,1,0:T(8,128)(2,1)}, bf16[4,256,256]{2,1,0:T(8,128)(2,1)}, bf16[4,256,256]{2,1,0:T(8,128)(2,1)}) custom-call(s32[2]{0:T(128)} %pad_add_fusion.keeps, bf16[1024,256]{1,0:T(8,128)(2,1)} %get-tuple-element.69.q0, bf16[1024,256]{1,0:T(8,128)(2,1)} %get-tuple-element.70.q1, ...), custom_call_target="tpu_custom_call" | custom-call | tf_op jit(solution)/shard_map/pallas_call | solution.py:412
  147.2 4.8 %collective-permute-done.26 = bf16[4,2,128,128]{3,2,1,0:T(8,128)(2,1)S(1)} collective-permute-done((bf16[4,2,128,128]{3,2,1,0:T(8,128)(2,1)S(1)}, bf16[4,2,128,128]{3,2,1,0:T(8,128)(2,1)S(1)}, u32[]{:S(2)}, u32[]{:S(2)}) %collective-permute-start.26) | collective-permute-done | bytes 262176 | tf_op jit(solution)/shard_map/ppermute | solution.py:55
  153.0 12.4 %shard_map.85 = (bf16[4,256,256]{2,1,0:T(8,128)(2,1)}, bf16[4,256,256]{2,1,0:T(8,128)(2,1)}, bf16[4,256,256]{2,1,0:T(8,128)(2,1)}, bf16[4,256,256]{2,1,0:T(8,128...) custom-call(s32[4]{0:T(128)} %pad_add_fusion.1.keeps, ...), custom_call_target="tpu_custom_call" | custom-call | tf_op jit(solution)/shard_map/pallas_call | solution.py:412
  170.6 4.2 %collective-permute-done.27 = bf16[4,256,256]{2,1,0:T(8,128)(2,1)S(1)} collective-permute-done((bf16[4,256,256]{2,1,0:T(8,128)(2,1)}, bf16[4,256,256]{2,1,0:T(8,128)(2,1)S(1)}, u32[]{:S(2)}, u32[]{:S(2)}) %collective-permute-start.27) | collective-permute-done | bytes 524320 | tf_op jit(solution)/shard_map/ppermute | solution.py:55
  184.2 7.3 %collective-permute-done.25 = bf16[256,256]{1,0:T(8,128)(2,1)S(1)} collective-permute-done((bf16[256,256]{1,0:T(8,128)(2,1)S(1)}, bf16[256,256]{1,0:T(8,128)(2,1)S(1)}, u32[]{:S(2)}, u32[]{:S(2)}) %collective-permute-start.25) | collective-permute-done | bytes 131104 | tf_op jit(solution)/shard_map/ppermute | solution.py:55
  191.6 4.9 %collective-permute-done.36 = bf16[256,256]{1,0:T(8,128)(2,1)S(1)} collective-permute-done((bf16[256,256]{1,0:T(8,128)(2,1)S(1)}, bf16[256,256]{1,0:T(8,128)(2,1)S(1)}, u32[]{:S(2)}, u32[]{:S(2)}) %collective-permute-start.36) | collective-permute-done | bytes 131104 | tf_op jit(solution)/shard_map/ppermute | solution.py:55
  207.8 3.8 %collective-permute-start.40 = (bf16[2,256,256]{2,1,0:T(8,128)(2,1)S(1)}, bf16[2,256,256]{2,1,0:T(8,128)(2,1)S(1)}, u32[]{:S(2)}, u32[]{:S(2)}) collective-permute-start(bf16[2,256,256]{2,1,0:T(8,128)(2,1)S(1)} %pad_maximum_fusion.9), channel_id=1, source_target_pairs={{8,16},{16,8},{24,0},{0,24},{9,17},{17,9},{25,1},{1,25},{10,18},{1... | collective-permute-start | bytes 786440 | tf_op jit(solution)/shard_map/ppermute | solution.py:55
  213.5 4.6 %collective-permute-done.48 = bf16[1,256,256]{2,1,0:T(8,128)(2,1)S(1)} collective-permute-done((bf16[1,256,256]{2,1,0:T(8,128)(2,1)S(1)}, bf16[1,256,256]{2,1,0:T(8,128)(2,1)S(1)}, u32[]{:S(2)}, u32[]{:S(2)}) %collective-permute-start.48) | collective-permute-done | bytes 131104 | tf_op jit(solution)/shard_map/ppermute | solution.py:55
  225.1 2.8 %collective-permute-done.31 = bf16[2,256,256]{2,1,0:T(8,128)(2,1)S(1)} collective-permute-done((bf16[2,256,256]{2,1,0:T(8,128)(2,1)S(1)}, bf16[2,256,256]{2,1,0:T(8,128)(2,1)S(1)}, u32[]{:S(2)}, u32[]{:S(2)}) %collective-permute-start.31) | collective-permute-done | bytes 262176 | tf_op jit(solution)/shard_map/ppermute | solution.py:55
  230.9 3.6 %collective-permute-done.32 = bf16[2,256,256]{2,1,0:T(8,128)(2,1)S(1)} collective-permute-done((bf16[2,256,256]{2,1,0:T(8,128)(2,1)S(1)}, bf16[2,256,256]{2,1,0:T(8,128)(2,1)S(1)}, u32[]{:S(2)}, u32[]{:S(2)}) %collective-permute-start.32) | collective-permute-done | bytes 262176 | tf_op jit(solution)/shard_map/ppermute | solution.py:55
  239.5 3.7 %collective-permute-done.57.refs_7_ = bf16[1,256,256]{2,1,0:T(8,128)(2,1)S(1)} collective-permute-done((bf16[1,256,256]{2,1,0:T(8,128)(2,1)S(1)}, bf16[1,256,256]{2,1,0:T(8,128)(2,1)S(1)}, u32[]{:S(2)}, u32[]{:S(2)}) %collective-permute-start.57) | collective-permute-done | bytes 131104 | tf_op jit(solution)/shard_map/ppermute | solution.py:55
  244.6 2.9 %sort_pieces.1 = (bf16[256,1536]{1,0:T(8,128)(2,1)}, bf16[256,1536]{1,0:T(8,128)(2,1)}) custom-call(s32[4]{0:T(128)} %add_convert_fusion.21.holds, bf16[2,256,256]{2,1,0:T(8,128)(2,1)} %copy-done.8, bf16[2,256,256]{2,1,0:T(8,128)(2,1)} %copy-done.19, bf16[2,256,256]{2,1,0:T(8,128)(2,1)} %copy-done.9, bf16[2,256,256]{2,1,0:T(8,128)(2,1)} %copy-done.20, ...), custom_call_target="tpu_custom_call" | custom-call | tf_op jit(solution)/shard_map/sort_pieces/pallas_call | solution.py:488
  259.7 5.9 %multiply_subtract_fusion = (f32[256,3072]{1,0:T(8,128)}, f32[256,3072]{1,0:T(8,128)}, f32[256,3072]{1,0:T(8,128)}) fusion(f32[256,3072]{1,0:T(8,128)S(1)} %copy-done, bf16[256,3072]{1,0:T(8,128)(2,1)S(1)} %select_dynamic-update-slice_fusion, f32[256,3072]{1,0:T(8,128)S(1)} %copy-done.3, f32[256,3072]{1,0:T(8,128)} %param.8), kind=kLoop, calls=%fused_computation.12 | loop fusion | flops 12582912 | bytes 20447232 | tf_op jit(solution)/shard_map/sub | solution.py:529
  (258 shorter events, 99.9 us)
Async XLA Ops:
  3.8 25.1 %collective-permute-start.5 = (bf16[512,2048]{1,0:T(8,128)(2,1)}, bf16[512,2048]{1,0:T(8,128)(2,1)}, u32[]{:S(2)}, u32[]{:S(2)}) collective-permute-start(bf16[512,2048]{1,0:T(8,128)(2,1)} %bitcast.10.own), channel_id=1, source_target_pairs={{0,1},{1,0},{2,3},{3,2},{4,5},{5,4},{6,7},{7,6},{8,9},{9,8},{10,11... | collective-permute-start | bytes 6291464 | tf_op jit(solution)/shard_map/ppermute | solution.py:54
  15.9 10.0 %collective-permute-start.4 = (bf16[2,256,384]{2,1,0:T(8,128)(2,1)S(1)}, bf16[2,256,384]{2,1,0:T(8,128)(2,1)S(1)}, u32[]{:S(2)}, u32[]{:S(2)}) collective-permute-start(bf16[2,256,384]{2,1,0:T(8,128)(2,1)S(1)} %pad_maximum_fusion.5), channel_id=1, source_target_pairs={{0,2},{2,0},{4,6},{6,4},{1,3},{3,1},{5,7},{7,5},{8,10},{10,8},{12,... | collective-permute-start | bytes 1179656 | tf_op jit(solution)/shard_map/ppermute | solution.py:55
  17.9 9.8 %collective-permute-start.2 = (bf16[2,256,384]{2,1,0:T(8,128)(2,1)S(1)}, bf16[2,256,384]{2,1,0:T(8,128)(2,1)}, u32[]{:S(2)}, u32[]{:S(2)}) collective-permute-start(bf16[2,256,384]{2,1,0:T(8,128)(2,1)S(1)} %pad_maximum_fusion.4), channel_id=1, source_target_pairs={{2,4},{4,2},{6,0},{0,6},{3,5},{5,3},{7,1},{1,7},{10,12},{12,10},{1... | collective-permute-start | bytes 1179656 | tf_op jit(solution)/shard_map/ppermute | solution.py:55
  38.2 11.8 %collective-permute-start.6 = (bf16[1,256,384]{2,1,0:T(8,128)(2,1)S(1)}, bf16[1,256,384]{2,1,0:T(8,128)(2,1)S(1)}, u32[]{:S(2)}, u32[]{:S(2)}) collective-permute-start(bf16[1,256,384]{2,1,0:T(8,128)(2,1)S(1)} %get-tuple-element.104), channel_id=1, source_target_pairs={{0,2},{2,0},{4,6},{6,4},{1,3},{3,1},{5,7},{7,5},{8,10},{10,8},{12,... | collective-permute-start | bytes 589832 | tf_op jit(solution)/shard_map/ppermute | solution.py:55
  38.3 12.4 %collective-permute-start.12 = (bf16[2,256,384]{2,1,0:T(8,128)(2,1)S(1)}, bf16[2,256,384]{2,1,0:T(8,128)(2,1)S(1)}, u32[]{:S(2)}, u32[]{:S(2)}) collective-permute-start(bf16[2,256,384]{2,1,0:T(8,128)(2,1)S(1)} %get-tuple-element.102), channel_id=1, source_target_pairs={{0,8},{8,0},{16,24},{24,16},{1,9},{9,1},{17,25},{25,17},{2,10},{10... | collective-permute-start | bytes 1179656 | tf_op jit(solution)/shard_map/ppermute | solution.py:55
  42.5 15.2 %collective-permute-start.11 = (bf16[2,256,384]{2,1,0:T(8,128)(2,1)S(1)}, bf16[2,256,384]{2,1,0:T(8,128)(2,1)S(1)}, u32[]{:S(2)}, u32[]{:S(2)}) collective-permute-start(bf16[2,256,384]{2,1,0:T(8,128)(2,1)S(1)} %get-tuple-element.99), channel_id=1, source_target_pairs={{32,64},{64,32},{96,0},{0,96},{33,65},{65,33},{97,1},{1,97},{34,66... | collective-permute-start | bytes 1179656 | tf_op jit(solution)/shard_map/ppermute | solution.py:55
  43.8 13.8 %collective-permute-start.10 = (bf16[2,256,384]{2,1,0:T(8,128)(2,1)S(1)}, bf16[2,256,384]{2,1,0:T(8,128)(2,1)S(1)}, u32[]{:S(2)}, u32[]{:S(2)}) collective-permute-start(bf16[2,256,384]{2,1,0:T(8,128)(2,1)S(1)} %get-tuple-element.100), channel_id=1, source_target_pairs={{0,32},{32,0},{64,96},{96,64},{1,33},{33,1},{65,97},{97,65},{2,34}... | collective-permute-start | bytes 1179656 | tf_op jit(solution)/shard_map/ppermute | solution.py:55
  45.6 11.9 %collective-permute-start.13 = (bf16[2,256,384]{2,1,0:T(8,128)(2,1)S(1)}, bf16[2,256,384]{2,1,0:T(8,128)(2,1)S(1)}, u32[]{:S(2)}, u32[]{:S(2)}) collective-permute-start(bf16[2,256,384]{2,1,0:T(8,128)(2,1)S(1)} %get-tuple-element.101), channel_id=1, source_target_pairs={{8,16},{16,8},{24,0},{0,24},{9,17},{17,9},{25,1},{1,25},{10,18},{1... | collective-permute-start | bytes 1179656 | tf_op jit(solution)/shard_map/ppermute | solution.py:55
  49.9 12.5 %collective-permute-start.9 = (bf16[2,256,384]{2,1,0:T(8,128)(2,1)S(1)}, bf16[2,256,384]{2,1,0:T(8,128)(2,1)S(1)}, u32[]{:S(2)}, u32[]{:S(2)}) collective-permute-start(bf16[2,256,384]{2,1,0:T(8,128)(2,1)S(1)} %pad_maximum_fusion.7), channel_id=1, source_target_pairs={{0,2},{2,0},{4,6},{6,4},{1,3},{3,1},{5,7},{7,5},{8,10},{10,8},{12,... | collective-permute-start | bytes 1179656 | tf_op jit(solution)/shard_map/ppermute | solution.py:55
  50.8 11.8 %collective-permute-start.7 = (bf16[2,256,384]{2,1,0:T(8,128)(2,1)S(1)}, bf16[2,256,384]{2,1,0:T(8,128)(2,1)S(1)}, u32[]{:S(2)}, u32[]{:S(2)}) collective-permute-start(bf16[2,256,384]{2,1,0:T(8,128)(2,1)S(1)} %pad_maximum_fusion.6), channel_id=1, source_target_pairs={{2,4},{4,2},{6,0},{0,6},{3,5},{5,3},{7,1},{1,7},{10,12},{12,10},{1... | collective-permute-start | bytes 1179656 | tf_op jit(solution)/shard_map/ppermute | solution.py:55
  62.8 11.1 %collective-permute-start.15 = (bf16[2,256,384]{2,1,0:T(8,128)(2,1)S(1)}, bf16[2,256,384]{2,1,0:T(8,128)(2,1)S(1)}, u32[]{:S(2)}, u32[]{:S(2)}) collective-permute-start(bf16[2,256,384]{2,1,0:T(8,128)(2,1)S(1)} %get-tuple-element.95), channel_id=1, source_target_pairs={{32,64},{64,32},{96,0},{0,96},{33,65},{65,33},{97,1},{1,97},{34,66... | collective-permute-start | bytes 1179656 | tf_op jit(solution)/shard_map/ppermute | solution.py:55
  65.9 11.0 %collective-permute-start.17 = (bf16[2,256,384]{2,1,0:T(8,128)(2,1)S(1)}, bf16[2,256,384]{2,1,0:T(8,128)(2,1)S(1)}, u32[]{:S(2)}, u32[]{:S(2)}) collective-permute-start(bf16[2,256,384]{2,1,0:T(8,128)(2,1)S(1)} %get-tuple-element.97), channel_id=1, source_target_pairs={{8,16},{16,8},{24,0},{0,24},{9,17},{17,9},{25,1},{1,25},{10,18},{1... | collective-permute-start | bytes 1179656 | tf_op jit(solution)/shard_map/ppermute | solution.py:55
  84.3 13.9 %all-to-all-start = ((f32[16,64,128]{2,1,0:T(8,128)}), f32[16,64,128]{2,1,0:T(8,128)S(1)}, u32[]{:S(2)}, u32[]{:S(2)}) async-start(f32[16,64,128]{2,1,0:T(8,128)} %bitcast.220), calls=%async_computation | async-start | bytes 1048576 | tf_op jit(solution)/shard_map/all_to_all | solution.py:213
  88.1 22.9 %collective-permute-start.18 = (bf16[512,512]{1,0:T(8,128)(2,1)S(1)}, bf16[512,512]{1,0:T(8,128)(2,1)S(1)}, u32[]{:S(2)}, u32[]{:S(2)}) collective-permute-start(bf16[512,512]{1,0:T(8,128)(2,1)S(1)} %copy-done.23), channel_id=1, source_target_pairs={{0,1},{1,0},{2,3},{3,2},{4,5},{5,4},{6,7},{7,6},{8,9},{9,8},{10,11... | collective-permute-start | bytes 1572872 | tf_op jit(solution)/shard_map/ppermute | solution.py:54
  100.7 12.0 %all-to-all-start.1 = ((bf16[16,64,128]{2,1,0:T(8,128)(2,1)}), bf16[16,64,128]{2,1,0:T(8,128)(2,1)S(1)}, u32[]{:S(2)}, u32[]{:S(2)}) async-start(bf16[16,64,128]{2,1,0:T(8,128)(2,1)} %running.1), calls=%async_computation.1 | async-start | bytes 524288 | tf_op jit(solution)/shard_map/all_to_all | solution.py:221
  143.6 24.0 %collective-permute-start.23 = (bf16[4,256,256]{2,1,0:T(8,128)(2,1)}, bf16[4,256,256]{2,1,0:T(8,128)(2,1)S(1)}, u32[]{:S(2)}, u32[]{:S(2)}) collective-permute-start(bf16[4,256,256]{2,1,0:T(8,128)(2,1)} %get-tuple-element.76), channel_id=1, source_target_pairs={{0,32},{32,0},{64,96},{96,64},{1,33},{33,1},{65,97},{97,65},{2,34}... | collective-permute-start | bytes 1572872 | tf_op jit(solution)/shard_map/ppermute | solution.py:55
  146.3 24.0 %collective-permute-start.34 = (bf16[4,256,256]{2,1,0:T(8,128)(2,1)}, bf16[4,256,256]{2,1,0:T(8,128)(2,1)S(1)}, u32[]{:S(2)}, u32[]{:S(2)}) collective-permute-start(bf16[4,256,256]{2,1,0:T(8,128)(2,1)} %get-tuple-element.83), channel_id=1, source_target_pairs={{0,8},{8,0},{16,24},{24,16},{1,9},{9,1},{17,25},{25,17},{2,10},{10... | collective-permute-start | bytes 1572872 | tf_op jit(solution)/shard_map/ppermute | solution.py:55
  165.6 10.5 %collective-permute-start.37 = (bf16[4,256,256]{2,1,0:T(8,128)(2,1)}, bf16[4,256,256]{2,1,0:T(8,128)(2,1)S(1)}, u32[]{:S(2)}, u32[]{:S(2)}) collective-permute-start(bf16[4,256,256]{2,1,0:T(8,128)(2,1)} %get-tuple-element.85), channel_id=1, source_target_pairs={{0,8},{8,0},{16,24},{24,16},{1,9},{9,1},{17,25},{25,17},{2,10},{10... | collective-permute-start | bytes 1572872 | tf_op jit(solution)/shard_map/ppermute | solution.py:55
  165.6 10.9 %collective-permute-start.44 = (bf16[4,256,256]{2,1,0:T(8,128)(2,1)}, bf16[4,256,256]{2,1,0:T(8,128)(2,1)S(1)}, u32[]{:S(2)}, u32[]{:S(2)}) collective-permute-start(bf16[4,256,256]{2,1,0:T(8,128)(2,1)} %get-tuple-element.87), channel_id=1, source_target_pairs={{32,64},{64,32},{96,0},{0,96},{33,65},{65,33},{97,1},{1,97},{34,66... | collective-permute-start | bytes 1572872 | tf_op jit(solution)/shard_map/ppermute | solution.py:55
  167.7 11.1 %collective-permute-start.51 = (bf16[4,256,256]{2,1,0:T(8,128)(2,1)}, bf16[4,256,256]{2,1,0:T(8,128)(2,1)S(1)}, u32[]{:S(2)}, u32[]{:S(2)}) collective-permute-start(bf16[4,256,256]{2,1,0:T(8,128)(2,1)} %get-tuple-element.89), channel_id=1, source_target_pairs={{8,16},{16,8},{24,0},{0,24},{9,17},{17,9},{25,1},{1,25},{10,18},{1... | collective-permute-start | bytes 1572872 | tf_op jit(solution)/shard_map/ppermute | solution.py:55
  170.3 10.3 %collective-permute-start.24 = (bf16[2,256,256]{2,1,0:T(8,128)(2,1)S(1)}, bf16[2,256,256]{2,1,0:T(8,128)(2,1)S(1)}, u32[]{:S(2)}, u32[]{:S(2)}) collective-permute-start(bf16[2,256,256]{2,1,0:T(8,128)(2,1)S(1)} %slice.331), channel_id=1, source_target_pairs={{0,2},{2,0},{4,6},{6,4},{1,3},{3,1},{5,7},{7,5},{8,10},{10,8},{12,... | collective-permute-start | bytes 786440 | tf_op jit(solution)/shard_map/ppermute | solution.py:55
  176.1 20.4 %collective-permute-start.28 = (bf16[2,256,256]{2,1,0:T(8,128)(2,1)S(1)}, bf16[2,256,256]{2,1,0:T(8,128)(2,1)S(1)}, u32[]{:S(2)}, u32[]{:S(2)}) collective-permute-start(bf16[2,256,256]{2,1,0:T(8,128)(2,1)S(1)} %slice.335), channel_id=1, source_target_pairs={{0,2},{2,0},{4,6},{6,4},{1,3},{3,1},{5,7},{7,5},{8,10},{10,8},{12,... | collective-permute-start | bytes 786440 | tf_op jit(solution)/shard_map/ppermute | solution.py:55
  176.5 21.4 %collective-permute-start.38 = (bf16[2,256,256]{2,1,0:T(8,128)(2,1)S(1)}, bf16[2,256,256]{2,1,0:T(8,128)(2,1)S(1)}, u32[]{:S(2)}, u32[]{:S(2)}) collective-permute-start(bf16[2,256,256]{2,1,0:T(8,128)(2,1)S(1)} %slice_bitcast_fusion.2), channel_id=1, source_target_pairs={{2,4},{4,2},{6,0},{0,6},{3,5},{5,3},{7,1},{1,7},{10,12},{12,10},{1... | collective-permute-start | bytes 786440 | tf_op jit(solution)/shard_map/ppermute | solution.py:55
  178.8 19.5 %collective-permute-start.45 = (bf16[2,256,256]{2,1,0:T(8,128)(2,1)S(1)}, bf16[2,256,256]{2,1,0:T(8,128)(2,1)S(1)}, u32[]{:S(2)}, u32[]{:S(2)}) collective-permute-start(bf16[2,256,256]{2,1,0:T(8,128)(2,1)S(1)} %slice.347), channel_id=1, source_target_pairs={{0,2},{2,0},{4,6},{6,4},{1,3},{3,1},{5,7},{7,5},{8,10},{10,8},{12,... | collective-permute-start | bytes 786440 | tf_op jit(solution)/shard_map/ppermute | solution.py:55
  180.7 19.7 %collective-permute-start.52 = (bf16[2,256,256]{2,1,0:T(8,128)(2,1)S(1)}, bf16[2,256,256]{2,1,0:T(8,128)(2,1)S(1)}, u32[]{:S(2)}, u32[]{:S(2)}) collective-permute-start(bf16[2,256,256]{2,1,0:T(8,128)(2,1)S(1)} %slice_bitcast_fusion), channel_id=1, source_target_pairs={{2,4},{4,2},{6,0},{0,6},{3,5},{5,3},{7,1},{1,7},{10,12},{12,10},{1... | collective-permute-start | bytes 786440 | tf_op jit(solution)/shard_map/ppermute | solution.py:55
  196.7 10.1 %collective-permute-start.29 = (bf16[256,256]{1,0:T(8,128)(2,1)S(1)}, bf16[256,256]{1,0:T(8,128)(2,1)S(1)}, u32[]{:S(2)}, u32[]{:S(2)}) collective-permute-start(bf16[256,256]{1,0:T(8,128)(2,1)S(1)} %slice_bitcast_fusion.30), channel_id=1, source_target_pairs={{2,4},{4,2},{6,0},{0,6},{3,5},{5,3},{7,1},{1,7},{10,12},{12,10},{1... | collective-permute-start | bytes 393224 | tf_op jit(solution)/shard_map/ppermute | solution.py:55
  206.9 12.8 %collective-permute-start.30 = (bf16[2,256,256]{2,1,0:T(8,128)(2,1)S(1)}, bf16[2,256,256]{2,1,0:T(8,128)(2,1)S(1)}, u32[]{:S(2)}, u32[]{:S(2)}) collective-permute-start(bf16[2,256,256]{2,1,0:T(8,128)(2,1)S(1)} %pad_maximum_fusion.8), channel_id=1, source_target_pairs={{32,64},{64,32},{96,0},{0,96},{33,65},{65,33},{97,1},{1,97},{34,66... | collective-permute-start | bytes 786440 | tf_op jit(solution)/shard_map/ppermute | solution.py:55
  207.8 13.8 %collective-permute-start.40 = (bf16[2,256,256]{2,1,0:T(8,128)(2,1)S(1)}, bf16[2,256,256]{2,1,0:T(8,128)(2,1)S(1)}, u32[]{:S(2)}, u32[]{:S(2)}) collective-permute-start(bf16[2,256,256]{2,1,0:T(8,128)(2,1)S(1)} %pad_maximum_fusion.9), channel_id=1, source_target_pairs={{8,16},{16,8},{24,0},{0,24},{9,17},{17,9},{25,1},{1,25},{10,18},{1... | collective-permute-start | bytes 786440 | tf_op jit(solution)/shard_map/ppermute | solution.py:55
  212.6 10.4 %collective-permute-start.55 = (bf16[1,256,256]{2,1,0:T(8,128)(2,1)S(1)}, bf16[1,256,256]{2,1,0:T(8,128)(2,1)S(1)}, u32[]{:S(2)}, u32[]{:S(2)}) collective-permute-start(bf16[1,256,256]{2,1,0:T(8,128)(2,1)S(1)} %add_convert_fusion.17), channel_id=1, source_target_pairs={{0,8},{8,0},{16,24},{24,16},{1,9},{9,1},{17,25},{25,17},{2,10},{10... | collective-permute-start | bytes 393224 | tf_op jit(solution)/shard_map/ppermute | solution.py:55
  218.1 11.4 %collective-permute-start.49 = (bf16[1,256,256]{2,1,0:T(8,128)(2,1)S(1)}, bf16[1,256,256]{2,1,0:T(8,128)(2,1)S(1)}, u32[]{:S(2)}, u32[]{:S(2)}) collective-permute-start(bf16[1,256,256]{2,1,0:T(8,128)(2,1)S(1)} %add_convert_fusion.19), channel_id=1, source_target_pairs={{8,16},{16,8},{24,0},{0,24},{9,17},{17,9},{25,1},{1,25},{10,18},{1... | collective-permute-start | bytes 393224 | tf_op jit(solution)/shard_map/ppermute | solution.py:55
  223.0 13.9 %collective-permute-start.56 = (bf16[1,256,256]{2,1,0:T(8,128)(2,1)S(1)}, bf16[1,256,256]{2,1,0:T(8,128)(2,1)S(1)}, u32[]{:S(2)}, u32[]{:S(2)}) collective-permute-start(bf16[1,256,256]{2,1,0:T(8,128)(2,1)S(1)} %add_convert_fusion.16), channel_id=1, source_target_pairs={{32,64},{64,32},{96,0},{0,96},{33,65},{65,33},{97,1},{1,97},{34,66... | collective-permute-start | bytes 393224 | tf_op jit(solution)/shard_map/ppermute | solution.py:55
  229.6 9.9 %collective-permute-start.50 = (bf16[1,256,256]{2,1,0:T(8,128)(2,1)S(1)}, bf16[1,256,256]{2,1,0:T(8,128)(2,1)S(1)}, u32[]{:S(2)}, u32[]{:S(2)}) collective-permute-start(bf16[1,256,256]{2,1,0:T(8,128)(2,1)S(1)} %add_convert_fusion.18.refs_4_), channel_id=1, source_target_pairs={{32,64},{64,32},{96,0},{0,96},{33,65},{65,33},{97,1},{1,97},{34,66... | collective-permute-start | bytes 393224 | tf_op jit(solution)/shard_map/ppermute | solution.py:55
  (53 other events, 337.1 us)

commit v4 on v3

--- a/solution.py
+++ b/solution.py
@@ -30,18 +30,18 @@
 
 GATHER_ORDERS = [("z0", "z1"), ("z1", "z0")]
 HALVING = [
-    ("x0", "z0", "z1"),
-    ("y0", "z1", "z0"),
-    ("x0", "z0", "z1"),
-    ("y0", "z1", "z0"),
+    ("z0", "x0", "z1"),
+    ("z1", "y0", "z0"),
     ("x1", "z0", "z1"),
     ("y1", "z1", "z0"),
+    ("z0", "x0", "z1"),
+    ("z1", "y0", "z0"),
 ]
 GROUPS = [
-    ((0, 2), ("x1", "y1", "y0"), "x0"),
-    ((1, 3), ("y1", "x1", "x0"), "y0"),
-    ((4,), ("y0", "x0", "y1"), "x1"),
-    ((5,), ("x0", "y0", "x1"), "y1"),
+    ((0, 4), ("x1", "y1", "y0"), "x0"),
+    ((1, 5), ("y1", "x1", "x0"), "y0"),
+    ((2,), ("y0", "x0", "y1"), "x1"),
+    ((3,), ("x0", "y0", "x1"), "y1"),
 ]
 WIDTH = HEADS_CORE * HDIM
 ROWS = 2 * BLOCK
@@ -360,7 +360,7 @@
         token_copy(i, tokens, held, sems).start()
 
 
-def multiply_blocks(keeps, offset, turned, held, arriving, outs):
+def multiply_blocks(first, keeps, turned, held, arriving, outs):
     def blocks(i, carry):
         if arriving is not None:
             token_copy(i, *arriving).wait()
@@ -368,11 +368,27 @@
         piece = dot(turned[...], held[:, at], 1, 0).astype(BF)
         for part in range(2):
             sent, kept = outs[2 * part], outs[2 * part + 1]
-            first = piece[part * 256 : (part + 1) * 256, :256]
-            second = piece[part * 256 : (part + 1) * 256, 256:]
-            straight = keeps[offset + part] == 0
-            kept[i] = jnp.where(straight, first, second)
-            sent[i] = jnp.where(straight, second, first)
+            even = piece[part * 256 : (part + 1) * 256, :256]
+            odd = piece[part * 256 : (part + 1) * 256, 256:]
+            dim = HALVING[first + part][0]
+            if dim[0] != "z":
+                straight = keeps[part] == 0
+                kept[i] = jnp.where(straight, even, odd)
+                sent[i] = jnp.where(straight, odd, even)
+                continue
+            bits = (i >> 1, i & 1)
+            moves, place = bits[int(dim[1])], 2 * bits[1 - int(dim[1])]
+
+            @pl.when(moves == 1)
+            def _():
+                sent[place] = even
+                sent[place + 1] = odd
+
+            @pl.when(moves == 0)
+            def _():
+                kept[place] = even
+                kept[place + 1] = odd
+
         return carry
 
     lax.fori_loop(0, 4, blocks, 0)
@@ -382,7 +398,7 @@
     fetch_tokens(tokens, held, sems)
     turned[:256, :] = q0[...].T
     turned[256:, :] = q1[...].T
-    multiply_blocks(keeps, 0, turned, held, (tokens, held, sems), (s0, k0, s1, k1))
+    multiply_blocks(0, keeps, turned, held, (tokens, held, sems), (s0, k0, s1, k1))
 
 
 def gradient_kernel(keeps, k0, v0, k1, v1, d0, d1, state, tokens, *refs):
@@ -403,12 +419,12 @@
                     turned[head_cols(head), span] = total.astype(BF).T
 
         arriving = (tokens, held, sems) if kind == 0 else None
-        multiply_blocks(keeps, 2 * kind, turned, held, arriving, outs[4 * kind : 4 * kind + 4])
+        multiply_blocks(2 + 2 * kind, keeps, turned, held, arriving, outs[4 * kind : 4 * kind + 4])
 
 
 def gradient_call(kernel, first, ins, specs, tokens):
     count = len(first)
-    keeps = jnp.stack([colour() ^ place_bit(HALVING[p][0]) for p in first]).astype(jnp.int32)
+    keeps = jnp.stack([colour() ^ place_bit(HALVING[p][0]) for p in (2, 3)]).astype(jnp.int32)
     return pl.pallas_call(
         kernel,
         grid=(1,),
@@ -446,11 +462,15 @@
 def reduce_part(sent, kept, order):
     received = swap(sent, order[0])
     part = add(kept, received).reshape(2, 2, 256, 256)
-    for i, dim in enumerate(order[1:]):
-        axis = int(dim[1]) if i == 0 else 0
-        send = lax.index_in_dim(part, 1, axis, False)
-        part = add(lax.index_in_dim(part, 0, axis, False), swap(send, dim))
-    return part
+    if order[0][0] == "z":
+        keeps = colour() ^ place_bit(order[1])
+        send = lax.dynamic_index_in_dim(part, 1 - keeps, 1, False)
+        keep = lax.dynamic_index_in_dim(part, keeps, 1, False)
+    else:
+        send = lax.index_in_dim(part, 1, int(order[1][1]), False)
+        keep = lax.index_in_dim(part, 0, int(order[1][1]), False)
+    part = add(keep, swap(send, order[1]))
+    return add(part[0], swap(part[1], order[2]))
 
 
 def finish_group(parts, exchanged, last):
@@ -515,21 +535,37 @@
     )(core.reshape(1), own, other)
 
 
-def adam(core, kept, received, weights, first, second):
-    pieces = []
-    for kind in range(3):
-        at = slice(kind * WIDTH, (kind + 1) * WIDTH)
-        pieces.append(jnp.where(core == 0, kept[:, at], received[:, at]))
-        pieces.append(jnp.where(core == 0, received[:, at], kept[:, at]))
-    gradient = jnp.concatenate(pieces, 1).astype(F32)
-    new_first = BETA_ONE * first + (1.0 - BETA_ONE) * gradient
-    new_second = BETA_TWO * second + (1.0 - BETA_TWO) * gradient * gradient
-    first_hat = new_first * (1.0 / (1.0 - BETA_ONE**STEP))
-    second_hat = new_second * (1.0 / (1.0 - BETA_TWO**STEP))
-    new_weights = weights - LEARN_RATE * (
-        first_hat / (jnp.sqrt(second_hat) + EPS_ADAM) + DECAY_WEIGHT * weights
-    )
-    return new_weights, new_first, new_second
+def adam_kernel(core, kept, received, weights, first, second, out_weights, out_first, out_second):
+    for block in range(6):
+        at = slice(block * WIDTH, (block + 1) * WIDTH)
+        source = slice((block // 2) * WIDTH, (block // 2 + 1) * WIDTH)
+        gradient = jnp.where(block % 2 == core[0], kept[:, source], received[:, source]).astype(F32)
+        new_first = BETA_ONE * first[:, at] + (1.0 - BETA_ONE) * gradient
+        new_second = BETA_TWO * second[:, at] + (1.0 - BETA_TWO) * gradient * gradient
+        first_hat = new_first * (1.0 / (1.0 - BETA_ONE**STEP))
+        second_hat = new_second * (1.0 / (1.0 - BETA_TWO**STEP))
+        root = second_hat * lax.rsqrt(second_hat)
+        out_first[:, at] = new_first
+        out_second[:, at] = new_second
+        out_weights[:, at] = weights[:, at] - LEARN_RATE * (
+            first_hat * pl.reciprocal(root + EPS_ADAM) + DECAY_WEIGHT * weights[:, at]
+        )
+
+
+def adam(core, kept, received, *arrays):
+    piece = pl.BlockSpec((32, 3 * WIDTH), lambda i, c: (i, 0))
+    block = pl.BlockSpec((32, 6 * WIDTH), lambda i, c: (i, 0))
+    return pl.pallas_call(
+        adam_kernel,
+        name="adam",
+        grid_spec=pltpu.PrefetchScalarGridSpec(
+            num_scalar_prefetch=1,
+            grid=(8,),
+            in_specs=[piece, piece, block, block, block],
+            out_specs=(block,) * 3,
+        ),
+        out_shape=tuple(shape(x.shape, F32) for x in arrays),
+    )(core.reshape(1), kept, received, *arrays)
 
 
 def gather_step(step, mine):

time: 268 us -> 255 us (0.951)
  waiting for transfers between devices: 86.5 us -> 70.7 us
  other arithmetic: 20.4 us -> 8.38 us
  Pallas kernels: 63.3 us -> 74.2 us
    ppermute x54, waiting for transfers between devices: 70 us -> 54.4 us  [swap(): return lax.ppermute(x, dim[0], PAIRS[dim[1]])]
    pallas_call x0 -> x1, Pallas kernels: none -> 9.82 us  [adam(): pl.pallas_call(adam_kernel, name='adam', grid_spec=pltpu.PrefetchScalarGr...]
    sub x1 -> x0, other arithmetic: 5.91 us -> none  [adam(): weights - LEARN_RATE * (first_hat / (jnp.sqrt(second_hat) + EPS_ADAM) + D...]
    unnamed x5 -> x0, other arithmetic: 5.49 us -> none
    unnamed x75 -> x73, local copies, waits for them, and re-layouts: 3.84 us -> 5.5 us
  transfers between devices with their start and end apart: 61 -> 61, of which waited for: 27 -> 35; matrix products, arithmetic and copies ran while one was open for 5% -> 6% of each run, Pallas kernels for 15% -> 16%
where the time goes in v4:
time: 255 us; the launch traced here: 252 us
  starting transfers between devices  81.7 us (32%)
  Pallas kernels  74.2 us (29%)
  waiting for transfers between devices  70.7 us (28%)
  matrix products  9 us (4%)
  other arithmetic  8.38 us (3%)
  local copies, waits for them, and re-layouts  6.9 us (3%)
    ppermute x54, starting transfers between devices, swap(): return lax.ppermute(x, dim[0], PAIRS[dim[1]])  72.9 us
    ppermute x54, waiting for transfers between devices, swap(): return lax.ppermute(x, dim[0], PAIRS[dim[1]])  54.4 us
    pallas_call x2, Pallas kernels, gradient_call(): pl.pallas_call(kernel, grid=(1,), in_specs=[pl.BlockSpec(memory_space=plt...  20.3 us
    pallas_call x2, Pallas kernels, backward(): pl.pallas_call(backward_kernel, name='backward', grid_spec=pltpu.Prefetch...  10.8 us
    all_to_all x1, waiting for transfers between devices, earlier_states(): received = lax.all_to_all(cut, ('x', 'y'), 0, 0, tiled=True)  9.99 us
    pallas_call x1, Pallas kernels, adam(): pl.pallas_call(adam_kernel, name='adam', grid_spec=pltpu.PrefetchScalarGr...  9.82 us
    dot_general x2, matrix products, project(): return jnp.dot(tokens, weights, preferred_element_type=F32).astype(BF)  9 us
    pallas_call x1, Pallas kernels, arrange(): pl.pallas_call(arrange_kernel, name='arrange', grid_spec=pltpu.PrefetchSc...  7.34 us
  transfers between devices with their start and end apart: 61, of which 35 were waited for; matrix products, arithmetic and copies ran while one was open for 6% of the time, Pallas kernels for 16%

profile of v4, /device:TPU:0, one launch (start us, length us, event | category | flops | bytes accessed | tf_op | source)
XLA Modules:
  0.0 252.5 jit_solution(12270519595034046280)
XLA Ops:
  0.6 3.1 %prepare.1 = (bf16[4,256,384]{2,1,0:T(8,128)(2,1)}, bf16[4,256,384]{2,1,0:T(8,128)(2,1)}, bf16[512,512]{1,0:T(8,128)(2,1)}) custom-call(s32[1]{0:T(128)} %bitcast.core, f32[256,3072]{1,0:T(8,128)} %weights.1, f32[256,3072]{1,0:T(8,128)} %weights.1, f32[256,3072]{1,0:T(8,128)} %weights.1, f32[256,3072]{1,0:T(8,128)} %weights.1, f32[256,3072]{1,0:T(8,128)} %weights.1, ...), custom_call_target="tpu_custom_call" | custom-call | tf_op jit(solution)/shard_map/prepare/pallas_call | solution.py:119
  9.7 2.5 collective-permute-start.3
  13.8 3.9 %collective-permute-start.2 = (bf16[2,256,384]{2,1,0:T(8,128)(2,1)S(1)}, bf16[2,256,384]{2,1,0:T(8,128)(2,1)}, u32[]{:S(2)}, u32[]{:S(2)}) collective-permute-start(bf16[2,256,384]{2,1,0:T(8,128)(2,1)S(1)} %pad_maximum_fusion.4), channel_id=1, source_target_pairs={{2,4},{4,2},{6,0},{0,6},{3,5},{5,3},{7,1},{1,7},{10,12},{12,10},{1... | collective-permute-start | bytes 1179656 | tf_op jit(solution)/shard_map/ppermute | solution.py:55
  18.5 6.7 %collective-permute-done.2 = bf16[2,256,384]{2,1,0:T(8,128)(2,1)} collective-permute-done((bf16[2,256,384]{2,1,0:T(8,128)(2,1)S(1)}, bf16[2,256,384]{2,1,0:T(8,128)(2,1)}, u32[]{:S(2)}, u32[]{:S(2)}) %collective-permute-start.2) | collective-permute-done | bytes 393248 | tf_op jit(solution)/shard_map/ppermute | solution.py:55
  28.0 7.3 %arrange.1.tokens = bf16[1024,2048]{1,0:T(8,128)(2,1)} custom-call(s32[8]{0:T(128)} %stack.82.blocks, bf16[512,2048]{1,0:T(8,128)(2,1)} %bitcast.10.own, bf16[512,2048]{1,0:T(8,128)(2,1)} %collective-permute-done.5.other), custom_call_target="tpu_custom_call" | custom-call | tf_op jit(solution)/shard_map/arrange/pallas_call | solution.py:140
  35.7 2.3 collective-permute-start.8
  38.1 4.5 %collective-permute-start.12 = (bf16[2,256,384]{2,1,0:T(8,128)(2,1)S(1)}, bf16[2,256,384]{2,1,0:T(8,128)(2,1)S(1)}, u32[]{:S(2)}, u32[]{:S(2)}) collective-permute-start(bf16[2,256,384]{2,1,0:T(8,128)(2,1)S(1)} %get-tuple-element.105), channel_id=1, source_target_pairs={{0,8},{8,0},{16,24},{24,16},{1,9},{9,1},{17,25},{25,17},{2,10},{10... | collective-permute-start | bytes 1179656 | tf_op jit(solution)/shard_map/ppermute | solution.py:55
  54.5 2.6 %collective-permute-done.11 = bf16[2,256,384]{2,1,0:T(8,128)(2,1)S(1)} collective-permute-done((bf16[2,256,384]{2,1,0:T(8,128)(2,1)S(1)}, bf16[2,256,384]{2,1,0:T(8,128)(2,1)S(1)}, u32[]{:S(2)}, u32[]{:S(2)}) %collective-permute-start.11) | collective-permute-done | bytes 393248 | tf_op jit(solution)/shard_map/ppermute | solution.py:55
  57.3 4.5 %fusion.11.first.k0.v0.qkv = bf16[1024,768]{1,0:T(8,128)(2,1)} fusion(bf16[1024,2048]{1,0:T(8,128)(2,1)S(1)} %copy-done, bf16[2048,384]{1,0:T(8,128)(2,1)S(1)} %fusion.40, bf16[2048,384]{1,0:T(8,128)(2,1)S(1)} %fusion.44), kind=kOutput, calls=%fused_computation.9 | convolution fusion | flops 3228303360 | bytes 8912896 | tf_op jit(solution)/shard_map/dot_general | solution.py:184
  68.4 2.5 collective-permute-done.16
  73.1 2.3 collective-permute-done.15
  75.6 4.5 %fusion.8.second.k1.v1.qkv = bf16[1024,768]{1,0:T(8,128)(2,1)} fusion(bf16[1024,2048]{1,0:T(8,128)(2,1)S(1)} %copy-done, bf16[2048,384]{1,0:T(8,128)(2,1)S(1)} %fusion.32, bf16[2048,384]{1,0:T(8,128)(2,1)S(1)} %fusion.36), kind=kOutput, calls=%fused_computation.8 | convolution fusion | flops 3228303360 | bytes 8912896 | tf_op jit(solution)/shard_map/dot_general | solution.py:184
  80.1 2.7 %outer.1 = f32[4,2,128,128]{3,2,1,0:T(8,128)} custom-call(bf16[1024,768]{1,0:T(8,128)(2,1)} %fusion.11.first.k0.v0.qkv, bf16[1024,768]{1,0:T(8,128)(2,1)} %fusion.11.first.k0.v0.qkv, bf16[1024,768]{1,0:T(8,128)(2,1)} %fusion.8.second.k1.v1.qkv, bf16[1024,768]{1,0:T(8,128)(2,1)} %fusion.8.second.k1.v1.qkv), custom_call_target="tpu_custom_call" | custom-call | tf_op jit(solution)/shard_map/outer/pallas_call | solution.py:162
  82.8 4.0 %all-to-all-start = ((f32[16,64,128]{2,1,0:T(8,128)}), f32[16,64,128]{2,1,0:T(8,128)S(1)}, u32[]{:S(2)}, u32[]{:S(2)}) async-start(f32[16,64,128]{2,1,0:T(8,128)} %bitcast.230), calls=%async_computation | async-start | bytes 1048576 | tf_op jit(solution)/shard_map/all_to_all | solution.py:213
  86.9 10.0 %all-to-all-done.received = f32[16,64,128]{2,1,0:T(8,128)S(1)} async-done(((f32[16,64,128]{2,1,0:T(8,128)}), f32[16,64,128]{2,1,0:T(8,128)S(1)}, u32[]{:S(2)}, u32[]{:S(2)}) %all-to-all-start) | async-done | bytes 524320 | tf_op jit(solution)/shard_map/all_to_all | solution.py:213
  99.5 3.7 %all-to-all-start.1 = ((bf16[16,64,128]{2,1,0:T(8,128)(2,1)}), bf16[16,64,128]{2,1,0:T(8,128)(2,1)S(1)}, u32[]{:S(2)}, u32[]{:S(2)}) async-start(bf16[16,64,128]{2,1,0:T(8,128)(2,1)} %running.1), calls=%async_computation.1 | async-start | bytes 524288 | tf_op jit(solution)/shard_map/all_to_all | solution.py:221
  103.2 6.5 %within.1 = f32[1024,512]{1,0:T(8,128)} custom-call(bf16[1024,768]{1,0:T(8,128)(2,1)} %fusion.11.first.k0.v0.qkv, bf16[1024,768]{1,0:T(8,128)(2,1)} %fusion.8.second.k1.v1.qkv), custom_call_target="tpu_custom_call" | custom-call | tf_op jit(solution)/shard_map/within/pallas_call | solution.py:265
  112.2 6.9 %forward.1 = (bf16[1024,512]{1,0:T(8,128)(2,1)}, bf16[1024,512]{1,0:T(8,128)(2,1)}, bf16[4,2,128,128]{3,2,1,0:T(8,128)(2,1)}) custom-call(s32[1]{0:T(128)} %bitcast.core, bf16[1024,768]{1,0:T(8,128)(2,1)} %fusion.11.first.k0.v0.qkv, bf16[1024,768]{1,0:T(8,128)(2,1)} %fusion.8.second.k1.v1.qkv, f32[1024,512]{1,0:T(8,128)} %within.1, ...), custom_call_target="tpu_custom_call" | custom-call | tf_op jit(solution)/shard_map/forward/pallas_call | solution.py:297
  119.6 5.4 %backward.2 = (bf16[1024,256]{1,0:T(8,128)(2,1)}, f32[2,1024,256]{2,1,0:T(8,128)}) custom-call(s32[1]{0:T(128)} %constant.44.clone.1.pair, bf16[1024,768]{1,0:T(8,128)(2,1)} %fusion.11.first.k0.v0.qkv, bf16[1024,512]{1,0:T(8,128)(2,1)} %get-tuple-element.68.grad, bf16[4,2,128,128]{3,2,1,0:T(8,128)(2,1)} %bitcast.216), custom_call_target="tpu_custom_call" | custom-call | tf_op jit(solution)/shard_map/backward/pallas_call | solution.py:333
  127.2 5.4 %backward.3 = (bf16[1024,256]{1,0:T(8,128)(2,1)}, f32[2,1024,256]{2,1,0:T(8,128)}) custom-call(s32[1]{0:T(128)} %constant.45.clone.1.pair, bf16[1024,768]{1,0:T(8,128)(2,1)} %fusion.8.second.k1.v1.qkv, bf16[1024,512]{1,0:T(8,128)(2,1)} %get-tuple-element.68.grad, bf16[4,2,128,128]{3,2,1,0:T(8,128)(2,1)} %bitcast.217), custom_call_target="tpu_custom_call" | custom-call | tf_op jit(solution)/shard_map/backward/pallas_call | solution.py:333
  134.9 6.9 %shard_map.84 = (bf16[4,256,256]{2,1,0:T(8,128)(2,1)}, bf16[4,256,256]{2,1,0:T(8,128)(2,1)}, bf16[4,256,256]{2,1,0:T(8,128)(2,1)}, bf16[4,256,256]{2,1,0:T(8,128)(2,1)}) custom-call(s32[2]{0:T(128)} %pad_add_fusion.keeps, bf16[1024,256]{1,0:T(8,128)(2,1)} %get-tuple-element.72.q0, bf16[1024,256]{1,0:T(8,128)(2,1)} %get-tuple-element.73.q1, ...), custom_call_target="tpu_custom_call" | custom-call | tf_op jit(solution)/shard_map/pallas_call | solution.py:428
  146.6 3.9 %collective-permute-done.26 = bf16[4,2,128,128]{3,2,1,0:T(8,128)(2,1)S(1)} collective-permute-done((bf16[4,2,128,128]{3,2,1,0:T(8,128)(2,1)S(1)}, bf16[4,2,128,128]{3,2,1,0:T(8,128)(2,1)S(1)}, u32[]{:S(2)}, u32[]{:S(2)}) %collective-permute-start.26) | collective-permute-done | bytes 262176 | tf_op jit(solution)/shard_map/ppermute | solution.py:55
  151.4 13.3 %shard_map.85 = (bf16[4,256,256]{2,1,0:T(8,128)(2,1)}, bf16[4,256,256]{2,1,0:T(8,128)(2,1)}, bf16[4,256,256]{2,1,0:T(8,128)(2,1)}, bf16[4,256,256]{2,1,0:T(8,128...) custom-call(s32[2]{0:T(128)} %pad_add_fusion.keeps, ...), custom_call_target="tpu_custom_call" | custom-call | tf_op jit(solution)/shard_map/pallas_call | solution.py:428
  172.3 3.2 %collective-permute-done.27 = bf16[4,256,256]{2,1,0:T(8,128)(2,1)S(1)} collective-permute-done((bf16[4,256,256]{2,1,0:T(8,128)(2,1)}, bf16[4,256,256]{2,1,0:T(8,128)(2,1)S(1)}, u32[]{:S(2)}, u32[]{:S(2)}) %collective-permute-start.27) | collective-permute-done | bytes 524320 | tf_op jit(solution)/shard_map/ppermute | solution.py:55
  175.7 2.8 %collective-permute-done.24 = bf16[2,256,256]{2,1,0:T(8,128)(2,1)S(1)} collective-permute-done((bf16[2,256,256]{2,1,0:T(8,128)(2,1)S(1)}, bf16[2,256,256]{2,1,0:T(8,128)(2,1)S(1)}, u32[]{:S(2)}, u32[]{:S(2)}) %collective-permute-start.24) | collective-permute-done | bytes 262176 | tf_op jit(solution)/shard_map/ppermute | solution.py:55
  196.6 2.7 %collective-permute-start.40 = (bf16[2,256,256]{2,1,0:T(8,128)(2,1)S(1)}, bf16[2,256,256]{2,1,0:T(8,128)(2,1)S(1)}, u32[]{:S(2)}, u32[]{:S(2)}) collective-permute-start(bf16[2,256,256]{2,1,0:T(8,128)(2,1)S(1)} %pad_maximum_fusion.9), channel_id=1, source_target_pairs={{8,16},{16,8},{24,0},{0,24},{9,17},{17,9},{25,1},{1,25},{10,18},{1... | collective-permute-start | bytes 786440 | tf_op jit(solution)/shard_map/ppermute | solution.py:55
  201.0 4.6 %collective-permute-done.47 = bf16[1,256,256]{2,1,0:T(8,128)(2,1)S(1)} collective-permute-done((bf16[1,256,256]{2,1,0:T(8,128)(2,1)S(1)}, bf16[1,256,256]{2,1,0:T(8,128)(2,1)S(1)}, u32[]{:S(2)}, u32[]{:S(2)}) %collective-permute-start.47) | collective-permute-done | bytes 131104 | tf_op jit(solution)/shard_map/ppermute | solution.py:55
  219.8 2.9 %collective-permute-done.32 = bf16[2,256,256]{2,1,0:T(8,128)(2,1)S(1)} collective-permute-done((bf16[2,256,256]{2,1,0:T(8,128)(2,1)S(1)}, bf16[2,256,256]{2,1,0:T(8,128)(2,1)S(1)}, u32[]{:S(2)}, u32[]{:S(2)}) %collective-permute-start.32) | collective-permute-done | bytes 262176 | tf_op jit(solution)/shard_map/ppermute | solution.py:55
  227.4 4.0 %collective-permute-done.57.refs_7_ = bf16[1,256,256]{2,1,0:T(8,128)(2,1)S(1)} collective-permute-done((bf16[1,256,256]{2,1,0:T(8,128)(2,1)S(1)}, bf16[1,256,256]{2,1,0:T(8,128)(2,1)S(1)}, u32[]{:S(2)}, u32[]{:S(2)}) %collective-permute-start.57) | collective-permute-done | bytes 131104 | tf_op jit(solution)/shard_map/ppermute | solution.py:55
  232.8 2.9 %sort_pieces.1 = (bf16[256,1536]{1,0:T(8,128)(2,1)}, bf16[256,1536]{1,0:T(8,128)(2,1)}) custom-call(s32[4]{0:T(128)} %add_convert_fusion.19.holds, bf16[2,256,256]{2,1,0:T(8,128)(2,1)} %copy-done.5, bf16[2,256,256]{2,1,0:T(8,128)(2,1)} %copy-done.18, bf16[2,256,256]{2,1,0:T(8,128)(2,1)} %copy-done.6, bf16[2,256,256]{2,1,0:T(8,128)(2,1)} %copy-done.19, ...), custom_call_target="tpu_custom_call" | custom-call | tf_op jit(solution)/shard_map/sort_pieces/pallas_call | solution.py:508
  236.3 2.6 %collective-permute-done.19.other = bf16[512,512]{1,0:T(8,128)(2,1)S(1)} collective-permute-done((bf16[512,512]{1,0:T(8,128)(2,1)S(1)}, bf16[512,512]{1,0:T(8,128)(2,1)S(1)}, u32[]{:S(2)}, u32[]{:S(2)}) %collective-permute-start.19) | collective-permute-done | bytes 524320 | tf_op jit(solution)/shard_map/ppermute | solution.py:54
  242.7 9.8 %adam.1 = (f32[256,3072]{1,0:T(8,128)}, f32[256,3072]{1,0:T(8,128)}, f32[256,3072]{1,0:T(8,128)}) custom-call(s32[1]{0:T(128)} %bitcast.core, bf16[256,1536]{1,0:T(8,128)(2,1)} %get-tuple-element.93.kept, bf16[256,1536]{1,0:T(8,128)(2,1)} %copy-done.7, f32[256,3072]{1,0:T(8,128)} %weights.1, f32[256,3072]{1,0:T(8,128)} %first.1, f32[256,3072]{1,0:T(8,128)} %second.1), custom_call_target="tpu_custom_call" | custom-call | tf_op jit(solution)/shard_map/adam/pallas_call | solution.py:558
  (249 shorter events, 99.9 us)
Async XLA Ops:
  3.8 24.2 %collective-permute-start.5 = (bf16[512,2048]{1,0:T(8,128)(2,1)}, bf16[512,2048]{1,0:T(8,128)(2,1)}, u32[]{:S(2)}, u32[]{:S(2)}) collective-permute-start(bf16[512,2048]{1,0:T(8,128)(2,1)} %bitcast.10.own), channel_id=1, source_target_pairs={{0,1},{1,0},{2,3},{3,2},{4,5},{5,4},{6,7},{7,6},{8,9},{9,8},{10,11... | collective-permute-start | bytes 6291464 | tf_op jit(solution)/shard_map/ppermute | solution.py:54
  13.8 11.5 %collective-permute-start.2 = (bf16[2,256,384]{2,1,0:T(8,128)(2,1)S(1)}, bf16[2,256,384]{2,1,0:T(8,128)(2,1)}, u32[]{:S(2)}, u32[]{:S(2)}) collective-permute-start(bf16[2,256,384]{2,1,0:T(8,128)(2,1)S(1)} %pad_maximum_fusion.4), channel_id=1, source_target_pairs={{2,4},{4,2},{6,0},{0,6},{3,5},{5,3},{7,1},{1,7},{10,12},{12,10},{1... | collective-permute-start | bytes 1179656 | tf_op jit(solution)/shard_map/ppermute | solution.py:55
  17.8 9.1 %collective-permute-start.4 = (bf16[2,256,384]{2,1,0:T(8,128)(2,1)S(1)}, bf16[2,256,384]{2,1,0:T(8,128)(2,1)}, u32[]{:S(2)}, u32[]{:S(2)}) collective-permute-start(bf16[2,256,384]{2,1,0:T(8,128)(2,1)S(1)} %pad_maximum_fusion.5), channel_id=1, source_target_pairs={{0,2},{2,0},{4,6},{6,4},{1,3},{3,1},{5,7},{7,5},{8,10},{10,8},{12,... | collective-permute-start | bytes 1179656 | tf_op jit(solution)/shard_map/ppermute | solution.py:55
  35.4 11.1 %collective-permute-start.6 = (bf16[1,256,384]{2,1,0:T(8,128)(2,1)S(1)}, bf16[1,256,384]{2,1,0:T(8,128)(2,1)S(1)}, u32[]{:S(2)}, u32[]{:S(2)}) collective-permute-start(bf16[1,256,384]{2,1,0:T(8,128)(2,1)S(1)} %get-tuple-element.107), channel_id=1, source_target_pairs={{0,2},{2,0},{4,6},{6,4},{1,3},{3,1},{5,7},{7,5},{8,10},{10,8},{12,... | collective-permute-start | bytes 589832 | tf_op jit(solution)/shard_map/ppermute | solution.py:55
  35.7 12.1 %collective-permute-start.8 = (bf16[1,256,384]{2,1,0:T(8,128)(2,1)S(1)}, bf16[1,256,384]{2,1,0:T(8,128)(2,1)S(1)}, u32[]{:S(2)}, u32[]{:S(2)}) collective-permute-start(bf16[1,256,384]{2,1,0:T(8,128)(2,1)S(1)} %get-tuple-element.106), channel_id=1, source_target_pairs={{2,4},{4,2},{6,0},{0,6},{3,5},{5,3},{7,1},{1,7},{10,12},{12,10},{1... | collective-permute-start | bytes 589832 | tf_op jit(solution)/shard_map/ppermute | solution.py:55
  38.1 13.0 %collective-permute-start.12 = (bf16[2,256,384]{2,1,0:T(8,128)(2,1)S(1)}, bf16[2,256,384]{2,1,0:T(8,128)(2,1)S(1)}, u32[]{:S(2)}, u32[]{:S(2)}) collective-permute-start(bf16[2,256,384]{2,1,0:T(8,128)(2,1)S(1)} %get-tuple-element.105), channel_id=1, source_target_pairs={{0,8},{8,0},{16,24},{24,16},{1,9},{9,1},{17,25},{25,17},{2,10},{10... | collective-permute-start | bytes 1179656 | tf_op jit(solution)/shard_map/ppermute | solution.py:55
  42.7 11.3 %collective-permute-start.13 = (bf16[2,256,384]{2,1,0:T(8,128)(2,1)S(1)}, bf16[2,256,384]{2,1,0:T(8,128)(2,1)S(1)}, u32[]{:S(2)}, u32[]{:S(2)}) collective-permute-start(bf16[2,256,384]{2,1,0:T(8,128)(2,1)S(1)} %get-tuple-element.104), channel_id=1, source_target_pairs={{8,16},{16,8},{24,0},{0,24},{9,17},{17,9},{25,1},{1,25},{10,18},{1... | collective-permute-start | bytes 1179656 | tf_op jit(solution)/shard_map/ppermute | solution.py:55
  44.2 10.2 %collective-permute-start.10 = (bf16[2,256,384]{2,1,0:T(8,128)(2,1)S(1)}, bf16[2,256,384]{2,1,0:T(8,128)(2,1)S(1)}, u32[]{:S(2)}, u32[]{:S(2)}) collective-permute-start(bf16[2,256,384]{2,1,0:T(8,128)(2,1)S(1)} %get-tuple-element.103), channel_id=1, source_target_pairs={{0,32},{32,0},{64,96},{96,64},{1,33},{33,1},{65,97},{97,65},{2,34}... | collective-permute-start | bytes 1179656 | tf_op jit(solution)/shard_map/ppermute | solution.py:55
  46.4 10.7 %collective-permute-start.11 = (bf16[2,256,384]{2,1,0:T(8,128)(2,1)S(1)}, bf16[2,256,384]{2,1,0:T(8,128)(2,1)S(1)}, u32[]{:S(2)}, u32[]{:S(2)}) collective-permute-start(bf16[2,256,384]{2,1,0:T(8,128)(2,1)S(1)} %get-tuple-element.102), channel_id=1, source_target_pairs={{32,64},{64,32},{96,0},{0,96},{33,65},{65,33},{97,1},{1,97},{34,66... | collective-permute-start | bytes 1179656 | tf_op jit(solution)/shard_map/ppermute | solution.py:55
  47.9 14.0 %collective-permute-start.7 = (bf16[2,256,384]{2,1,0:T(8,128)(2,1)S(1)}, bf16[2,256,384]{2,1,0:T(8,128)(2,1)S(1)}, u32[]{:S(2)}, u32[]{:S(2)}) collective-permute-start(bf16[2,256,384]{2,1,0:T(8,128)(2,1)S(1)} %pad_maximum_fusion.6), channel_id=1, source_target_pairs={{2,4},{4,2},{6,0},{0,6},{3,5},{5,3},{7,1},{1,7},{10,12},{12,10},{1... | collective-permute-start | bytes 1179656 | tf_op jit(solution)/shard_map/ppermute | solution.py:55
  51.1 10.8 %collective-permute-start.9 = (bf16[2,256,384]{2,1,0:T(8,128)(2,1)S(1)}, bf16[2,256,384]{2,1,0:T(8,128)(2,1)S(1)}, u32[]{:S(2)}, u32[]{:S(2)}) collective-permute-start(bf16[2,256,384]{2,1,0:T(8,128)(2,1)S(1)} %pad_maximum_fusion.7), channel_id=1, source_target_pairs={{0,2},{2,0},{4,6},{6,4},{1,3},{3,1},{5,7},{7,5},{8,10},{10,8},{12,... | collective-permute-start | bytes 1179656 | tf_op jit(solution)/shard_map/ppermute | solution.py:55
  62.1 8.7 %collective-permute-start.16 = (bf16[2,256,384]{2,1,0:T(8,128)(2,1)S(1)}, bf16[2,256,384]{2,1,0:T(8,128)(2,1)S(1)}, u32[]{:S(2)}, u32[]{:S(2)}) collective-permute-start(bf16[2,256,384]{2,1,0:T(8,128)(2,1)S(1)} %get-tuple-element.101), channel_id=1, source_target_pairs={{0,8},{8,0},{16,24},{24,16},{1,9},{9,1},{17,25},{25,17},{2,10},{10... | collective-permute-start | bytes 1179656 | tf_op jit(solution)/shard_map/ppermute | solution.py:55
  62.5 9.6 %collective-permute-start.17 = (bf16[2,256,384]{2,1,0:T(8,128)(2,1)S(1)}, bf16[2,256,384]{2,1,0:T(8,128)(2,1)S(1)}, u32[]{:S(2)}, u32[]{:S(2)}) collective-permute-start(bf16[2,256,384]{2,1,0:T(8,128)(2,1)S(1)} %get-tuple-element.100), channel_id=1, source_target_pairs={{8,16},{16,8},{24,0},{0,24},{9,17},{17,9},{25,1},{1,25},{10,18},{1... | collective-permute-start | bytes 1179656 | tf_op jit(solution)/shard_map/ppermute | solution.py:55
  64.6 8.4 %collective-permute-start.14 = (bf16[2,256,384]{2,1,0:T(8,128)(2,1)S(1)}, bf16[2,256,384]{2,1,0:T(8,128)(2,1)S(1)}, u32[]{:S(2)}, u32[]{:S(2)}) collective-permute-start(bf16[2,256,384]{2,1,0:T(8,128)(2,1)S(1)} %get-tuple-element.99), channel_id=1, source_target_pairs={{0,32},{32,0},{64,96},{96,64},{1,33},{33,1},{65,97},{97,65},{2,34}... | collective-permute-start | bytes 1179656 | tf_op jit(solution)/shard_map/ppermute | solution.py:55
  66.4 9.0 %collective-permute-start.15 = (bf16[2,256,384]{2,1,0:T(8,128)(2,1)S(1)}, bf16[2,256,384]{2,1,0:T(8,128)(2,1)S(1)}, u32[]{:S(2)}, u32[]{:S(2)}) collective-permute-start(bf16[2,256,384]{2,1,0:T(8,128)(2,1)S(1)} %get-tuple-element.98), channel_id=1, source_target_pairs={{32,64},{64,32},{96,0},{0,96},{33,65},{65,33},{97,1},{1,97},{34,66... | collective-permute-start | bytes 1179656 | tf_op jit(solution)/shard_map/ppermute | solution.py:55
  82.8 14.1 %all-to-all-start = ((f32[16,64,128]{2,1,0:T(8,128)}), f32[16,64,128]{2,1,0:T(8,128)S(1)}, u32[]{:S(2)}, u32[]{:S(2)}) async-start(f32[16,64,128]{2,1,0:T(8,128)} %bitcast.230), calls=%async_computation | async-start | bytes 1048576 | tf_op jit(solution)/shard_map/all_to_all | solution.py:213
  86.8 22.9 %collective-permute-start.18 = (bf16[512,512]{1,0:T(8,128)(2,1)S(1)}, bf16[512,512]{1,0:T(8,128)(2,1)S(1)}, u32[]{:S(2)}, u32[]{:S(2)}) collective-permute-start(bf16[512,512]{1,0:T(8,128)(2,1)S(1)} %copy-done.22), channel_id=1, source_target_pairs={{0,1},{1,0},{2,3},{3,2},{4,5},{5,4},{6,7},{7,6},{8,9},{9,8},{10,11... | collective-permute-start | bytes 1572872 | tf_op jit(solution)/shard_map/ppermute | solution.py:54
  99.5 12.0 %all-to-all-start.1 = ((bf16[16,64,128]{2,1,0:T(8,128)(2,1)}), bf16[16,64,128]{2,1,0:T(8,128)(2,1)S(1)}, u32[]{:S(2)}, u32[]{:S(2)}) async-start(bf16[16,64,128]{2,1,0:T(8,128)(2,1)} %running.1), calls=%async_computation.1 | async-start | bytes 524288 | tf_op jit(solution)/shard_map/all_to_all | solution.py:221
  133.6 8.3 %collective-permute-start.22 = (bf16[4,2,128,128]{3,2,1,0:T(8,128)(2,1)S(1)}, bf16[4,2,128,128]{3,2,1,0:T(8,128)(2,1)S(1)}, u32[]{:S(2)}, u32[]{:S(2)}) collective-permute-start(bf16[4,2,128,128]{3,2,1,0:T(8,128)(2,1)S(1)} %fusion.25), channel_id=1, source_target_pairs={{0,32},{32,0},{64,96},{96,64},{1,33},{33,1},{65,97},{97,65},{2,34}... | collective-permute-start | bytes 786440 | tf_op jit(solution)/shard_map/ppermute | solution.py:55
  141.8 27.8 %collective-permute-start.23 = (bf16[4,256,256]{2,1,0:T(8,128)(2,1)}, bf16[4,256,256]{2,1,0:T(8,128)(2,1)S(1)}, u32[]{:S(2)}, u32[]{:S(2)}) collective-permute-start(bf16[4,256,256]{2,1,0:T(8,128)(2,1)} %get-tuple-element.79), channel_id=1, source_target_pairs={{0,2},{2,0},{4,6},{6,4},{1,3},{3,1},{5,7},{7,5},{8,10},{10,8},{12,... | collective-permute-start | bytes 1572872 | tf_op jit(solution)/shard_map/ppermute | solution.py:55
  145.0 27.0 %collective-permute-start.34 = (bf16[4,256,256]{2,1,0:T(8,128)(2,1)}, bf16[4,256,256]{2,1,0:T(8,128)(2,1)S(1)}, u32[]{:S(2)}, u32[]{:S(2)}) collective-permute-start(bf16[4,256,256]{2,1,0:T(8,128)(2,1)} %get-tuple-element.86), channel_id=1, source_target_pairs={{2,4},{4,2},{6,0},{0,6},{3,5},{5,3},{7,1},{1,7},{10,12},{12,10},{1... | collective-permute-start | bytes 1572872 | tf_op jit(solution)/shard_map/ppermute | solution.py:55
  164.7 10.8 %collective-permute-start.27 = (bf16[4,256,256]{2,1,0:T(8,128)(2,1)}, bf16[4,256,256]{2,1,0:T(8,128)(2,1)S(1)}, u32[]{:S(2)}, u32[]{:S(2)}) collective-permute-start(bf16[4,256,256]{2,1,0:T(8,128)(2,1)} %get-tuple-element.84), channel_id=1, source_target_pairs={{0,2},{2,0},{4,6},{6,4},{1,3},{3,1},{5,7},{7,5},{8,10},{10,8},{12,... | collective-permute-start | bytes 1572872 | tf_op jit(solution)/shard_map/ppermute | solution.py:55
  166.1 12.5 %collective-permute-start.37 = (bf16[4,256,256]{2,1,0:T(8,128)(2,1)}, bf16[4,256,256]{2,1,0:T(8,128)(2,1)S(1)}, u32[]{:S(2)}, u32[]{:S(2)}) collective-permute-start(bf16[4,256,256]{2,1,0:T(8,128)(2,1)} %get-tuple-element.88), channel_id=1, source_target_pairs={{2,4},{4,2},{6,0},{0,6},{3,5},{5,3},{7,1},{1,7},{10,12},{12,10},{1... | collective-permute-start | bytes 1572872 | tf_op jit(solution)/shard_map/ppermute | solution.py:55
  167.6 14.4 %collective-permute-start.44 = (bf16[4,256,256]{2,1,0:T(8,128)(2,1)}, bf16[4,256,256]{2,1,0:T(8,128)(2,1)S(1)}, u32[]{:S(2)}, u32[]{:S(2)}) collective-permute-start(bf16[4,256,256]{2,1,0:T(8,128)(2,1)} %get-tuple-element.90), channel_id=1, source_target_pairs={{32,64},{64,32},{96,0},{0,96},{33,65},{65,33},{97,1},{1,97},{34,66... | collective-permute-start | bytes 1572872 | tf_op jit(solution)/shard_map/ppermute | solution.py:55
  169.6 13.4 %collective-permute-start.51 = (bf16[4,256,256]{2,1,0:T(8,128)(2,1)}, bf16[4,256,256]{2,1,0:T(8,128)(2,1)S(1)}, u32[]{:S(2)}, u32[]{:S(2)}) collective-permute-start(bf16[4,256,256]{2,1,0:T(8,128)(2,1)} %get-tuple-element.92), channel_id=1, source_target_pairs={{8,16},{16,8},{24,0},{0,24},{9,17},{17,9},{25,1},{1,25},{10,18},{1... | collective-permute-start | bytes 1572872 | tf_op jit(solution)/shard_map/ppermute | solution.py:55
  178.5 8.6 %collective-permute-start.28 = (bf16[2,256,256]{2,1,0:T(8,128)(2,1)S(1)}, bf16[2,256,256]{2,1,0:T(8,128)(2,1)S(1)}, u32[]{:S(2)}, u32[]{:S(2)}) collective-permute-start(bf16[2,256,256]{2,1,0:T(8,128)(2,1)S(1)} %dynamic-slice_bitcast_fusion.2), channel_id=1, source_target_pairs={{0,32},{32,0},{64,96},{96,64},{1,33},{33,1},{65,97},{97,65},{2,34}... | collective-permute-start | bytes 786440 | tf_op jit(solution)/shard_map/ppermute | solution.py:55
  189.9 9.4 %collective-permute-start.46 = (bf16[256,256]{1,0:T(8,128)(2,1)S(1)}, bf16[256,256]{1,0:T(8,128)(2,1)S(1)}, u32[]{:S(2)}, u32[]{:S(2)}) collective-permute-start(bf16[256,256]{1,0:T(8,128)(2,1)S(1)} %slice_bitcast_fusion.20), channel_id=1, source_target_pairs={{2,4},{4,2},{6,0},{0,6},{3,5},{5,3},{7,1},{1,7},{10,12},{12,10},{1... | collective-permute-start | bytes 393224 | tf_op jit(solution)/shard_map/ppermute | solution.py:55
  194.4 13.7 %collective-permute-start.30 = (bf16[2,256,256]{2,1,0:T(8,128)(2,1)S(1)}, bf16[2,256,256]{2,1,0:T(8,128)(2,1)S(1)}, u32[]{:S(2)}, u32[]{:S(2)}) collective-permute-start(bf16[2,256,256]{2,1,0:T(8,128)(2,1)S(1)} %pad_maximum_fusion.8), channel_id=1, source_target_pairs={{32,64},{64,32},{96,0},{0,96},{33,65},{65,33},{97,1},{1,97},{34,66... | collective-permute-start | bytes 786440 | tf_op jit(solution)/shard_map/ppermute | solution.py:55
  196.6 12.5 %collective-permute-start.40 = (bf16[2,256,256]{2,1,0:T(8,128)(2,1)S(1)}, bf16[2,256,256]{2,1,0:T(8,128)(2,1)S(1)}, u32[]{:S(2)}, u32[]{:S(2)}) collective-permute-start(bf16[2,256,256]{2,1,0:T(8,128)(2,1)S(1)} %pad_maximum_fusion.9), channel_id=1, source_target_pairs={{8,16},{16,8},{24,0},{0,24},{9,17},{17,9},{25,1},{1,25},{10,18},{1... | collective-permute-start | bytes 786440 | tf_op jit(solution)/shard_map/ppermute | solution.py:55
  213.7 11.3 %collective-permute-start.56 = (bf16[1,256,256]{2,1,0:T(8,128)(2,1)S(1)}, bf16[1,256,256]{2,1,0:T(8,128)(2,1)S(1)}, u32[]{:S(2)}, u32[]{:S(2)}) collective-permute-start(bf16[1,256,256]{2,1,0:T(8,128)(2,1)S(1)} %add_convert_fusion.14), channel_id=1, source_target_pairs={{32,64},{64,32},{96,0},{0,96},{33,65},{65,33},{97,1},{1,97},{34,66... | collective-permute-start | bytes 393224 | tf_op jit(solution)/shard_map/ppermute | solution.py:55
  218.4 8.9 %collective-permute-start.50 = (bf16[1,256,256]{2,1,0:T(8,128)(2,1)S(1)}, bf16[1,256,256]{2,1,0:T(8,128)(2,1)S(1)}, u32[]{:S(2)}, u32[]{:S(2)}) collective-permute-start(bf16[1,256,256]{2,1,0:T(8,128)(2,1)S(1)} %add_convert_fusion.16.refs_4_), channel_id=1, source_target_pairs={{32,64},{64,32},{96,0},{0,96},{33,65},{65,33},{97,1},{1,97},{34,66... | collective-permute-start | bytes 393224 | tf_op jit(solution)/shard_map/ppermute | solution.py:55
  222.7 8.6 %collective-permute-start.33 = (bf16[2,256,256]{2,1,0:T(8,128)(2,1)S(1)}, bf16[2,256,256]{2,1,0:T(8,128)(2,1)S(1)}, u32[]{:S(2)}, u32[]{:S(2)}) collective-permute-start(bf16[2,256,256]{2,1,0:T(8,128)(2,1)S(1)} %add_convert_fusion.10.refs_0_), channel_id=1, source_target_pairs={{0,32},{32,0},{64,96},{96,64},{1,33},{33,1},{65,97},{97,65},{2,34}... | collective-permute-start | bytes 786440 | tf_op jit(solution)/shard_map/ppermute | solution.py:55
  (52 other events, 311.1 us)

commit v5 on v4

--- a/solution.py
+++ b/solution.py
@@ -535,37 +535,35 @@
     )(core.reshape(1), own, other)
 
 
-def adam_kernel(core, kept, received, weights, first, second, out_weights, out_first, out_second):
+def assemble_kernel(core, kept, received, out):
     for block in range(6):
-        at = slice(block * WIDTH, (block + 1) * WIDTH)
         source = slice((block // 2) * WIDTH, (block // 2 + 1) * WIDTH)
-        gradient = jnp.where(block % 2 == core[0], kept[:, source], received[:, source]).astype(F32)
-        new_first = BETA_ONE * first[:, at] + (1.0 - BETA_ONE) * gradient
-        new_second = BETA_TWO * second[:, at] + (1.0 - BETA_TWO) * gradient * gradient
-        first_hat = new_first * (1.0 / (1.0 - BETA_ONE**STEP))
-        second_hat = new_second * (1.0 / (1.0 - BETA_TWO**STEP))
-        root = second_hat * lax.rsqrt(second_hat)
-        out_first[:, at] = new_first
-        out_second[:, at] = new_second
-        out_weights[:, at] = weights[:, at] - LEARN_RATE * (
-            first_hat * pl.reciprocal(root + EPS_ADAM) + DECAY_WEIGHT * weights[:, at]
+        straight = core[0] == block % 2
+        out[:, block * WIDTH : (block + 1) * WIDTH] = jnp.where(
+            straight, kept[:, source], received[:, source]
         )
 
 
-def adam(core, kept, received, *arrays):
-    piece = pl.BlockSpec((32, 3 * WIDTH), lambda i, c: (i, 0))
-    block = pl.BlockSpec((32, 6 * WIDTH), lambda i, c: (i, 0))
-    return pl.pallas_call(
-        adam_kernel,
-        name="adam",
-        grid_spec=pltpu.PrefetchScalarGridSpec(
-            num_scalar_prefetch=1,
-            grid=(8,),
-            in_specs=[piece, piece, block, block, block],
-            out_specs=(block,) * 3,
-        ),
-        out_shape=tuple(shape(x.shape, F32) for x in arrays),
-    )(core.reshape(1), kept, received, *arrays)
+def assemble(core, kept, received):
+    return pl.pallas_call(
+        assemble_kernel,
+        name="assemble",
+        in_specs=[pl.BlockSpec(memory_space=pltpu.SMEM), VMEM, VMEM],
+        out_specs=VMEM,
+        out_shape=shape((256, 6 * WIDTH), BF),
+    )(core.reshape(1), kept, received)
+
+
+def adam(core, kept, received, weights, first, second):
+    gradient = assemble(core, kept, received).astype(F32)
+    new_first = BETA_ONE * first + (1.0 - BETA_ONE) * gradient
+    new_second = BETA_TWO * second + (1.0 - BETA_TWO) * gradient * gradient
+    first_hat = new_first * (1.0 / (1.0 - BETA_ONE**STEP))
+    second_hat = new_second * (1.0 / (1.0 - BETA_TWO**STEP))
+    new_weights = weights - LEARN_RATE * (
+        first_hat / (jnp.sqrt(second_hat) + EPS_ADAM) + DECAY_WEIGHT * weights
+    )
+    return new_weights, new_first, new_second
 
 
 def gather_step(step, mine):

time: 255 us -> 252 us (0.988)
  Pallas kernels: 74.2 us -> 67.1 us
  other arithmetic: 8.38 us -> 14 us
    pallas_call x1, Pallas kernels: 9.82 us -> 2.77 us  [assemble(): pl.pallas_call(assemble_kernel, name='assemble', in_specs=[pl.BlockSpec(m...]
    sub x0 -> x1, other arithmetic: none -> 6.57 us  [adam(): weights - LEARN_RATE * (first_hat / (jnp.sqrt(second_hat) + EPS_ADAM) + D...]
    unnamed x73 -> x75, local copies, waits for them, and re-layouts: 5.5 us -> 5.5 us
  transfers between devices with their start and end apart: 61 -> 61, of which waited for: 35 -> 33; matrix products, arithmetic and copies ran while one was open for 6% -> 5% of each run, Pallas kernels for 16% -> 17%
where the time goes in v5:
time: 252 us; the launch traced here: 251 us
  starting transfers between devices  81.6 us (32%)
  waiting for transfers between devices  70.3 us (28%)
  Pallas kernels  67.1 us (27%)
  other arithmetic  14 us (6%)
  matrix products  9 us (4%)
  local copies, waits for them, and re-layouts  6.96 us (3%)
    ppermute x54, starting transfers between devices, swap(): return lax.ppermute(x, dim[0], PAIRS[dim[1]])  72.7 us
    ppermute x54, waiting for transfers between devices, swap(): return lax.ppermute(x, dim[0], PAIRS[dim[1]])  54 us
    pallas_call x2, Pallas kernels, gradient_call(): pl.pallas_call(kernel, grid=(1,), in_specs=[pl.BlockSpec(memory_space=plt...  20.3 us
    pallas_call x2, Pallas kernels, backward(): pl.pallas_call(backward_kernel, name='backward', grid_spec=pltpu.Prefetch...  10.8 us
    all_to_all x1, waiting for transfers between devices, earlier_states(): received = lax.all_to_all(cut, ('x', 'y'), 0, 0, tiled=True)  9.99 us
    dot_general x2, matrix products, project(): return jnp.dot(tokens, weights, preferred_element_type=F32).astype(BF)  9 us
    pallas_call x1, Pallas kernels, arrange(): pl.pallas_call(arrange_kernel, name='arrange', grid_spec=pltpu.PrefetchSc...  7.34 us
    pallas_call x1, Pallas kernels, forward(): pl.pallas_call(forward_kernel, name='forward', grid_spec=pltpu.PrefetchSc...  6.87 us
  transfers between devices with their start and end apart: 61, of which 33 were waited for; matrix products, arithmetic and copies ran while one was open for 5% of the time, Pallas kernels for 17%

profile of v5, /device:TPU:0, one launch (start us, length us, event | category | flops | bytes accessed | tf_op | source)
XLA Modules:
  0.0 250.5 jit_solution(14005266261861101423)
XLA Ops:
  0.6 3.1 %prepare.1 = (bf16[4,256,384]{2,1,0:T(8,128)(2,1)}, bf16[4,256,384]{2,1,0:T(8,128)(2,1)}, bf16[512,512]{1,0:T(8,128)(2,1)}) custom-call(s32[1]{0:T(128)} %bitcast.core, f32[256,3072]{1,0:T(8,128)} %refs_5_.1, f32[256,3072]{1,0:T(8,128)} %refs_5_.1, f32[256,3072]{1,0:T(8,128)} %refs_5_.1, f32[256,3072]{1,0:T(8,128)} %refs_5_.1, f32[256,3072]{1,0:T(8,128)} %refs_5_.1, ...), custom_call_target="tpu_custom_call" | custom-call | tf_op jit(solution)/shard_map/prepare/pallas_call | solution.py:119
  9.7 2.5 %collective-permute-start.3 = (bf16[1,256,384]{2,1,0:T(8,128)(2,1)S(1)}, bf16[1,256,384]{2,1,0:T(8,128)(2,1)S(1)}, u32[]{:S(2)}, u32[]{:S(2)}) collective-permute-start(bf16[1,256,384]{2,1,0:T(8,128)(2,1)S(1)} %get-tuple-element.105), channel_id=1, source_target_pairs={{2,4},{4,2},{6,0},{0,6},{3,5},{5,3},{7,1},{1,7},{10,12},{12,10},{1... | collective-permute-start | bytes 589832 | tf_op jit(solution)/shard_map/ppermute | solution.py:55
  13.8 3.9 %collective-permute-start.2 = (bf16[2,256,384]{2,1,0:T(8,128)(2,1)S(1)}, bf16[2,256,384]{2,1,0:T(8,128)(2,1)S(1)}, u32[]{:S(2)}, u32[]{:S(2)}) collective-permute-start(bf16[2,256,384]{2,1,0:T(8,128)(2,1)S(1)} %pad_maximum_fusion.4), channel_id=1, source_target_pairs={{2,4},{4,2},{6,0},{0,6},{3,5},{5,3},{7,1},{1,7},{10,12},{12,10},{1... | collective-permute-start | bytes 1179656 | tf_op jit(solution)/shard_map/ppermute | solution.py:55
  18.6 6.6 %collective-permute-done.2 = bf16[2,256,384]{2,1,0:T(8,128)(2,1)S(1)} collective-permute-done((bf16[2,256,384]{2,1,0:T(8,128)(2,1)S(1)}, bf16[2,256,384]{2,1,0:T(8,128)(2,1)S(1)}, u32[]{:S(2)}, u32[]{:S(2)}) %collective-permute-start.2) | collective-permute-done | bytes 393248 | tf_op jit(solution)/shard_map/ppermute | solution.py:55
  28.0 7.3 %arrange.1.tokens = bf16[1024,2048]{1,0:T(8,128)(2,1)} custom-call(s32[8]{0:T(128)} %stack.82.blocks, bf16[512,2048]{1,0:T(8,128)(2,1)} %bitcast.10.own, bf16[512,2048]{1,0:T(8,128)(2,1)} %collective-permute-done.5.other), custom_call_target="tpu_custom_call" | custom-call | tf_op jit(solution)/shard_map/arrange/pallas_call | solution.py:140
  37.3 4.9 %collective-permute-start.12 = (bf16[2,256,384]{2,1,0:T(8,128)(2,1)S(1)}, bf16[2,256,384]{2,1,0:T(8,128)(2,1)S(1)}, u32[]{:S(2)}, u32[]{:S(2)}) collective-permute-start(bf16[2,256,384]{2,1,0:T(8,128)(2,1)S(1)} %get-tuple-element.102), channel_id=1, source_target_pairs={{0,8},{8,0},{16,24},{24,16},{1,9},{9,1},{17,25},{25,17},{2,10},{10... | collective-permute-start | bytes 1179656 | tf_op jit(solution)/shard_map/ppermute | solution.py:55
  43.8 2.2 collective-permute-start.10
  53.5 2.6 %collective-permute-done.11 = bf16[2,256,384]{2,1,0:T(8,128)(2,1)S(1)} collective-permute-done((bf16[2,256,384]{2,1,0:T(8,128)(2,1)S(1)}, bf16[2,256,384]{2,1,0:T(8,128)(2,1)S(1)}, u32[]{:S(2)}, u32[]{:S(2)}) %collective-permute-start.11) | collective-permute-done | bytes 393248 | tf_op jit(solution)/shard_map/ppermute | solution.py:55
  56.4 4.5 %fusion.13.first.k0.v0.qkv = bf16[1024,768]{1,0:T(8,128)(2,1)} fusion(bf16[1024,2048]{1,0:T(8,128)(2,1)S(1)} %copy-done.1, bf16[2048,384]{1,0:T(8,128)(2,1)S(1)} %fusion.42, bf16[2048,384]{1,0:T(8,128)(2,1)S(1)} %fusion.46), kind=kOutput, calls=%fused_computation.14 | convolution fusion | flops 3228303360 | bytes 8912896 | tf_op jit(solution)/shard_map/dot_general | solution.py:184
  66.9 2.3 collective-permute-done.16
  74.0 4.5 %fusion.10.second.k1.v1.qkv = bf16[1024,768]{1,0:T(8,128)(2,1)} fusion(bf16[1024,2048]{1,0:T(8,128)(2,1)S(1)} %copy-done.1, bf16[2048,384]{1,0:T(8,128)(2,1)S(1)} %fusion.34, bf16[2048,384]{1,0:T(8,128)(2,1)S(1)} %fusion.38), kind=kOutput, calls=%fused_computation.13 | convolution fusion | flops 3228303360 | bytes 8912896 | tf_op jit(solution)/shard_map/dot_general | solution.py:184
  78.6 2.7 %outer.1 = f32[4,2,128,128]{3,2,1,0:T(8,128)} custom-call(bf16[1024,768]{1,0:T(8,128)(2,1)} %fusion.13.first.k0.v0.qkv, bf16[1024,768]{1,0:T(8,128)(2,1)} %fusion.13.first.k0.v0.qkv, bf16[1024,768]{1,0:T(8,128)(2,1)} %fusion.10.second.k1.v1.qkv, bf16[1024,768]{1,0:T(8,128)(2,1)} %fusion.10.second.k1.v1.qkv), custom_call_target="tpu_custom_call" | custom-call | tf_op jit(solution)/shard_map/outer/pallas_call | solution.py:162
  81.3 4.0 %all-to-all-start = ((f32[16,64,128]{2,1,0:T(8,128)}), f32[16,64,128]{2,1,0:T(8,128)S(1)}, u32[]{:S(2)}, u32[]{:S(2)}) async-start(f32[16,64,128]{2,1,0:T(8,128)} %bitcast.230), calls=%async_computation | async-start | bytes 1048576 | tf_op jit(solution)/shard_map/all_to_all | solution.py:213
  85.3 10.0 %all-to-all-done.received = f32[16,64,128]{2,1,0:T(8,128)S(1)} async-done(((f32[16,64,128]{2,1,0:T(8,128)}), f32[16,64,128]{2,1,0:T(8,128)S(1)}, u32[]{:S(2)}, u32[]{:S(2)}) %all-to-all-start) | async-done | bytes 524320 | tf_op jit(solution)/shard_map/all_to_all | solution.py:213
  97.9 3.7 %all-to-all-start.1 = ((bf16[16,64,128]{2,1,0:T(8,128)(2,1)}), bf16[16,64,128]{2,1,0:T(8,128)(2,1)S(1)}, u32[]{:S(2)}, u32[]{:S(2)}) async-start(bf16[16,64,128]{2,1,0:T(8,128)(2,1)} %running.1), calls=%async_computation.1 | async-start | bytes 524288 | tf_op jit(solution)/shard_map/all_to_all | solution.py:221
  101.6 6.5 %within.1 = f32[1024,512]{1,0:T(8,128)} custom-call(bf16[1024,768]{1,0:T(8,128)(2,1)} %fusion.13.first.k0.v0.qkv, bf16[1024,768]{1,0:T(8,128)(2,1)} %fusion.10.second.k1.v1.qkv), custom_call_target="tpu_custom_call" | custom-call | tf_op jit(solution)/shard_map/within/pallas_call | solution.py:265
  110.6 6.9 %forward.1 = (bf16[1024,512]{1,0:T(8,128)(2,1)}, bf16[1024,512]{1,0:T(8,128)(2,1)}, bf16[4,2,128,128]{3,2,1,0:T(8,128)(2,1)}) custom-call(s32[1]{0:T(128)} %bitcast.core, bf16[1024,768]{1,0:T(8,128)(2,1)} %fusion.13.first.k0.v0.qkv, bf16[1024,768]{1,0:T(8,128)(2,1)} %fusion.10.second.k1.v1.qkv, f32[1024,512]{1,0:T(8,128)} %within.1, ...), custom_call_target="tpu_custom_call" | custom-call | tf_op jit(solution)/shard_map/forward/pallas_call | solution.py:297
  118.0 5.4 %backward.2 = (bf16[1024,256]{1,0:T(8,128)(2,1)}, f32[2,1024,256]{2,1,0:T(8,128)}) custom-call(s32[1]{0:T(128)} %constant.53.clone.1.pair, bf16[1024,768]{1,0:T(8,128)(2,1)} %fusion.13.first.k0.v0.qkv, bf16[1024,512]{1,0:T(8,128)(2,1)} %get-tuple-element.65.grad, bf16[4,2,128,128]{3,2,1,0:T(8,128)(2,1)} %bitcast.216), custom_call_target="tpu_custom_call" | custom-call | tf_op jit(solution)/shard_map/backward/pallas_call | solution.py:333
  125.6 5.4 %backward.3 = (bf16[1024,256]{1,0:T(8,128)(2,1)}, f32[2,1024,256]{2,1,0:T(8,128)}) custom-call(s32[1]{0:T(128)} %constant.54.clone.1.pair, bf16[1024,768]{1,0:T(8,128)(2,1)} %fusion.10.second.k1.v1.qkv, bf16[1024,512]{1,0:T(8,128)(2,1)} %get-tuple-element.65.grad, bf16[4,2,128,128]{3,2,1,0:T(8,128)(2,1)} %bitcast.217), custom_call_target="tpu_custom_call" | custom-call | tf_op jit(solution)/shard_map/backward/pallas_call | solution.py:333
  133.3 6.9 %shard_map.84 = (bf16[4,256,256]{2,1,0:T(8,128)(2,1)}, bf16[4,256,256]{2,1,0:T(8,128)(2,1)}, bf16[4,256,256]{2,1,0:T(8,128)(2,1)}, bf16[4,256,256]{2,1,0:T(8,128)(2,1)}) custom-call(s32[2]{0:T(128)} %pad_add_fusion.keeps, bf16[1024,256]{1,0:T(8,128)(2,1)} %get-tuple-element.69.q0, bf16[1024,256]{1,0:T(8,128)(2,1)} %get-tuple-element.70.q1, ...), custom_call_target="tpu_custom_call" | custom-call | tf_op jit(solution)/shard_map/pallas_call | solution.py:428
  145.2 3.9 %collective-permute-done.26 = bf16[4,2,128,128]{3,2,1,0:T(8,128)(2,1)S(1)} collective-permute-done((bf16[4,2,128,128]{3,2,1,0:T(8,128)(2,1)S(1)}, bf16[4,2,128,128]{3,2,1,0:T(8,128)(2,1)S(1)}, u32[]{:S(2)}, u32[]{:S(2)}) %collective-permute-start.26) | collective-permute-done | bytes 262176 | tf_op jit(solution)/shard_map/ppermute | solution.py:55
  150.1 13.3 %shard_map.85 = (bf16[4,256,256]{2,1,0:T(8,128)(2,1)}, bf16[4,256,256]{2,1,0:T(8,128)(2,1)}, bf16[4,256,256]{2,1,0:T(8,128)(2,1)}, bf16[4,256,256]{2,1,0:T(8,128...) custom-call(s32[2]{0:T(128)} %pad_add_fusion.keeps, ...), custom_call_target="tpu_custom_call" | custom-call | tf_op jit(solution)/shard_map/pallas_call | solution.py:428
  173.6 3.8 %collective-permute-done.24 = bf16[2,256,256]{2,1,0:T(8,128)(2,1)S(1)} collective-permute-done((bf16[2,256,256]{2,1,0:T(8,128)(2,1)S(1)}, bf16[2,256,256]{2,1,0:T(8,128)(2,1)S(1)}, u32[]{:S(2)}, u32[]{:S(2)}) %collective-permute-start.24) | collective-permute-done | bytes 262176 | tf_op jit(solution)/shard_map/ppermute | solution.py:55
  188.6 2.6 %collective-permute-start.46 = (bf16[256,256]{1,0:T(8,128)(2,1)S(1)}, bf16[256,256]{1,0:T(8,128)(2,1)S(1)}, u32[]{:S(2)}, u32[]{:S(2)}) collective-permute-start(bf16[256,256]{1,0:T(8,128)(2,1)S(1)} %slice_bitcast_fusion.20), channel_id=1, source_target_pairs={{2,4},{4,2},{6,0},{0,6},{3,5},{5,3},{7,1},{1,7},{10,12},{12,10},{1... | collective-permute-start | bytes 393224 | tf_op jit(solution)/shard_map/ppermute | solution.py:55
  195.3 2.4 collective-permute-start.40
  198.9 5.1 %collective-permute-done.47 = bf16[1,256,256]{2,1,0:T(8,128)(2,1)S(1)} collective-permute-done((bf16[1,256,256]{2,1,0:T(8,128)(2,1)S(1)}, bf16[1,256,256]{2,1,0:T(8,128)(2,1)S(1)}, u32[]{:S(2)}, u32[]{:S(2)}) %collective-permute-start.47) | collective-permute-done | bytes 131104 | tf_op jit(solution)/shard_map/ppermute | solution.py:55
  218.3 2.9 %collective-permute-done.32 = bf16[2,256,256]{2,1,0:T(8,128)(2,1)S(1)} collective-permute-done((bf16[2,256,256]{2,1,0:T(8,128)(2,1)S(1)}, bf16[2,256,256]{2,1,0:T(8,128)(2,1)S(1)}, u32[]{:S(2)}, u32[]{:S(2)}) %collective-permute-start.32) | collective-permute-done | bytes 262176 | tf_op jit(solution)/shard_map/ppermute | solution.py:55
  225.4 4.4 %collective-permute-done.57.refs_7_ = bf16[1,256,256]{2,1,0:T(8,128)(2,1)S(1)} collective-permute-done((bf16[1,256,256]{2,1,0:T(8,128)(2,1)S(1)}, bf16[1,256,256]{2,1,0:T(8,128)(2,1)S(1)}, u32[]{:S(2)}, u32[]{:S(2)}) %collective-permute-start.57) | collective-permute-done | bytes 131104 | tf_op jit(solution)/shard_map/ppermute | solution.py:55
  231.3 2.9 %sort_pieces.1 = (bf16[256,1536]{1,0:T(8,128)(2,1)}, bf16[256,1536]{1,0:T(8,128)(2,1)}) custom-call(s32[4]{0:T(128)} %add_convert_fusion.19.holds, bf16[2,256,256]{2,1,0:T(8,128)(2,1)} %copy-done.6, bf16[2,256,256]{2,1,0:T(8,128)(2,1)} %copy-done.19, bf16[2,256,256]{2,1,0:T(8,128)(2,1)} %copy-done.7, bf16[2,256,256]{2,1,0:T(8,128)(2,1)} %copy-done.20, ...), custom_call_target="tpu_custom_call" | custom-call | tf_op jit(solution)/shard_map/sort_pieces/pallas_call | solution.py:508
  234.8 2.6 %collective-permute-done.19.other = bf16[512,512]{1,0:T(8,128)(2,1)S(1)} collective-permute-done((bf16[512,512]{1,0:T(8,128)(2,1)S(1)}, bf16[512,512]{1,0:T(8,128)(2,1)S(1)}, u32[]{:S(2)}, u32[]{:S(2)}) %collective-permute-start.19) | collective-permute-done | bytes 524320 | tf_op jit(solution)/shard_map/ppermute | solution.py:54
  241.2 2.8 %assemble.1 = bf16[256,3072]{1,0:T(8,128)(2,1)} custom-call(s32[1]{0:T(128)} %bitcast.core, bf16[256,1536]{1,0:T(8,128)(2,1)} %get-tuple-element.90.kept, bf16[256,1536]{1,0:T(8,128)(2,1)} %copy-done.8), custom_call_target="tpu_custom_call" | custom-call | tf_op jit(solution)/shard_map/assemble/pallas_call | solution.py:548
  244.0 6.6 %multiply_subtract_fusion = (f32[256,3072]{1,0:T(8,128)}, f32[256,3072]{1,0:T(8,128)}, f32[256,3072]{1,0:T(8,128)}) fusion(f32[256,3072]{1,0:T(8,128)S(1)} %copy-done, bf16[256,3072]{1,0:T(8,128)(2,1)} %assemble.1, f32[256,3072]{1,0:T(8,128)} %param.7, f32[256,3072]{1,0:T(8,128)} %param.8), kind=kLoop, calls=%fused_computation.12 | loop fusion | flops 12582912 | bytes 20447232 | tf_op jit(solution)/shard_map/sub | solution.py:563
  (252 shorter events, 99.5 us)
Async XLA Ops:
  3.8 24.2 %collective-permute-start.5 = (bf16[512,2048]{1,0:T(8,128)(2,1)}, bf16[512,2048]{1,0:T(8,128)(2,1)}, u32[]{:S(2)}, u32[]{:S(2)}) collective-permute-start(bf16[512,2048]{1,0:T(8,128)(2,1)} %bitcast.10.own), channel_id=1, source_target_pairs={{0,1},{1,0},{2,3},{3,2},{4,5},{5,4},{6,7},{7,6},{8,9},{9,8},{10,11... | collective-permute-start | bytes 6291464 | tf_op jit(solution)/shard_map/ppermute | solution.py:54
  13.8 11.4 %collective-permute-start.2 = (bf16[2,256,384]{2,1,0:T(8,128)(2,1)S(1)}, bf16[2,256,384]{2,1,0:T(8,128)(2,1)S(1)}, u32[]{:S(2)}, u32[]{:S(2)}) collective-permute-start(bf16[2,256,384]{2,1,0:T(8,128)(2,1)S(1)} %pad_maximum_fusion.4), channel_id=1, source_target_pairs={{2,4},{4,2},{6,0},{0,6},{3,5},{5,3},{7,1},{1,7},{10,12},{12,10},{1... | collective-permute-start | bytes 1179656 | tf_op jit(solution)/shard_map/ppermute | solution.py:55
  17.8 9.1 %collective-permute-start.4 = (bf16[2,256,384]{2,1,0:T(8,128)(2,1)S(1)}, bf16[2,256,384]{2,1,0:T(8,128)(2,1)}, u32[]{:S(2)}, u32[]{:S(2)}) collective-permute-start(bf16[2,256,384]{2,1,0:T(8,128)(2,1)S(1)} %pad_maximum_fusion.5), channel_id=1, source_target_pairs={{0,2},{2,0},{4,6},{6,4},{1,3},{3,1},{5,7},{7,5},{8,10},{10,8},{12,... | collective-permute-start | bytes 1179656 | tf_op jit(solution)/shard_map/ppermute | solution.py:55
  35.4 10.7 %collective-permute-start.6 = (bf16[1,256,384]{2,1,0:T(8,128)(2,1)S(1)}, bf16[1,256,384]{2,1,0:T(8,128)(2,1)S(1)}, u32[]{:S(2)}, u32[]{:S(2)}) collective-permute-start(bf16[1,256,384]{2,1,0:T(8,128)(2,1)S(1)} %get-tuple-element.104), channel_id=1, source_target_pairs={{0,2},{2,0},{4,6},{6,4},{1,3},{3,1},{5,7},{7,5},{8,10},{10,8},{12,... | collective-permute-start | bytes 589832 | tf_op jit(solution)/shard_map/ppermute | solution.py:55
  35.7 11.7 %collective-permute-start.8 = (bf16[1,256,384]{2,1,0:T(8,128)(2,1)S(1)}, bf16[1,256,384]{2,1,0:T(8,128)(2,1)S(1)}, u32[]{:S(2)}, u32[]{:S(2)}) collective-permute-start(bf16[1,256,384]{2,1,0:T(8,128)(2,1)S(1)} %get-tuple-element.103), channel_id=1, source_target_pairs={{2,4},{4,2},{6,0},{0,6},{3,5},{5,3},{7,1},{1,7},{10,12},{12,10},{1... | collective-permute-start | bytes 589832 | tf_op jit(solution)/shard_map/ppermute | solution.py:55
  37.3 12.8 %collective-permute-start.12 = (bf16[2,256,384]{2,1,0:T(8,128)(2,1)S(1)}, bf16[2,256,384]{2,1,0:T(8,128)(2,1)S(1)}, u32[]{:S(2)}, u32[]{:S(2)}) collective-permute-start(bf16[2,256,384]{2,1,0:T(8,128)(2,1)S(1)} %get-tuple-element.102), channel_id=1, source_target_pairs={{0,8},{8,0},{16,24},{24,16},{1,9},{9,1},{17,25},{25,17},{2,10},{10... | collective-permute-start | bytes 1179656 | tf_op jit(solution)/shard_map/ppermute | solution.py:55
  42.3 10.7 %collective-permute-start.13 = (bf16[2,256,384]{2,1,0:T(8,128)(2,1)S(1)}, bf16[2,256,384]{2,1,0:T(8,128)(2,1)S(1)}, u32[]{:S(2)}, u32[]{:S(2)}) collective-permute-start(bf16[2,256,384]{2,1,0:T(8,128)(2,1)S(1)} %get-tuple-element.101), channel_id=1, source_target_pairs={{8,16},{16,8},{24,0},{0,24},{9,17},{17,9},{25,1},{1,25},{10,18},{1... | collective-permute-start | bytes 1179656 | tf_op jit(solution)/shard_map/ppermute | solution.py:55
  43.8 9.6 %collective-permute-start.10 = (bf16[2,256,384]{2,1,0:T(8,128)(2,1)S(1)}, bf16[2,256,384]{2,1,0:T(8,128)(2,1)S(1)}, u32[]{:S(2)}, u32[]{:S(2)}) collective-permute-start(bf16[2,256,384]{2,1,0:T(8,128)(2,1)S(1)} %get-tuple-element.100), channel_id=1, source_target_pairs={{0,32},{32,0},{64,96},{96,64},{1,33},{33,1},{65,97},{97,65},{2,34}... | collective-permute-start | bytes 1179656 | tf_op jit(solution)/shard_map/ppermute | solution.py:55
  46.0 10.1 %collective-permute-start.11 = (bf16[2,256,384]{2,1,0:T(8,128)(2,1)S(1)}, bf16[2,256,384]{2,1,0:T(8,128)(2,1)S(1)}, u32[]{:S(2)}, u32[]{:S(2)}) collective-permute-start(bf16[2,256,384]{2,1,0:T(8,128)(2,1)S(1)} %get-tuple-element.99), channel_id=1, source_target_pairs={{32,64},{64,32},{96,0},{0,96},{33,65},{65,33},{97,1},{1,97},{34,66... | collective-permute-start | bytes 1179656 | tf_op jit(solution)/shard_map/ppermute | solution.py:55
  47.4 13.4 %collective-permute-start.7 = (bf16[2,256,384]{2,1,0:T(8,128)(2,1)S(1)}, bf16[2,256,384]{2,1,0:T(8,128)(2,1)S(1)}, u32[]{:S(2)}, u32[]{:S(2)}) collective-permute-start(bf16[2,256,384]{2,1,0:T(8,128)(2,1)S(1)} %pad_maximum_fusion.6), channel_id=1, source_target_pairs={{2,4},{4,2},{6,0},{0,6},{3,5},{5,3},{7,1},{1,7},{10,12},{12,10},{1... | collective-permute-start | bytes 1179656 | tf_op jit(solution)/shard_map/ppermute | solution.py:55
  50.1 10.8 %collective-permute-start.9 = (bf16[2,256,384]{2,1,0:T(8,128)(2,1)S(1)}, bf16[2,256,384]{2,1,0:T(8,128)(2,1)S(1)}, u32[]{:S(2)}, u32[]{:S(2)}) collective-permute-start(bf16[2,256,384]{2,1,0:T(8,128)(2,1)S(1)} %pad_maximum_fusion.7), channel_id=1, source_target_pairs={{0,2},{2,0},{4,6},{6,4},{1,3},{3,1},{5,7},{7,5},{8,10},{10,8},{12,... | collective-permute-start | bytes 1179656 | tf_op jit(solution)/shard_map/ppermute | solution.py:55
  61.2 8.1 %collective-permute-start.16 = (bf16[2,256,384]{2,1,0:T(8,128)(2,1)S(1)}, bf16[2,256,384]{2,1,0:T(8,128)(2,1)S(1)}, u32[]{:S(2)}, u32[]{:S(2)}) collective-permute-start(bf16[2,256,384]{2,1,0:T(8,128)(2,1)S(1)} %get-tuple-element.98), channel_id=1, source_target_pairs={{0,8},{8,0},{16,24},{24,16},{1,9},{9,1},{17,25},{25,17},{2,10},{10... | collective-permute-start | bytes 1179656 | tf_op jit(solution)/shard_map/ppermute | solution.py:55
  61.7 9.5 %collective-permute-start.17 = (bf16[2,256,384]{2,1,0:T(8,128)(2,1)S(1)}, bf16[2,256,384]{2,1,0:T(8,128)(2,1)S(1)}, u32[]{:S(2)}, u32[]{:S(2)}) collective-permute-start(bf16[2,256,384]{2,1,0:T(8,128)(2,1)S(1)} %get-tuple-element.97), channel_id=1, source_target_pairs={{8,16},{16,8},{24,0},{0,24},{9,17},{17,9},{25,1},{1,25},{10,18},{1... | collective-permute-start | bytes 1179656 | tf_op jit(solution)/shard_map/ppermute | solution.py:55
  63.7 8.4 %collective-permute-start.14 = (bf16[2,256,384]{2,1,0:T(8,128)(2,1)S(1)}, bf16[2,256,384]{2,1,0:T(8,128)(2,1)S(1)}, u32[]{:S(2)}, u32[]{:S(2)}) collective-permute-start(bf16[2,256,384]{2,1,0:T(8,128)(2,1)S(1)} %get-tuple-element.96), channel_id=1, source_target_pairs={{0,32},{32,0},{64,96},{96,64},{1,33},{33,1},{65,97},{97,65},{2,34}... | collective-permute-start | bytes 1179656 | tf_op jit(solution)/shard_map/ppermute | solution.py:55
  64.8 9.0 %collective-permute-start.15 = (bf16[2,256,384]{2,1,0:T(8,128)(2,1)S(1)}, bf16[2,256,384]{2,1,0:T(8,128)(2,1)S(1)}, u32[]{:S(2)}, u32[]{:S(2)}) collective-permute-start(bf16[2,256,384]{2,1,0:T(8,128)(2,1)S(1)} %get-tuple-element.95), channel_id=1, source_target_pairs={{32,64},{64,32},{96,0},{0,96},{33,65},{65,33},{97,1},{1,97},{34,66... | collective-permute-start | bytes 1179656 | tf_op jit(solution)/shard_map/ppermute | solution.py:55
  81.3 14.1 %all-to-all-start = ((f32[16,64,128]{2,1,0:T(8,128)}), f32[16,64,128]{2,1,0:T(8,128)S(1)}, u32[]{:S(2)}, u32[]{:S(2)}) async-start(f32[16,64,128]{2,1,0:T(8,128)} %bitcast.230), calls=%async_computation | async-start | bytes 1048576 | tf_op jit(solution)/shard_map/all_to_all | solution.py:213
  85.2 22.9 %collective-permute-start.18 = (bf16[512,512]{1,0:T(8,128)(2,1)S(1)}, bf16[512,512]{1,0:T(8,128)(2,1)S(1)}, u32[]{:S(2)}, u32[]{:S(2)}) collective-permute-start(bf16[512,512]{1,0:T(8,128)(2,1)S(1)} %copy-done.23), channel_id=1, source_target_pairs={{0,1},{1,0},{2,3},{3,2},{4,5},{5,4},{6,7},{7,6},{8,9},{9,8},{10,11... | collective-permute-start | bytes 1572872 | tf_op jit(solution)/shard_map/ppermute | solution.py:54
  97.9 12.0 %all-to-all-start.1 = ((bf16[16,64,128]{2,1,0:T(8,128)(2,1)}), bf16[16,64,128]{2,1,0:T(8,128)(2,1)S(1)}, u32[]{:S(2)}, u32[]{:S(2)}) async-start(bf16[16,64,128]{2,1,0:T(8,128)(2,1)} %running.1), calls=%async_computation.1 | async-start | bytes 524288 | tf_op jit(solution)/shard_map/all_to_all | solution.py:221
  132.0 8.3 %collective-permute-start.22 = (bf16[4,2,128,128]{3,2,1,0:T(8,128)(2,1)S(1)}, bf16[4,2,128,128]{3,2,1,0:T(8,128)(2,1)S(1)}, u32[]{:S(2)}, u32[]{:S(2)}) collective-permute-start(bf16[4,2,128,128]{3,2,1,0:T(8,128)(2,1)S(1)} %fusion.27), channel_id=1, source_target_pairs={{0,32},{32,0},{64,96},{96,64},{1,33},{33,1},{65,97},{97,65},{2,34}... | collective-permute-start | bytes 786440 | tf_op jit(solution)/shard_map/ppermute | solution.py:55
  140.3 28.3 %collective-permute-start.23 = (bf16[4,256,256]{2,1,0:T(8,128)(2,1)}, bf16[4,256,256]{2,1,0:T(8,128)(2,1)S(1)}, u32[]{:S(2)}, u32[]{:S(2)}) collective-permute-start(bf16[4,256,256]{2,1,0:T(8,128)(2,1)} %get-tuple-element.76), channel_id=1, source_target_pairs={{0,2},{2,0},{4,6},{6,4},{1,3},{3,1},{5,7},{7,5},{8,10},{10,8},{12,... | collective-permute-start | bytes 1572872 | tf_op jit(solution)/shard_map/ppermute | solution.py:55
  143.7 27.3 %collective-permute-start.34 = (bf16[4,256,256]{2,1,0:T(8,128)(2,1)}, bf16[4,256,256]{2,1,0:T(8,128)(2,1)S(1)}, u32[]{:S(2)}, u32[]{:S(2)}) collective-permute-start(bf16[4,256,256]{2,1,0:T(8,128)(2,1)} %get-tuple-element.83), channel_id=1, source_target_pairs={{2,4},{4,2},{6,0},{0,6},{3,5},{5,3},{7,1},{1,7},{10,12},{12,10},{1... | collective-permute-start | bytes 1572872 | tf_op jit(solution)/shard_map/ppermute | solution.py:55
  163.4 10.0 %collective-permute-start.27 = (bf16[4,256,256]{2,1,0:T(8,128)(2,1)}, bf16[4,256,256]{2,1,0:T(8,128)(2,1)S(1)}, u32[]{:S(2)}, u32[]{:S(2)}) collective-permute-start(bf16[4,256,256]{2,1,0:T(8,128)(2,1)} %get-tuple-element.81), channel_id=1, source_target_pairs={{0,2},{2,0},{4,6},{6,4},{1,3},{3,1},{5,7},{7,5},{8,10},{10,8},{12,... | collective-permute-start | bytes 1572872 | tf_op jit(solution)/shard_map/ppermute | solution.py:55
  164.5 13.0 %collective-permute-start.37 = (bf16[4,256,256]{2,1,0:T(8,128)(2,1)}, bf16[4,256,256]{2,1,0:T(8,128)(2,1)S(1)}, u32[]{:S(2)}, u32[]{:S(2)}) collective-permute-start(bf16[4,256,256]{2,1,0:T(8,128)(2,1)} %get-tuple-element.85), channel_id=1, source_target_pairs={{2,4},{4,2},{6,0},{0,6},{3,5},{5,3},{7,1},{1,7},{10,12},{12,10},{1... | collective-permute-start | bytes 1572872 | tf_op jit(solution)/shard_map/ppermute | solution.py:55
  166.5 13.4 %collective-permute-start.44 = (bf16[4,256,256]{2,1,0:T(8,128)(2,1)}, bf16[4,256,256]{2,1,0:T(8,128)(2,1)S(1)}, u32[]{:S(2)}, u32[]{:S(2)}) collective-permute-start(bf16[4,256,256]{2,1,0:T(8,128)(2,1)} %get-tuple-element.87), channel_id=1, source_target_pairs={{32,64},{64,32},{96,0},{0,96},{33,65},{65,33},{97,1},{1,97},{34,66... | collective-permute-start | bytes 1572872 | tf_op jit(solution)/shard_map/ppermute | solution.py:55
  168.6 13.1 %collective-permute-start.51 = (bf16[4,256,256]{2,1,0:T(8,128)(2,1)}, bf16[4,256,256]{2,1,0:T(8,128)(2,1)S(1)}, u32[]{:S(2)}, u32[]{:S(2)}) collective-permute-start(bf16[4,256,256]{2,1,0:T(8,128)(2,1)} %get-tuple-element.89), channel_id=1, source_target_pairs={{8,16},{16,8},{24,0},{0,24},{9,17},{17,9},{25,1},{1,25},{10,18},{1... | collective-permute-start | bytes 1572872 | tf_op jit(solution)/shard_map/ppermute | solution.py:55
  177.4 8.2 %collective-permute-start.28 = (bf16[2,256,256]{2,1,0:T(8,128)(2,1)S(1)}, bf16[2,256,256]{2,1,0:T(8,128)(2,1)S(1)}, u32[]{:S(2)}, u32[]{:S(2)}) collective-permute-start(bf16[2,256,256]{2,1,0:T(8,128)(2,1)S(1)} %dynamic-slice_bitcast_fusion.2), channel_id=1, source_target_pairs={{0,32},{32,0},{64,96},{96,64},{1,33},{33,1},{65,97},{97,65},{2,34}... | collective-permute-start | bytes 786440 | tf_op jit(solution)/shard_map/ppermute | solution.py:55
  188.6 9.2 %collective-permute-start.46 = (bf16[256,256]{1,0:T(8,128)(2,1)S(1)}, bf16[256,256]{1,0:T(8,128)(2,1)S(1)}, u32[]{:S(2)}, u32[]{:S(2)}) collective-permute-start(bf16[256,256]{1,0:T(8,128)(2,1)S(1)} %slice_bitcast_fusion.20), channel_id=1, source_target_pairs={{2,4},{4,2},{6,0},{0,6},{3,5},{5,3},{7,1},{1,7},{10,12},{12,10},{1... | collective-permute-start | bytes 393224 | tf_op jit(solution)/shard_map/ppermute | solution.py:55
  193.1 13.4 %collective-permute-start.30 = (bf16[2,256,256]{2,1,0:T(8,128)(2,1)S(1)}, bf16[2,256,256]{2,1,0:T(8,128)(2,1)S(1)}, u32[]{:S(2)}, u32[]{:S(2)}) collective-permute-start(bf16[2,256,256]{2,1,0:T(8,128)(2,1)S(1)} %pad_maximum_fusion.8), channel_id=1, source_target_pairs={{32,64},{64,32},{96,0},{0,96},{33,65},{65,33},{97,1},{1,97},{34,66... | collective-permute-start | bytes 786440 | tf_op jit(solution)/shard_map/ppermute | solution.py:55
  195.3 12.5 %collective-permute-start.40 = (bf16[2,256,256]{2,1,0:T(8,128)(2,1)S(1)}, bf16[2,256,256]{2,1,0:T(8,128)(2,1)S(1)}, u32[]{:S(2)}, u32[]{:S(2)}) collective-permute-start(bf16[2,256,256]{2,1,0:T(8,128)(2,1)S(1)} %pad_maximum_fusion.9), channel_id=1, source_target_pairs={{8,16},{16,8},{24,0},{0,24},{9,17},{17,9},{25,1},{1,25},{10,18},{1... | collective-permute-start | bytes 786440 | tf_op jit(solution)/shard_map/ppermute | solution.py:55
  212.1 11.5 %collective-permute-start.56 = (bf16[1,256,256]{2,1,0:T(8,128)(2,1)S(1)}, bf16[1,256,256]{2,1,0:T(8,128)(2,1)S(1)}, u32[]{:S(2)}, u32[]{:S(2)}) collective-permute-start(bf16[1,256,256]{2,1,0:T(8,128)(2,1)S(1)} %add_convert_fusion.14), channel_id=1, source_target_pairs={{32,64},{64,32},{96,0},{0,96},{33,65},{65,33},{97,1},{1,97},{34,66... | collective-permute-start | bytes 393224 | tf_op jit(solution)/shard_map/ppermute | solution.py:55
  216.9 8.6 %collective-permute-start.50 = (bf16[1,256,256]{2,1,0:T(8,128)(2,1)S(1)}, bf16[1,256,256]{2,1,0:T(8,128)(2,1)S(1)}, u32[]{:S(2)}, u32[]{:S(2)}) collective-permute-start(bf16[1,256,256]{2,1,0:T(8,128)(2,1)S(1)} %add_convert_fusion.16.refs_4_), channel_id=1, source_target_pairs={{32,64},{64,32},{96,0},{0,96},{33,65},{65,33},{97,1},{1,97},{34,66... | collective-permute-start | bytes 393224 | tf_op jit(solution)/shard_map/ppermute | solution.py:55
  221.3 8.6 %collective-permute-start.33 = (bf16[2,256,256]{2,1,0:T(8,128)(2,1)S(1)}, bf16[2,256,256]{2,1,0:T(8,128)(2,1)S(1)}, u32[]{:S(2)}, u32[]{:S(2)}) collective-permute-start(bf16[2,256,256]{2,1,0:T(8,128)(2,1)S(1)} %add_convert_fusion.10.refs_0_), channel_id=1, source_target_pairs={{0,32},{32,0},{64,96},{96,64},{1,33},{33,1},{65,97},{97,65},{2,34}... | collective-permute-start | bytes 786440 | tf_op jit(solution)/shard_map/ppermute | solution.py:55
  (53 other events, 315.3 us)

commit v6 on v5

--- a/solution.py
+++ b/solution.py
@@ -548,8 +548,10 @@
     return pl.pallas_call(
         assemble_kernel,
         name="assemble",
-        in_specs=[pl.BlockSpec(memory_space=pltpu.SMEM), VMEM, VMEM],
-        out_specs=VMEM,
+        grid=(4,),
+        in_specs=[pl.BlockSpec(memory_space=pltpu.SMEM)]
+        + [pl.BlockSpec((64, 3 * WIDTH), lambda i: (i, 0))] * 2,
+        out_specs=pl.BlockSpec((64, 6 * WIDTH), lambda i: (i, 0)),
         out_shape=shape((256, 6 * WIDTH), BF),
     )(core.reshape(1), kept, received)
 

time: 252 us -> 254 us (level)
  transfers between devices with their start and end apart: 61 -> 61, of which waited for: 33 -> 33; matrix products, arithmetic and copies ran while one was open for 5% -> 5% of each run, Pallas kernels for 17% -> 16%
where the time goes in v6:
time: 254 us; the launch traced here: 252 us
  starting transfers between devices  81.6 us (32%)
  waiting for transfers between devices  70.3 us (28%)
  Pallas kernels  68.2 us (27%)
  other arithmetic  14 us (6%)
  matrix products  9 us (4%)
  local copies, waits for them, and re-layouts  6.96 us (3%)
    ppermute x54, starting transfers between devices, swap(): return lax.ppermute(x, dim[0], PAIRS[dim[1]])  72.7 us
    ppermute x54, waiting for transfers between devices, swap(): return lax.ppermute(x, dim[0], PAIRS[dim[1]])  54 us
    pallas_call x2, Pallas kernels, gradient_call(): pl.pallas_call(kernel, grid=(1,), in_specs=[pl.BlockSpec(memory_space=plt...  20.3 us
    pallas_call x2, Pallas kernels, backward(): pl.pallas_call(backward_kernel, name='backward', grid_spec=pltpu.Prefetch...  10.8 us
    all_to_all x1, waiting for transfers between devices, earlier_states(): received = lax.all_to_all(cut, ('x', 'y'), 0, 0, tiled=True)  9.99 us
    dot_general x2, matrix products, project(): return jnp.dot(tokens, weights, preferred_element_type=F32).astype(BF)  9 us
    pallas_call x1, Pallas kernels, arrange(): pl.pallas_call(arrange_kernel, name='arrange', grid_spec=pltpu.PrefetchSc...  7.34 us
    pallas_call x1, Pallas kernels, forward(): pl.pallas_call(forward_kernel, name='forward', grid_spec=pltpu.PrefetchSc...  6.87 us
  transfers between devices with their start and end apart: 61, of which 33 were waited for; matrix products, arithmetic and copies ran while one was open for 5% of the time, Pallas kernels for 16%

profile of v6, /device:TPU:0, one launch (start us, length us, event | category | flops | bytes accessed | tf_op | source)
XLA Modules:
  0.0 251.6 jit_solution(14349851620011194044)
XLA Ops:
  0.6 3.1 %prepare.1 = (bf16[4,256,384]{2,1,0:T(8,128)(2,1)}, bf16[4,256,384]{2,1,0:T(8,128)(2,1)}, bf16[512,512]{1,0:T(8,128)(2,1)}) custom-call(s32[1]{0:T(128)} %bitcast.core, f32[256,3072]{1,0:T(8,128)} %refs_5_.1, f32[256,3072]{1,0:T(8,128)} %refs_5_.1, f32[256,3072]{1,0:T(8,128)} %refs_5_.1, f32[256,3072]{1,0:T(8,128)} %refs_5_.1, f32[256,3072]{1,0:T(8,128)} %refs_5_.1, ...), custom_call_target="tpu_custom_call" | custom-call | tf_op jit(solution)/shard_map/prepare/pallas_call | solution.py:119
  9.7 2.5 %collective-permute-start.3 = (bf16[1,256,384]{2,1,0:T(8,128)(2,1)S(1)}, bf16[1,256,384]{2,1,0:T(8,128)(2,1)S(1)}, u32[]{:S(2)}, u32[]{:S(2)}) collective-permute-start(bf16[1,256,384]{2,1,0:T(8,128)(2,1)S(1)} %get-tuple-element.105), channel_id=1, source_target_pairs={{2,4},{4,2},{6,0},{0,6},{3,5},{5,3},{7,1},{1,7},{10,12},{12,10},{1... | collective-permute-start | bytes 589832 | tf_op jit(solution)/shard_map/ppermute | solution.py:55
  13.8 3.9 %collective-permute-start.2 = (bf16[2,256,384]{2,1,0:T(8,128)(2,1)S(1)}, bf16[2,256,384]{2,1,0:T(8,128)(2,1)S(1)}, u32[]{:S(2)}, u32[]{:S(2)}) collective-permute-start(bf16[2,256,384]{2,1,0:T(8,128)(2,1)S(1)} %pad_maximum_fusion.4), channel_id=1, source_target_pairs={{2,4},{4,2},{6,0},{0,6},{3,5},{5,3},{7,1},{1,7},{10,12},{12,10},{1... | collective-permute-start | bytes 1179656 | tf_op jit(solution)/shard_map/ppermute | solution.py:55
  18.6 6.6 %collective-permute-done.2 = bf16[2,256,384]{2,1,0:T(8,128)(2,1)S(1)} collective-permute-done((bf16[2,256,384]{2,1,0:T(8,128)(2,1)S(1)}, bf16[2,256,384]{2,1,0:T(8,128)(2,1)S(1)}, u32[]{:S(2)}, u32[]{:S(2)}) %collective-permute-start.2) | collective-permute-done | bytes 393248 | tf_op jit(solution)/shard_map/ppermute | solution.py:55
  28.0 7.3 %arrange.1.tokens = bf16[1024,2048]{1,0:T(8,128)(2,1)} custom-call(s32[8]{0:T(128)} %stack.82.blocks, bf16[512,2048]{1,0:T(8,128)(2,1)} %bitcast.10.own, bf16[512,2048]{1,0:T(8,128)(2,1)} %collective-permute-done.5.other), custom_call_target="tpu_custom_call" | custom-call | tf_op jit(solution)/shard_map/arrange/pallas_call | solution.py:140
  37.3 4.9 %collective-permute-start.12 = (bf16[2,256,384]{2,1,0:T(8,128)(2,1)S(1)}, bf16[2,256,384]{2,1,0:T(8,128)(2,1)S(1)}, u32[]{:S(2)}, u32[]{:S(2)}) collective-permute-start(bf16[2,256,384]{2,1,0:T(8,128)(2,1)S(1)} %get-tuple-element.102), channel_id=1, source_target_pairs={{0,8},{8,0},{16,24},{24,16},{1,9},{9,1},{17,25},{25,17},{2,10},{10... | collective-permute-start | bytes 1179656 | tf_op jit(solution)/shard_map/ppermute | solution.py:55
  43.8 2.2 collective-permute-start.10
  53.5 2.6 %collective-permute-done.11 = bf16[2,256,384]{2,1,0:T(8,128)(2,1)S(1)} collective-permute-done((bf16[2,256,384]{2,1,0:T(8,128)(2,1)S(1)}, bf16[2,256,384]{2,1,0:T(8,128)(2,1)S(1)}, u32[]{:S(2)}, u32[]{:S(2)}) %collective-permute-start.11) | collective-permute-done | bytes 393248 | tf_op jit(solution)/shard_map/ppermute | solution.py:55
  56.4 4.5 %fusion.13.first.k0.v0.qkv = bf16[1024,768]{1,0:T(8,128)(2,1)} fusion(bf16[1024,2048]{1,0:T(8,128)(2,1)S(1)} %copy-done.1, bf16[2048,384]{1,0:T(8,128)(2,1)S(1)} %fusion.42, bf16[2048,384]{1,0:T(8,128)(2,1)S(1)} %fusion.46), kind=kOutput, calls=%fused_computation.14 | convolution fusion | flops 3228303360 | bytes 8912896 | tf_op jit(solution)/shard_map/dot_general | solution.py:184
  66.9 2.3 collective-permute-done.16
  74.0 4.5 %fusion.10.second.k1.v1.qkv = bf16[1024,768]{1,0:T(8,128)(2,1)} fusion(bf16[1024,2048]{1,0:T(8,128)(2,1)S(1)} %copy-done.1, bf16[2048,384]{1,0:T(8,128)(2,1)S(1)} %fusion.34, bf16[2048,384]{1,0:T(8,128)(2,1)S(1)} %fusion.38), kind=kOutput, calls=%fused_computation.13 | convolution fusion | flops 3228303360 | bytes 8912896 | tf_op jit(solution)/shard_map/dot_general | solution.py:184
  78.6 2.7 %outer.1 = f32[4,2,128,128]{3,2,1,0:T(8,128)} custom-call(bf16[1024,768]{1,0:T(8,128)(2,1)} %fusion.13.first.k0.v0.qkv, bf16[1024,768]{1,0:T(8,128)(2,1)} %fusion.13.first.k0.v0.qkv, bf16[1024,768]{1,0:T(8,128)(2,1)} %fusion.10.second.k1.v1.qkv, bf16[1024,768]{1,0:T(8,128)(2,1)} %fusion.10.second.k1.v1.qkv), custom_call_target="tpu_custom_call" | custom-call | tf_op jit(solution)/shard_map/outer/pallas_call | solution.py:162
  81.3 4.0 %all-to-all-start = ((f32[16,64,128]{2,1,0:T(8,128)}), f32[16,64,128]{2,1,0:T(8,128)S(1)}, u32[]{:S(2)}, u32[]{:S(2)}) async-start(f32[16,64,128]{2,1,0:T(8,128)} %bitcast.230), calls=%async_computation | async-start | bytes 1048576 | tf_op jit(solution)/shard_map/all_to_all | solution.py:213
  85.3 10.0 %all-to-all-done.received = f32[16,64,128]{2,1,0:T(8,128)S(1)} async-done(((f32[16,64,128]{2,1,0:T(8,128)}), f32[16,64,128]{2,1,0:T(8,128)S(1)}, u32[]{:S(2)}, u32[]{:S(2)}) %all-to-all-start) | async-done | bytes 524320 | tf_op jit(solution)/shard_map/all_to_all | solution.py:213
  97.9 3.7 %all-to-all-start.1 = ((bf16[16,64,128]{2,1,0:T(8,128)(2,1)}), bf16[16,64,128]{2,1,0:T(8,128)(2,1)S(1)}, u32[]{:S(2)}, u32[]{:S(2)}) async-start(bf16[16,64,128]{2,1,0:T(8,128)(2,1)} %running.1), calls=%async_computation.1 | async-start | bytes 524288 | tf_op jit(solution)/shard_map/all_to_all | solution.py:221
  101.6 6.5 %within.1 = f32[1024,512]{1,0:T(8,128)} custom-call(bf16[1024,768]{1,0:T(8,128)(2,1)} %fusion.13.first.k0.v0.qkv, bf16[1024,768]{1,0:T(8,128)(2,1)} %fusion.10.second.k1.v1.qkv), custom_call_target="tpu_custom_call" | custom-call | tf_op jit(solution)/shard_map/within/pallas_call | solution.py:265
  110.6 6.9 %forward.1 = (bf16[1024,512]{1,0:T(8,128)(2,1)}, bf16[1024,512]{1,0:T(8,128)(2,1)}, bf16[4,2,128,128]{3,2,1,0:T(8,128)(2,1)}) custom-call(s32[1]{0:T(128)} %bitcast.core, bf16[1024,768]{1,0:T(8,128)(2,1)} %fusion.13.first.k0.v0.qkv, bf16[1024,768]{1,0:T(8,128)(2,1)} %fusion.10.second.k1.v1.qkv, f32[1024,512]{1,0:T(8,128)} %within.1, ...), custom_call_target="tpu_custom_call" | custom-call | tf_op jit(solution)/shard_map/forward/pallas_call | solution.py:297
  118.0 5.4 %backward.2 = (bf16[1024,256]{1,0:T(8,128)(2,1)}, f32[2,1024,256]{2,1,0:T(8,128)}) custom-call(s32[1]{0:T(128)} %constant.53.clone.1.pair, bf16[1024,768]{1,0:T(8,128)(2,1)} %fusion.13.first.k0.v0.qkv, bf16[1024,512]{1,0:T(8,128)(2,1)} %get-tuple-element.65.grad, bf16[4,2,128,128]{3,2,1,0:T(8,128)(2,1)} %bitcast.216), custom_call_target="tpu_custom_call" | custom-call | tf_op jit(solution)/shard_map/backward/pallas_call | solution.py:333
  125.6 5.4 %backward.3 = (bf16[1024,256]{1,0:T(8,128)(2,1)}, f32[2,1024,256]{2,1,0:T(8,128)}) custom-call(s32[1]{0:T(128)} %constant.54.clone.1.pair, bf16[1024,768]{1,0:T(8,128)(2,1)} %fusion.10.second.k1.v1.qkv, bf16[1024,512]{1,0:T(8,128)(2,1)} %get-tuple-element.65.grad, bf16[4,2,128,128]{3,2,1,0:T(8,128)(2,1)} %bitcast.217), custom_call_target="tpu_custom_call" | custom-call | tf_op jit(solution)/shard_map/backward/pallas_call | solution.py:333
  133.3 6.9 %shard_map.84 = (bf16[4,256,256]{2,1,0:T(8,128)(2,1)}, bf16[4,256,256]{2,1,0:T(8,128)(2,1)}, bf16[4,256,256]{2,1,0:T(8,128)(2,1)}, bf16[4,256,256]{2,1,0:T(8,128)(2,1)}) custom-call(s32[2]{0:T(128)} %pad_add_fusion.keeps, bf16[1024,256]{1,0:T(8,128)(2,1)} %get-tuple-element.69.q0, bf16[1024,256]{1,0:T(8,128)(2,1)} %get-tuple-element.70.q1, ...), custom_call_target="tpu_custom_call" | custom-call | tf_op jit(solution)/shard_map/pallas_call | solution.py:428
  145.2 3.9 %collective-permute-done.26 = bf16[4,2,128,128]{3,2,1,0:T(8,128)(2,1)S(1)} collective-permute-done((bf16[4,2,128,128]{3,2,1,0:T(8,128)(2,1)S(1)}, bf16[4,2,128,128]{3,2,1,0:T(8,128)(2,1)S(1)}, u32[]{:S(2)}, u32[]{:S(2)}) %collective-permute-start.26) | collective-permute-done | bytes 262176 | tf_op jit(solution)/shard_map/ppermute | solution.py:55
  150.1 13.3 %shard_map.85 = (bf16[4,256,256]{2,1,0:T(8,128)(2,1)}, bf16[4,256,256]{2,1,0:T(8,128)(2,1)}, bf16[4,256,256]{2,1,0:T(8,128)(2,1)}, bf16[4,256,256]{2,1,0:T(8,128...) custom-call(s32[2]{0:T(128)} %pad_add_fusion.keeps, ...), custom_call_target="tpu_custom_call" | custom-call | tf_op jit(solution)/shard_map/pallas_call | solution.py:428
  173.6 3.8 %collective-permute-done.24 = bf16[2,256,256]{2,1,0:T(8,128)(2,1)S(1)} collective-permute-done((bf16[2,256,256]{2,1,0:T(8,128)(2,1)S(1)}, bf16[2,256,256]{2,1,0:T(8,128)(2,1)S(1)}, u32[]{:S(2)}, u32[]{:S(2)}) %collective-permute-start.24) | collective-permute-done | bytes 262176 | tf_op jit(solution)/shard_map/ppermute | solution.py:55
  188.6 2.6 %collective-permute-start.46 = (bf16[256,256]{1,0:T(8,128)(2,1)S(1)}, bf16[256,256]{1,0:T(8,128)(2,1)S(1)}, u32[]{:S(2)}, u32[]{:S(2)}) collective-permute-start(bf16[256,256]{1,0:T(8,128)(2,1)S(1)} %slice_bitcast_fusion.20), channel_id=1, source_target_pairs={{2,4},{4,2},{6,0},{0,6},{3,5},{5,3},{7,1},{1,7},{10,12},{12,10},{1... | collective-permute-start | bytes 393224 | tf_op jit(solution)/shard_map/ppermute | solution.py:55
  195.3 2.4 collective-permute-start.40
  198.9 5.1 %collective-permute-done.47 = bf16[1,256,256]{2,1,0:T(8,128)(2,1)S(1)} collective-permute-done((bf16[1,256,256]{2,1,0:T(8,128)(2,1)S(1)}, bf16[1,256,256]{2,1,0:T(8,128)(2,1)S(1)}, u32[]{:S(2)}, u32[]{:S(2)}) %collective-permute-start.47) | collective-permute-done | bytes 131104 | tf_op jit(solution)/shard_map/ppermute | solution.py:55
  218.3 2.9 %collective-permute-done.32 = bf16[2,256,256]{2,1,0:T(8,128)(2,1)S(1)} collective-permute-done((bf16[2,256,256]{2,1,0:T(8,128)(2,1)S(1)}, bf16[2,256,256]{2,1,0:T(8,128)(2,1)S(1)}, u32[]{:S(2)}, u32[]{:S(2)}) %collective-permute-start.32) | collective-permute-done | bytes 262176 | tf_op jit(solution)/shard_map/ppermute | solution.py:55
  225.4 4.4 %collective-permute-done.57.refs_7_ = bf16[1,256,256]{2,1,0:T(8,128)(2,1)S(1)} collective-permute-done((bf16[1,256,256]{2,1,0:T(8,128)(2,1)S(1)}, bf16[1,256,256]{2,1,0:T(8,128)(2,1)S(1)}, u32[]{:S(2)}, u32[]{:S(2)}) %collective-permute-start.57) | collective-permute-done | bytes 131104 | tf_op jit(solution)/shard_map/ppermute | solution.py:55
  231.3 2.9 %sort_pieces.1 = (bf16[256,1536]{1,0:T(8,128)(2,1)}, bf16[256,1536]{1,0:T(8,128)(2,1)}) custom-call(s32[4]{0:T(128)} %add_convert_fusion.19.holds, bf16[2,256,256]{2,1,0:T(8,128)(2,1)} %copy-done.6, bf16[2,256,256]{2,1,0:T(8,128)(2,1)} %copy-done.19, bf16[2,256,256]{2,1,0:T(8,128)(2,1)} %copy-done.7, bf16[2,256,256]{2,1,0:T(8,128)(2,1)} %copy-done.20, ...), custom_call_target="tpu_custom_call" | custom-call | tf_op jit(solution)/shard_map/sort_pieces/pallas_call | solution.py:508
  234.8 2.6 %collective-permute-done.19.other = bf16[512,512]{1,0:T(8,128)(2,1)S(1)} collective-permute-done((bf16[512,512]{1,0:T(8,128)(2,1)S(1)}, bf16[512,512]{1,0:T(8,128)(2,1)S(1)}, u32[]{:S(2)}, u32[]{:S(2)}) %collective-permute-start.19) | collective-permute-done | bytes 524320 | tf_op jit(solution)/shard_map/ppermute | solution.py:54
  241.2 3.8 %assemble.1 = bf16[256,3072]{1,0:T(8,128)(2,1)} custom-call(s32[1]{0:T(128)} %bitcast.core, bf16[256,1536]{1,0:T(8,128)(2,1)} %get-tuple-element.90.kept, bf16[256,1536]{1,0:T(8,128)(2,1)} %copy-done.8), custom_call_target="tpu_custom_call" | custom-call | tf_op jit(solution)/shard_map/assemble/pallas_call | solution.py:548
  245.0 6.6 %multiply_subtract_fusion = (f32[256,3072]{1,0:T(8,128)}, f32[256,3072]{1,0:T(8,128)}, f32[256,3072]{1,0:T(8,128)}) fusion(f32[256,3072]{1,0:T(8,128)S(1)} %copy-done, bf16[256,3072]{1,0:T(8,128)(2,1)} %assemble.1, f32[256,3072]{1,0:T(8,128)} %param.7, f32[256,3072]{1,0:T(8,128)} %param.8), kind=kLoop, calls=%fused_computation.12 | loop fusion | flops 12582912 | bytes 20447232 | tf_op jit(solution)/shard_map/sub | solution.py:565
  (252 shorter events, 99.5 us)
Async XLA Ops:
  3.8 24.2 %collective-permute-start.5 = (bf16[512,2048]{1,0:T(8,128)(2,1)}, bf16[512,2048]{1,0:T(8,128)(2,1)}, u32[]{:S(2)}, u32[]{:S(2)}) collective-permute-start(bf16[512,2048]{1,0:T(8,128)(2,1)} %bitcast.10.own), channel_id=1, source_target_pairs={{0,1},{1,0},{2,3},{3,2},{4,5},{5,4},{6,7},{7,6},{8,9},{9,8},{10,11... | collective-permute-start | bytes 6291464 | tf_op jit(solution)/shard_map/ppermute | solution.py:54
  13.8 11.4 %collective-permute-start.2 = (bf16[2,256,384]{2,1,0:T(8,128)(2,1)S(1)}, bf16[2,256,384]{2,1,0:T(8,128)(2,1)S(1)}, u32[]{:S(2)}, u32[]{:S(2)}) collective-permute-start(bf16[2,256,384]{2,1,0:T(8,128)(2,1)S(1)} %pad_maximum_fusion.4), channel_id=1, source_target_pairs={{2,4},{4,2},{6,0},{0,6},{3,5},{5,3},{7,1},{1,7},{10,12},{12,10},{1... | collective-permute-start | bytes 1179656 | tf_op jit(solution)/shard_map/ppermute | solution.py:55
  17.8 9.1 %collective-permute-start.4 = (bf16[2,256,384]{2,1,0:T(8,128)(2,1)S(1)}, bf16[2,256,384]{2,1,0:T(8,128)(2,1)}, u32[]{:S(2)}, u32[]{:S(2)}) collective-permute-start(bf16[2,256,384]{2,1,0:T(8,128)(2,1)S(1)} %pad_maximum_fusion.5), channel_id=1, source_target_pairs={{0,2},{2,0},{4,6},{6,4},{1,3},{3,1},{5,7},{7,5},{8,10},{10,8},{12,... | collective-permute-start | bytes 1179656 | tf_op jit(solution)/shard_map/ppermute | solution.py:55
  35.4 10.7 %collective-permute-start.6 = (bf16[1,256,384]{2,1,0:T(8,128)(2,1)S(1)}, bf16[1,256,384]{2,1,0:T(8,128)(2,1)S(1)}, u32[]{:S(2)}, u32[]{:S(2)}) collective-permute-start(bf16[1,256,384]{2,1,0:T(8,128)(2,1)S(1)} %get-tuple-element.104), channel_id=1, source_target_pairs={{0,2},{2,0},{4,6},{6,4},{1,3},{3,1},{5,7},{7,5},{8,10},{10,8},{12,... | collective-permute-start | bytes 589832 | tf_op jit(solution)/shard_map/ppermute | solution.py:55
  35.7 11.7 %collective-permute-start.8 = (bf16[1,256,384]{2,1,0:T(8,128)(2,1)S(1)}, bf16[1,256,384]{2,1,0:T(8,128)(2,1)S(1)}, u32[]{:S(2)}, u32[]{:S(2)}) collective-permute-start(bf16[1,256,384]{2,1,0:T(8,128)(2,1)S(1)} %get-tuple-element.103), channel_id=1, source_target_pairs={{2,4},{4,2},{6,0},{0,6},{3,5},{5,3},{7,1},{1,7},{10,12},{12,10},{1... | collective-permute-start | bytes 589832 | tf_op jit(solution)/shard_map/ppermute | solution.py:55
  37.3 12.8 %collective-permute-start.12 = (bf16[2,256,384]{2,1,0:T(8,128)(2,1)S(1)}, bf16[2,256,384]{2,1,0:T(8,128)(2,1)S(1)}, u32[]{:S(2)}, u32[]{:S(2)}) collective-permute-start(bf16[2,256,384]{2,1,0:T(8,128)(2,1)S(1)} %get-tuple-element.102), channel_id=1, source_target_pairs={{0,8},{8,0},{16,24},{24,16},{1,9},{9,1},{17,25},{25,17},{2,10},{10... | collective-permute-start | bytes 1179656 | tf_op jit(solution)/shard_map/ppermute | solution.py:55
  42.3 10.7 %collective-permute-start.13 = (bf16[2,256,384]{2,1,0:T(8,128)(2,1)S(1)}, bf16[2,256,384]{2,1,0:T(8,128)(2,1)S(1)}, u32[]{:S(2)}, u32[]{:S(2)}) collective-permute-start(bf16[2,256,384]{2,1,0:T(8,128)(2,1)S(1)} %get-tuple-element.101), channel_id=1, source_target_pairs={{8,16},{16,8},{24,0},{0,24},{9,17},{17,9},{25,1},{1,25},{10,18},{1... | collective-permute-start | bytes 1179656 | tf_op jit(solution)/shard_map/ppermute | solution.py:55
  43.8 9.6 %collective-permute-start.10 = (bf16[2,256,384]{2,1,0:T(8,128)(2,1)S(1)}, bf16[2,256,384]{2,1,0:T(8,128)(2,1)S(1)}, u32[]{:S(2)}, u32[]{:S(2)}) collective-permute-start(bf16[2,256,384]{2,1,0:T(8,128)(2,1)S(1)} %get-tuple-element.100), channel_id=1, source_target_pairs={{0,32},{32,0},{64,96},{96,64},{1,33},{33,1},{65,97},{97,65},{2,34}... | collective-permute-start | bytes 1179656 | tf_op jit(solution)/shard_map/ppermute | solution.py:55
  46.0 10.1 %collective-permute-start.11 = (bf16[2,256,384]{2,1,0:T(8,128)(2,1)S(1)}, bf16[2,256,384]{2,1,0:T(8,128)(2,1)S(1)}, u32[]{:S(2)}, u32[]{:S(2)}) collective-permute-start(bf16[2,256,384]{2,1,0:T(8,128)(2,1)S(1)} %get-tuple-element.99), channel_id=1, source_target_pairs={{32,64},{64,32},{96,0},{0,96},{33,65},{65,33},{97,1},{1,97},{34,66... | collective-permute-start | bytes 1179656 | tf_op jit(solution)/shard_map/ppermute | solution.py:55
  47.4 13.4 %collective-permute-start.7 = (bf16[2,256,384]{2,1,0:T(8,128)(2,1)S(1)}, bf16[2,256,384]{2,1,0:T(8,128)(2,1)S(1)}, u32[]{:S(2)}, u32[]{:S(2)}) collective-permute-start(bf16[2,256,384]{2,1,0:T(8,128)(2,1)S(1)} %pad_maximum_fusion.6), channel_id=1, source_target_pairs={{2,4},{4,2},{6,0},{0,6},{3,5},{5,3},{7,1},{1,7},{10,12},{12,10},{1... | collective-permute-start | bytes 1179656 | tf_op jit(solution)/shard_map/ppermute | solution.py:55
  50.1 10.8 %collective-permute-start.9 = (bf16[2,256,384]{2,1,0:T(8,128)(2,1)S(1)}, bf16[2,256,384]{2,1,0:T(8,128)(2,1)S(1)}, u32[]{:S(2)}, u32[]{:S(2)}) collective-permute-start(bf16[2,256,384]{2,1,0:T(8,128)(2,1)S(1)} %pad_maximum_fusion.7), channel_id=1, source_target_pairs={{0,2},{2,0},{4,6},{6,4},{1,3},{3,1},{5,7},{7,5},{8,10},{10,8},{12,... | collective-permute-start | bytes 1179656 | tf_op jit(solution)/shard_map/ppermute | solution.py:55
  61.2 8.1 %collective-permute-start.16 = (bf16[2,256,384]{2,1,0:T(8,128)(2,1)S(1)}, bf16[2,256,384]{2,1,0:T(8,128)(2,1)S(1)}, u32[]{:S(2)}, u32[]{:S(2)}) collective-permute-start(bf16[2,256,384]{2,1,0:T(8,128)(2,1)S(1)} %get-tuple-element.98), channel_id=1, source_target_pairs={{0,8},{8,0},{16,24},{24,16},{1,9},{9,1},{17,25},{25,17},{2,10},{10... | collective-permute-start | bytes 1179656 | tf_op jit(solution)/shard_map/ppermute | solution.py:55
  61.7 9.5 %collective-permute-start.17 = (bf16[2,256,384]{2,1,0:T(8,128)(2,1)S(1)}, bf16[2,256,384]{2,1,0:T(8,128)(2,1)S(1)}, u32[]{:S(2)}, u32[]{:S(2)}) collective-permute-start(bf16[2,256,384]{2,1,0:T(8,128)(2,1)S(1)} %get-tuple-element.97), channel_id=1, source_target_pairs={{8,16},{16,8},{24,0},{0,24},{9,17},{17,9},{25,1},{1,25},{10,18},{1... | collective-permute-start | bytes 1179656 | tf_op jit(solution)/shard_map/ppermute | solution.py:55
  63.7 8.4 %collective-permute-start.14 = (bf16[2,256,384]{2,1,0:T(8,128)(2,1)S(1)}, bf16[2,256,384]{2,1,0:T(8,128)(2,1)S(1)}, u32[]{:S(2)}, u32[]{:S(2)}) collective-permute-start(bf16[2,256,384]{2,1,0:T(8,128)(2,1)S(1)} %get-tuple-element.96), channel_id=1, source_target_pairs={{0,32},{32,0},{64,96},{96,64},{1,33},{33,1},{65,97},{97,65},{2,34}... | collective-permute-start | bytes 1179656 | tf_op jit(solution)/shard_map/ppermute | solution.py:55
  64.8 9.0 %collective-permute-start.15 = (bf16[2,256,384]{2,1,0:T(8,128)(2,1)S(1)}, bf16[2,256,384]{2,1,0:T(8,128)(2,1)S(1)}, u32[]{:S(2)}, u32[]{:S(2)}) collective-permute-start(bf16[2,256,384]{2,1,0:T(8,128)(2,1)S(1)} %get-tuple-element.95), channel_id=1, source_target_pairs={{32,64},{64,32},{96,0},{0,96},{33,65},{65,33},{97,1},{1,97},{34,66... | collective-permute-start | bytes 1179656 | tf_op jit(solution)/shard_map/ppermute | solution.py:55
  81.3 14.1 %all-to-all-start = ((f32[16,64,128]{2,1,0:T(8,128)}), f32[16,64,128]{2,1,0:T(8,128)S(1)}, u32[]{:S(2)}, u32[]{:S(2)}) async-start(f32[16,64,128]{2,1,0:T(8,128)} %bitcast.230), calls=%async_computation | async-start | bytes 1048576 | tf_op jit(solution)/shard_map/all_to_all | solution.py:213
  85.2 22.9 %collective-permute-start.18 = (bf16[512,512]{1,0:T(8,128)(2,1)S(1)}, bf16[512,512]{1,0:T(8,128)(2,1)S(1)}, u32[]{:S(2)}, u32[]{:S(2)}) collective-permute-start(bf16[512,512]{1,0:T(8,128)(2,1)S(1)} %copy-done.23), channel_id=1, source_target_pairs={{0,1},{1,0},{2,3},{3,2},{4,5},{5,4},{6,7},{7,6},{8,9},{9,8},{10,11... | collective-permute-start | bytes 1572872 | tf_op jit(solution)/shard_map/ppermute | solution.py:54
  97.9 12.0 %all-to-all-start.1 = ((bf16[16,64,128]{2,1,0:T(8,128)(2,1)}), bf16[16,64,128]{2,1,0:T(8,128)(2,1)S(1)}, u32[]{:S(2)}, u32[]{:S(2)}) async-start(bf16[16,64,128]{2,1,0:T(8,128)(2,1)} %running.1), calls=%async_computation.1 | async-start | bytes 524288 | tf_op jit(solution)/shard_map/all_to_all | solution.py:221
  132.0 8.3 %collective-permute-start.22 = (bf16[4,2,128,128]{3,2,1,0:T(8,128)(2,1)S(1)}, bf16[4,2,128,128]{3,2,1,0:T(8,128)(2,1)S(1)}, u32[]{:S(2)}, u32[]{:S(2)}) collective-permute-start(bf16[4,2,128,128]{3,2,1,0:T(8,128)(2,1)S(1)} %fusion.27), channel_id=1, source_target_pairs={{0,32},{32,0},{64,96},{96,64},{1,33},{33,1},{65,97},{97,65},{2,34}... | collective-permute-start | bytes 786440 | tf_op jit(solution)/shard_map/ppermute | solution.py:55
  140.3 28.3 %collective-permute-start.23 = (bf16[4,256,256]{2,1,0:T(8,128)(2,1)}, bf16[4,256,256]{2,1,0:T(8,128)(2,1)S(1)}, u32[]{:S(2)}, u32[]{:S(2)}) collective-permute-start(bf16[4,256,256]{2,1,0:T(8,128)(2,1)} %get-tuple-element.76), channel_id=1, source_target_pairs={{0,2},{2,0},{4,6},{6,4},{1,3},{3,1},{5,7},{7,5},{8,10},{10,8},{12,... | collective-permute-start | bytes 1572872 | tf_op jit(solution)/shard_map/ppermute | solution.py:55
  143.7 27.3 %collective-permute-start.34 = (bf16[4,256,256]{2,1,0:T(8,128)(2,1)}, bf16[4,256,256]{2,1,0:T(8,128)(2,1)S(1)}, u32[]{:S(2)}, u32[]{:S(2)}) collective-permute-start(bf16[4,256,256]{2,1,0:T(8,128)(2,1)} %get-tuple-element.83), channel_id=1, source_target_pairs={{2,4},{4,2},{6,0},{0,6},{3,5},{5,3},{7,1},{1,7},{10,12},{12,10},{1... | collective-permute-start | bytes 1572872 | tf_op jit(solution)/shard_map/ppermute | solution.py:55
  163.4 10.0 %collective-permute-start.27 = (bf16[4,256,256]{2,1,0:T(8,128)(2,1)}, bf16[4,256,256]{2,1,0:T(8,128)(2,1)S(1)}, u32[]{:S(2)}, u32[]{:S(2)}) collective-permute-start(bf16[4,256,256]{2,1,0:T(8,128)(2,1)} %get-tuple-element.81), channel_id=1, source_target_pairs={{0,2},{2,0},{4,6},{6,4},{1,3},{3,1},{5,7},{7,5},{8,10},{10,8},{12,... | collective-permute-start | bytes 1572872 | tf_op jit(solution)/shard_map/ppermute | solution.py:55
  164.5 13.0 %collective-permute-start.37 = (bf16[4,256,256]{2,1,0:T(8,128)(2,1)}, bf16[4,256,256]{2,1,0:T(8,128)(2,1)S(1)}, u32[]{:S(2)}, u32[]{:S(2)}) collective-permute-start(bf16[4,256,256]{2,1,0:T(8,128)(2,1)} %get-tuple-element.85), channel_id=1, source_target_pairs={{2,4},{4,2},{6,0},{0,6},{3,5},{5,3},{7,1},{1,7},{10,12},{12,10},{1... | collective-permute-start | bytes 1572872 | tf_op jit(solution)/shard_map/ppermute | solution.py:55
  166.5 13.4 %collective-permute-start.44 = (bf16[4,256,256]{2,1,0:T(8,128)(2,1)}, bf16[4,256,256]{2,1,0:T(8,128)(2,1)S(1)}, u32[]{:S(2)}, u32[]{:S(2)}) collective-permute-start(bf16[4,256,256]{2,1,0:T(8,128)(2,1)} %get-tuple-element.87), channel_id=1, source_target_pairs={{32,64},{64,32},{96,0},{0,96},{33,65},{65,33},{97,1},{1,97},{34,66... | collective-permute-start | bytes 1572872 | tf_op jit(solution)/shard_map/ppermute | solution.py:55
  168.6 13.1 %collective-permute-start.51 = (bf16[4,256,256]{2,1,0:T(8,128)(2,1)}, bf16[4,256,256]{2,1,0:T(8,128)(2,1)S(1)}, u32[]{:S(2)}, u32[]{:S(2)}) collective-permute-start(bf16[4,256,256]{2,1,0:T(8,128)(2,1)} %get-tuple-element.89), channel_id=1, source_target_pairs={{8,16},{16,8},{24,0},{0,24},{9,17},{17,9},{25,1},{1,25},{10,18},{1... | collective-permute-start | bytes 1572872 | tf_op jit(solution)/shard_map/ppermute | solution.py:55
  177.4 8.2 %collective-permute-start.28 = (bf16[2,256,256]{2,1,0:T(8,128)(2,1)S(1)}, bf16[2,256,256]{2,1,0:T(8,128)(2,1)S(1)}, u32[]{:S(2)}, u32[]{:S(2)}) collective-permute-start(bf16[2,256,256]{2,1,0:T(8,128)(2,1)S(1)} %dynamic-slice_bitcast_fusion.2), channel_id=1, source_target_pairs={{0,32},{32,0},{64,96},{96,64},{1,33},{33,1},{65,97},{97,65},{2,34}... | collective-permute-start | bytes 786440 | tf_op jit(solution)/shard_map/ppermute | solution.py:55
  188.6 9.2 %collective-permute-start.46 = (bf16[256,256]{1,0:T(8,128)(2,1)S(1)}, bf16[256,256]{1,0:T(8,128)(2,1)S(1)}, u32[]{:S(2)}, u32[]{:S(2)}) collective-permute-start(bf16[256,256]{1,0:T(8,128)(2,1)S(1)} %slice_bitcast_fusion.20), channel_id=1, source_target_pairs={{2,4},{4,2},{6,0},{0,6},{3,5},{5,3},{7,1},{1,7},{10,12},{12,10},{1... | collective-permute-start | bytes 393224 | tf_op jit(solution)/shard_map/ppermute | solution.py:55
  193.1 13.4 %collective-permute-start.30 = (bf16[2,256,256]{2,1,0:T(8,128)(2,1)S(1)}, bf16[2,256,256]{2,1,0:T(8,128)(2,1)S(1)}, u32[]{:S(2)}, u32[]{:S(2)}) collective-permute-start(bf16[2,256,256]{2,1,0:T(8,128)(2,1)S(1)} %pad_maximum_fusion.8), channel_id=1, source_target_pairs={{32,64},{64,32},{96,0},{0,96},{33,65},{65,33},{97,1},{1,97},{34,66... | collective-permute-start | bytes 786440 | tf_op jit(solution)/shard_map/ppermute | solution.py:55
  195.3 12.5 %collective-permute-start.40 = (bf16[2,256,256]{2,1,0:T(8,128)(2,1)S(1)}, bf16[2,256,256]{2,1,0:T(8,128)(2,1)S(1)}, u32[]{:S(2)}, u32[]{:S(2)}) collective-permute-start(bf16[2,256,256]{2,1,0:T(8,128)(2,1)S(1)} %pad_maximum_fusion.9), channel_id=1, source_target_pairs={{8,16},{16,8},{24,0},{0,24},{9,17},{17,9},{25,1},{1,25},{10,18},{1... | collective-permute-start | bytes 786440 | tf_op jit(solution)/shard_map/ppermute | solution.py:55
  212.1 11.5 %collective-permute-start.56 = (bf16[1,256,256]{2,1,0:T(8,128)(2,1)S(1)}, bf16[1,256,256]{2,1,0:T(8,128)(2,1)S(1)}, u32[]{:S(2)}, u32[]{:S(2)}) collective-permute-start(bf16[1,256,256]{2,1,0:T(8,128)(2,1)S(1)} %add_convert_fusion.14), channel_id=1, source_target_pairs={{32,64},{64,32},{96,0},{0,96},{33,65},{65,33},{97,1},{1,97},{34,66... | collective-permute-start | bytes 393224 | tf_op jit(solution)/shard_map/ppermute | solution.py:55
  216.9 8.6 %collective-permute-start.50 = (bf16[1,256,256]{2,1,0:T(8,128)(2,1)S(1)}, bf16[1,256,256]{2,1,0:T(8,128)(2,1)S(1)}, u32[]{:S(2)}, u32[]{:S(2)}) collective-permute-start(bf16[1,256,256]{2,1,0:T(8,128)(2,1)S(1)} %add_convert_fusion.16.refs_4_), channel_id=1, source_target_pairs={{32,64},{64,32},{96,0},{0,96},{33,65},{65,33},{97,1},{1,97},{34,66... | collective-permute-start | bytes 393224 | tf_op jit(solution)/shard_map/ppermute | solution.py:55
  221.3 8.6 %collective-permute-start.33 = (bf16[2,256,256]{2,1,0:T(8,128)(2,1)S(1)}, bf16[2,256,256]{2,1,0:T(8,128)(2,1)S(1)}, u32[]{:S(2)}, u32[]{:S(2)}) collective-permute-start(bf16[2,256,256]{2,1,0:T(8,128)(2,1)S(1)} %add_convert_fusion.10.refs_0_), channel_id=1, source_target_pairs={{0,32},{32,0},{64,96},{96,64},{1,33},{33,1},{65,97},{97,65},{2,34}... | collective-permute-start | bytes 786440 | tf_op jit(solution)/shard_map/ppermute | solution.py:55
  (53 other events, 316.3 us)
